TPU v7x, 32 devices: a whole 2x2x4 slice. The times are simulated.
32 devices in a mesh: rep: 2 (over y), fsdp: 16 (over z, x, core).
Axes of the slice: x: 2, y: 2, z: 4, core: 2. Of those that a mesh axis runs over, the one named last changes fastest.
Arguments:
- tokens: bfloat16 [32, 128, 1536], P(('rep', 'fsdp')), may hold values from -6 to 6
- cotangent: bfloat16 [32, 128, 1536], P(('rep', 'fsdp')), may hold values from -6 to 6
- pic_start: int32 [32], P(('rep', 'fsdp')), may hold values from 0 to 96
- valid_mask: int32 [32, 128], P(('rep', 'fsdp')), may hold values from 0 to 1, as said below
- gain_attn: bfloat16 [1536], P('fsdp'), may hold values from 0.5 to 1.5
- attn_in: bfloat16 [1536, 6144], P('fsdp'), may hold values from -0.15625 to 0.15625
- forget_w: bfloat16 [1536, 24], P('fsdp'), may hold values from -0.15625 to 0.15625
- forget_bias: bfloat16 [24], replicated, may hold values from 0 to 7
- attn_out: bfloat16 [1536, 1536], P('fsdp'), may hold values from -0.625 to 0.625
- gain_ffn: bfloat16 [1536], P('fsdp'), may hold values from 0.5 to 1.5
- ffn_in: bfloat16 [2, 1536, 4096], P(None, None, 'fsdp'), may hold values from -0.15625 to 0.15625
- ffn_down: bfloat16 [4096, 1536], P('fsdp'), may hold values from -0.09375 to 0.09375
Outputs:
- activations: bfloat16 [32, 128, 1536], P(('rep', 'fsdp'))
- input_grad: float32 [32, 128, 1536], P(('rep', 'fsdp'))
- grad_gain_attn: float32 [1536], P('fsdp')
- grad_attn_in: float32 [1536, 6144], P('fsdp')
- grad_forget_w: float32 [1536, 24], P('fsdp')
- grad_forget_bias: float32 [24], replicated
- grad_attn_out: float32 [1536, 1536], P('fsdp')
- grad_gain_ffn: float32 [1536], P('fsdp')
- grad_ffn_in: float32 [2, 1536, 4096], P(None, None, 'fsdp')
- grad_ffn_down: float32 [4096, 1536], P('fsdp')
- stats: float32 [3], replicated
Inputs may be any that keep to these rules, and one draw needn't show every extreme that they name: `valid_mask`: sequence b's valid tokens are a prefix of length 42 + 86 * b // 31 plus a jitter under 128 // 8, at most 128; the last sequence is full.
All inputs are finite; a program needn't handle non-finite values.
Results may differ from a plain program's by a relative error of at most 0.024.
Values may be sent and summed in bfloat16 or wider, within the bound.
A program may use at most 320 MiB of HBM per device.

v0:
```python
import jax
import jax.numpy as jnp
from jax import lax
from jax.sharding import PartitionSpec as P

H = 24
HD = 64
PIC = 32


EPSILON = 1e-06
NEGATIVE = -1e30


def norm_apply(values_in, gain_row):
    inverse = lax.rsqrt(jnp.mean(values_in * values_in, axis=-1, keepdims=True) + EPSILON)
    return values_in * inverse * gain_row


def swiglu(gate_part, up_part):
    return jax.nn.silu(gate_part) * up_part


def block_scores(row_start, block_rows, queries, keys_all, decay_sum, inside, key_valid):
    seq_len = keys_all.shape[0]
    dotted = jnp.einsum("ihe,jhe->hij", queries, keys_all, preferred_element_type=jnp.float32)
    row_pos = row_start + jnp.arange(block_rows, dtype=jnp.int32)
    col_pos = jnp.arange(seq_len, dtype=jnp.int32)
    causal = col_pos[None, :] <= row_pos[:, None]
    allowed = (causal | inside[:, None] & inside[None, :]) & key_valid[None, :]
    spread = decay_sum.T[:, :, None] - decay_sum.T[:, None, :]
    decay_bias = jnp.where(causal[None], spread, -spread)
    scores = dotted * HD ** (-0.5) + decay_bias
    return (queries, scores, allowed[None], causal[None])


def per_device(
    tokens,
    cotangent,
    pic_start,
    valid_mask,
    gain_attn,
    attn_in,
    forget_w,
    forget_bias,
    attn_out,
    gain_ffn,
    ffn_in,
    ffn_down,
):
    seq_len = tokens.shape[1]
    model_width = tokens.shape[2]
    layer_in = tokens[0].astype(jnp.float32)
    gain_a, weight_in, weight_forget, weight_out, gain_f = (
        lax.all_gather(gain_attn, "fsdp", axis=0, tiled=True),
        lax.all_gather(attn_in, "fsdp", axis=0, tiled=True),
        lax.all_gather(forget_w, "fsdp", axis=0, tiled=True),
        lax.all_gather(attn_out, "fsdp", axis=0, tiled=True),
        lax.all_gather(gain_ffn, "fsdp", axis=0, tiled=True),
    )
    normed_a, pull_a = jax.vjp(norm_apply, layer_in, gain_a.astype(jnp.float32))
    rows_a = normed_a.astype(jnp.bfloat16)
    projected = jnp.dot(rows_a, weight_in, preferred_element_type=jnp.float32)
    queries = projected[:, :model_width].astype(jnp.bfloat16).reshape(seq_len, H, HD)
    keys_all = (
        projected[:, model_width : 2 * model_width].astype(jnp.bfloat16).reshape(seq_len, H, HD)
    )
    values_all = (
        projected[:, 2 * model_width : 3 * model_width].astype(jnp.bfloat16).reshape(seq_len, H, HD)
    )
    out_gate = jax.nn.sigmoid(projected[:, 3 * model_width :])
    forget_logit = jnp.dot(
        rows_a, weight_forget, preferred_element_type=jnp.float32
    ) + forget_bias.astype(jnp.float32)
    decay_sum = jnp.cumsum(jax.nn.log_sigmoid(forget_logit), axis=0)
    positions = jnp.arange(seq_len, dtype=jnp.int32)
    inside = (positions >= pic_start[0]) & (positions < pic_start[0] + PIC)
    key_valid = valid_mask[0] > 0
    block_rows = min(seq_len, 512)
    block_starts = jnp.arange(seq_len // block_rows, dtype=jnp.int32) * block_rows

    def forward_block(row_start):
        query_rows, scores, allowed, causal = block_scores(
            row_start, block_rows, queries, keys_all, decay_sum, inside, key_valid
        )
        masked = jnp.where(allowed, scores, NEGATIVE)
        row_max = jnp.max(masked, axis=-1, keepdims=True)
        weights = jnp.where(allowed, jnp.exp(masked - row_max), 0.0)
        totals = jnp.sum(weights, axis=-1, keepdims=True)
        prob_low = (weights / totals).astype(jnp.bfloat16)
        attn_rows = jnp.einsum(
            "hij,jhe->ihe", prob_low, values_all, preferred_element_type=jnp.float32
        )
        return (attn_rows, row_max + jnp.log(totals))

    attn_rows, log_total = lax.map(forward_block, block_starts)
    attended = attn_rows.reshape(seq_len, model_width)
    gated_rows = (attended * out_gate).astype(jnp.bfloat16)
    branch_attn = jnp.dot(gated_rows, weight_out, preferred_element_type=jnp.float32)
    middle = layer_in + branch_attn
    normed_f, pull_f = jax.vjp(norm_apply, middle, gain_f.astype(jnp.float32))
    rows_f = normed_f.astype(jnp.bfloat16)
    weight_ffn, weight_down = (
        lax.all_gather(ffn_in, "fsdp", axis=2, tiled=True),
        lax.all_gather(ffn_down, "fsdp", axis=0, tiled=True),
    )
    gate_up = jnp.einsum("sd,kdf->ksf", rows_f, weight_ffn, preferred_element_type=jnp.float32)
    hidden_f, pull_h = jax.vjp(swiglu, gate_up[0], gate_up[1])
    hidden = hidden_f.astype(jnp.bfloat16)
    branch_ffn = jnp.dot(hidden, weight_down, preferred_element_type=jnp.float32)
    result = middle + branch_ffn
    out_grad = cotangent[0].astype(jnp.float32)
    ffn_grad = out_grad.astype(jnp.bfloat16)
    hidden_grad = jnp.einsum("sd,fd->sf", ffn_grad, weight_down, preferred_element_type=jnp.float32)
    down_full = jnp.einsum("sf,sd->fd", hidden, ffn_grad, preferred_element_type=jnp.float32)
    gate_grad, up_grad = pull_h(hidden_grad)
    gate_up_grad = jnp.stack([gate_grad, up_grad]).astype(jnp.bfloat16)
    in_full = jnp.einsum("sd,ksf->kdf", rows_f, gate_up_grad, preferred_element_type=jnp.float32)
    rows_f_grad = jnp.einsum(
        "ksf,kdf->sd", gate_up_grad, weight_ffn, preferred_element_type=jnp.float32
    )
    grad_ffn_in, grad_ffn_down = (
        lax.psum_scatter(
            in_full.astype(jnp.bfloat16), "fsdp", scatter_dimension=2, tiled=True
        ).astype(jnp.float32),
        lax.psum_scatter(
            down_full.astype(jnp.bfloat16), "fsdp", scatter_dimension=0, tiled=True
        ).astype(jnp.float32),
    )
    middle_part, gain_f_grad = pull_f(rows_f_grad)
    middle_grad = out_grad + middle_part
    branch_grad = middle_grad.astype(jnp.bfloat16)
    gated_grad = jnp.einsum(
        "so,io->si", branch_grad, weight_out, preferred_element_type=jnp.float32
    )
    out_full = jnp.einsum("si,so->io", gated_rows, branch_grad, preferred_element_type=jnp.float32)
    attended_grad = (gated_grad * out_gate).astype(jnp.bfloat16).reshape(seq_len, H, HD)
    outgate_grad = gated_grad * attended * (out_gate * (1.0 - out_gate))

    def backward_block(carry, inputs):
        key_grad, value_grad, decay_cols = carry
        row_start, block_total = inputs
        query_rows, scores, allowed, causal = block_scores(
            row_start, block_rows, queries, keys_all, decay_sum, inside, key_valid
        )
        probability = jnp.where(
            allowed, jnp.exp(jnp.where(allowed, scores - block_total, NEGATIVE)), 0.0
        )
        prob_grad = jnp.einsum(
            "ihe,jhe->hij", attended_grad, values_all, preferred_element_type=jnp.float32
        )
        score_grad = probability * (
            prob_grad - jnp.sum(probability * prob_grad, axis=-1, keepdims=True)
        )
        prob_low = probability.astype(jnp.bfloat16)
        value_grad = value_grad + jnp.einsum(
            "hij,ihe->jhe", prob_low, attended_grad, preferred_element_type=jnp.float32
        )
        dotted_grad = (score_grad * HD ** (-0.5)).astype(jnp.bfloat16)
        query_grad = jnp.einsum(
            "hij,jhe->ihe", dotted_grad, keys_all, preferred_element_type=jnp.float32
        )
        key_grad = key_grad + jnp.einsum(
            "hij,ihe->jhe", dotted_grad, query_rows, preferred_element_type=jnp.float32
        )
        signed = jnp.where(causal, score_grad, -score_grad)
        decay_rows = jnp.sum(signed, axis=-1)
        decay_cols = decay_cols - jnp.sum(signed, axis=1)
        return ((key_grad, value_grad, decay_cols), (query_grad, decay_rows))

    zero_heads = jnp.zeros((seq_len, H, HD), jnp.float32)
    initial = (zero_heads, zero_heads, jnp.zeros((H, seq_len), jnp.float32))
    (key_grad, value_grad, decay_cols), (query_grad, decay_rows) = lax.scan(
        backward_block, initial, (block_starts, log_total)
    )
    decay_grad = jnp.transpose(decay_rows, (1, 0, 2)).reshape(H, seq_len) + decay_cols
    later_sums = jnp.cumsum(decay_grad[:, ::-1], axis=1)[:, ::-1]
    logit_grad = later_sums.T * jax.nn.sigmoid(-forget_logit)
    bias_grad = jnp.sum(logit_grad, axis=0)
    logit_low = logit_grad.astype(jnp.bfloat16)
    proj_grad = jnp.concatenate(
        [
            query_grad.reshape(seq_len, model_width),
            key_grad.reshape(seq_len, model_width),
            value_grad.reshape(seq_len, model_width),
            outgate_grad,
        ],
        axis=1,
    ).astype(jnp.bfloat16)
    in_attn_full = jnp.einsum("sd,se->de", rows_a, proj_grad, preferred_element_type=jnp.float32)
    forget_full = jnp.einsum("sd,sh->dh", rows_a, logit_low, preferred_element_type=jnp.float32)
    rows_a_grad = jnp.einsum("se,de->sd", proj_grad, weight_in, preferred_element_type=jnp.float32)
    rows_a_grad = rows_a_grad + jnp.einsum(
        "sh,dh->sd", logit_low, weight_forget, preferred_element_type=jnp.float32
    )
    input_part, gain_a_grad = pull_a(rows_a_grad)
    input_grad = middle_grad + input_part
    own_gain_a, own_attn_in, own_forget, own_attn_out, own_gain_f = (
        lax.psum_scatter(
            gain_a_grad.astype(jnp.bfloat16), "fsdp", scatter_dimension=0, tiled=True
        ).astype(jnp.float32),
        lax.psum_scatter(
            in_attn_full.astype(jnp.bfloat16), "fsdp", scatter_dimension=0, tiled=True
        ).astype(jnp.float32),
        lax.psum_scatter(
            forget_full.astype(jnp.bfloat16), "fsdp", scatter_dimension=0, tiled=True
        ).astype(jnp.float32),
        lax.psum_scatter(
            out_full.astype(jnp.bfloat16), "fsdp", scatter_dimension=0, tiled=True
        ).astype(jnp.float32),
        lax.psum_scatter(
            gain_f_grad.astype(jnp.bfloat16), "fsdp", scatter_dimension=0, tiled=True
        ).astype(jnp.float32),
    )
    own_gain_a, own_attn_in, own_forget, own_attn_out, own_gain_f, grad_ffn_in, grad_ffn_down = (
        lax.psum(own_gain_a.astype(jnp.bfloat16), "rep").astype(jnp.float32),
        lax.psum(own_attn_in.astype(jnp.bfloat16), "rep").astype(jnp.float32),
        lax.psum(own_forget.astype(jnp.bfloat16), "rep").astype(jnp.float32),
        lax.psum(own_attn_out.astype(jnp.bfloat16), "rep").astype(jnp.float32),
        lax.psum(own_gain_f.astype(jnp.bfloat16), "rep").astype(jnp.float32),
        lax.psum(grad_ffn_in.astype(jnp.bfloat16), "rep").astype(jnp.float32),
        lax.psum(grad_ffn_down.astype(jnp.bfloat16), "rep").astype(jnp.float32),
    )
    valid_rows = valid_mask[0].astype(jnp.float32)
    valid_col = valid_rows[:, None]
    square_sums = jnp.stack(
        [
            jnp.sum(result * result * valid_col),
            jnp.sum(branch_attn * branch_attn * valid_col),
            jnp.sum(branch_ffn * branch_ffn * valid_col),
            jnp.sum(valid_rows),
        ]
    )
    square_sums, bias_total = lax.psum((square_sums, bias_grad), ("rep", "fsdp"))
    stats = jnp.sqrt(square_sums[:3] / (square_sums[3] * model_width) + EPSILON)
    return (
        result.astype(jnp.bfloat16)[None],
        input_grad[None],
        own_gain_a,
        own_attn_in,
        own_forget,
        bias_total,
        own_attn_out,
        own_gain_f,
        grad_ffn_in,
        grad_ffn_down,
        stats,
    )


def solution(mesh):
    placed = (
        P(("rep", "fsdp"), None, None),
        P(("rep", "fsdp"), None, None),
        P(("rep", "fsdp")),
        P(("rep", "fsdp"), None),
        P("fsdp"),
        P("fsdp", None),
        P("fsdp", None),
        P(),
        P("fsdp", None),
        P("fsdp"),
        P(None, None, "fsdp"),
        P("fsdp", None),
    )
    return jax.shard_map(
        per_device,
        mesh=mesh,
        in_specs=placed,
        out_specs=(
            P(("rep", "fsdp"), None, None),
            P(("rep", "fsdp"), None, None),
            P("fsdp"),
            P("fsdp", None),
            P("fsdp", None),
            P(),
            P("fsdp", None),
            P("fsdp"),
            P(None, None, "fsdp"),
            P("fsdp", None),
            P(),
        ),
        check_vma=False,
    )
```

profile of v0, /device:TPU:0, one launch (start us, length us, event | category | flops | bytes accessed | tf_op | source)
XLA Modules:
  0.0 1277.3 jit_solution(15114645129558079692)
XLA Ops:
  7.2 0.7 all-gather.6.cloned.1.call-update
  8.0 0.7 all-gather.8.cloned.1.call-update
  8.8 0.7 all-gather.10.cloned.1.call-update
  9.5 0.5 all-gather.12.cloned.1.call-update
  10.8 0.6 fusion.100
  12.6 37.8 %all-reduce.6 = (bf16[1536]{0:T(1024)(128)(2,1)S(1)}, bf16[1536]{0:T(1024)(128)(2,1)S(1)}) all-reduce(bf16[1536]{0:T(1024)(128)(2,1)S(1)} %dynamic-update-slice, bf16[1536]{0:T(1024)(128)(2,1)S(1)} %dynamic-update-slice.1), channel_id=1, replica_groups=mesh['rep'=2,'fsdp'=16] {'fsdp'}, use_global_device_ids=true, to_apply=%add | all-reduce | flops 3072 | bytes 12288
  50.4 18.3 %all-gather = bf16[16,96,24]{1,2,0:T(8,128)(2,1)S(1)} all-gather(bf16[1,96,24]{1,2,0:T(8,128)(2,1)S(1)} %bitcast.162), channel_id=1, replica_groups=mesh['rep'=2,'fsdp'=16] {'fsdp'}, dimensions={0}, use_global_device_ids=true | all-gather | bytes 78336 | tf_op jit(solution)/shard_map/all_gather | solution.py:57
  69.1 0.5 copy-done.31
  69.6 0.9 fusion.64
  70.9 0.5 convert_bitcast_fusion.2
  71.5 41.6 %all-gather.6.cloned.1.call-done = bf16[1536,6144]{1,0:T(8,128)(2,1)} async-done(((bf16[96,6144]{1,0:T(8,128)(2,1)}), bf16[1536,6144]{1,0:T(8,128)(2,1)}) %all-gather.6.cloned.1.call-update) | async-done | bytes 18874384 | tf_op jit(solution)/shard_map/all_gather | solution.py:56
  113.2 10.7 fusion.101
  124.7 0.8 select_reduce_fusion
  125.9 0.6 fusion.42
  126.9 1.3 multiply_convert_fusion.6
  128.3 40.4 %all-gather.8.cloned.1.call-done = bf16[1536,1536]{1,0:T(8,128)(2,1)} async-done(((bf16[96,1536]{1,0:T(8,128)(2,1)}), bf16[1536,1536]{1,0:T(8,128)(2,1)}) %all-gather.8.cloned.1.call-update) | async-done | bytes 4718608 | tf_op jit(solution)/shard_map/all_gather | solution.py:58
  168.7 3.2 multiply_reduce_fusion.6
  171.9 0.5 fusion.77
  172.5 132.0 %all-gather.10.cloned.1.call-done = bf16[2,1536,4096]{2,1,0:T(8,128)(2,1)} async-done(((bf16[2,1536,256]{2,1,0:T(8,128)(2,1)}), bf16[2,1536,4096]{2,1,0:T(8,128)(2,1)}) %all-gather.10.cloned.1.call-update) | async-done | bytes 25165840 | tf_op jit(solution)/shard_map/all_gather | solution.py:104
  304.5 14.1 %convolution_bitcast_fusion = f32[2,128,4096]{2,1,0:T(8,128)} fusion(bf16[2,1536,4096]{2,1,0:T(8,128)(2,1)} %all-gather.10.cloned.1.call-done, f32[128,1536]{1,0:T(8,128)S(1)} %get-tuple-element.140, f32[1536]{0:T(1024)S(1)} %convert_element_type.141, f32[128]{0:T(128)} %fusion.77), kind=kOutput, calls=%fused_computation.5 | convolution fusion | flops 3221815296 | bytes 30153216 | tf_op jit(solution)/shard_map/sd,kdf->ksf/dot_general | solution.py:107
  318.6 86.5 %all-gather.12.cloned.1.call-done = bf16[4096,1536]{1,0:T(8,128)(2,1)} async-done(((bf16[256,1536]{1,0:T(8,128)(2,1)}), bf16[4096,1536]{1,0:T(8,128)(2,1)}) %all-gather.12.cloned.1.call-update) | async-done | bytes 12582928 | tf_op jit(solution)/shard_map/all_gather | solution.py:105
  405.0 11.6 fusion.19
  416.6 14.4 %convolution_bitcast_fusion.1 = f32[128,1536]{1,0:T(8,128)} fusion(bf16[2,1536,4096]{2,1,0:T(8,128)(2,1)} %all-gather.10.cloned.1.call-done, bf16[1,128,4096]{2,1,0:T(8,128)(2,1)} %get-tuple-element.142, bf16[1,128,4096]{2,1,0:T(8,128)(2,1)} %get-tuple-element.141), kind=kOutput, calls=%fused_computation.8 | convolution fusion | flops 3222274048 | bytes 28049408 | tf_op jit(solution)/shard_map/ksf,kdf->sd/dot_general | solution.py:119
  431.1 9.7 multiply_reduce_fusion.3
  441.0 3.6 convolution_convert_fusion.2
  444.6 8.9 convolution_convert_fusion.1
  454.3 0.6 log_add_fusion
  454.9 5.3 multiply_convert_fusion.4
  460.4 3.1 convolution_convert_fusion.4
  463.5 2.0 copy.79
  465.5 2.7 fusion.106
  468.2 3.9 convolution_convert_fusion.5
  472.1 2.0 copy.78
  474.1 3.9 convolution_convert_fusion.6
  478.0 1.9 copy.77
  479.9 10.7 convolution_convert_fusion
  490.7 13.8 %convert_bitcast_fusion = bf16[2,1536,4096]{1,2,0:T(8,128)(2,1)} fusion(bf16[1,128,4096]{2,1,0:T(8,128)(2,1)} %get-tuple-element.142, bf16[1,128,4096]{2,1,0:T(8,128)(2,1)} %get-tuple-element.141, f32[128,1536]{1,0:T(8,128)S(1)} %get-tuple-element.140, f32[1536]{0:T(1024)S(1)} %convert_element_type.141, f32[128]{0:T(128)} %fusion.77), kind=kOutput, calls=%fused_computation.1 | convolution fusion | flops 3235446784 | bytes 28056064 | tf_op jit(solution)/shard_map/sd,ksf->kdf/dot_general | solution.py:118
  504.8 0.7 copy-done.4
  505.6 2.9 fusion.12
  508.5 0.7 subtract_add_fusion
  509.6 0.8 fusion.98
  510.8 0.9 copy.87
  511.8 6.8 reduce-scatter.10.cloned.1.call-done
  518.6 138.0 %reduce-scatter.14.cloned.1.call-done = bf16[256,1536]{1,0:T(8,128)(2,1)} async-done(((bf16[4096,1536]{1,0:T(8,128)(2,1)}), bf16[256,1536]{1,0:T(8,128)(2,1)}) %reduce-scatter.14.cloned.1.call-update) | async-done | bytes 786448 | tf_op jit(solution)/shard_map/reduce_scatter | solution.py:126
  656.7 197.4 %reduce-scatter.8.cloned.1.call-done = bf16[96,6144]{1,0:T(8,128)(2,1)} async-done(((bf16[1536,6144]{1,0:T(8,128)(2,1)}), bf16[96,6144]{1,0:T(8,128)(2,1)}) %reduce-scatter.8.cloned.1.call-update) | async-done | bytes 1179664 | tf_op jit(solution)/shard_map/reduce_scatter | solution.py:202
  854.1 246.6 %reduce-scatter.12.cloned.1.call-done = bf16[2,1536,256]{1,2,0:T(8,128)(2,1)} async-done(((bf16[2,1536,4096]{1,2,0:T(8,128)(2,1)}), bf16[2,1536,256]{1,2,0:T(8,128)(2,1)}) %reduce-scatter.12.cloned.1.call-update) | async-done | bytes 1572880 | tf_op jit(solution)/shard_map/reduce_scatter | solution.py:123
  1101.5 0.6 convert_reduce_fusion
  1102.1 2.7 pad_maximum_fusion.6
  1104.9 39.2 %all-reduce.4 = (f32[24]{0:T(128)}, f32[4]{0:T(128)S(1)}) all-reduce(f32[24]{0:T(128)S(1)} %get-tuple-element.137, f32[4]{0:T(128)S(1)} %pad_maximum_fusion.6), channel_id=1, replica_groups=mesh['rep'=2,'fsdp'=16] {'rep','fsdp'}, use_global_device_ids=true, to_apply=%region_19.20 | all-reduce | flops 28 | bytes 224 | tf_op jit(solution)/shard_map/psum | solution.py:234
  1144.1 0.6 slice.34
  1144.7 12.8 fusion.58
  1157.5 1.4 fusion.25
  1158.9 31.9 %all-reduce.5 = (bf16[1536]{0:T(1024)(128)(2,1)S(1)}, bf16[1536]{0:T(1024)(128)(2,1)S(1)}) all-reduce(bf16[1536]{0:T(1024)(128)(2,1)S(1)} %get-tuple-element.117, bf16[1536]{0:T(1024)(128)(2,1)S(1)} %copy-done.29), channel_id=2, replica_groups=mesh['rep'=2,'fsdp'=16] {'fsdp'}, use_global_device_ids=true, to_apply=%region_12.13.clone | all-reduce | flops 3072 | bytes 12288
  1191.6 0.5 add_sqrt_fusion
  1192.2 1.1 fusion.30
  1193.3 0.8 copy.88
  1194.1 5.3 all-reduce.7
  1199.4 0.5 convert_element_type.152
  1200.4 0.6 convert_element_type.156
  1201.0 60.7 %all-reduce.11.cloned.1.call-done = (bf16[2,1536,256]{1,2,0:T(8,128)(2,1)}, bf16[96,6144]{1,0:T(8,128)(2,1)}, bf16[96,1536]{1,0:T(8,128)(2,1)}, bf16[256,1536]{1,0:T(8,128)(2,1)}) async-done(((bf16[2,1536,256]{1,2,0:T(8,128)(2,1)}, bf16[96,6144]{1,0:T(8,128)(2,1)}, bf16[96,1536]{1,0:T(8,128)(2,1)}, bf16[256,1536]{1,0:T(8,128)(2,1)}), (bf16[2,1536,256]{1,2,0:T(8,128)(2,1)}, bf16[96,6144]{1,0:T(8,128)(2,1)}, ...) | async-done | bytes 3833872 | tf_op jit(solution)/shard_map/psum | solution.py:221
  1261.8 1.8 convert_element_type.158
  1263.6 3.1 copy.81
  1266.7 1.3 convert_element_type.167
  1268.4 1.6 convert_element_type.154
  (129 shorter events, 6.7 us)
Async XLA Ops:
  7.2 106.0 %all-gather.6.cloned.1.call-start = ((), (), s32[]{:S(2)}) async-start(), calls=%async_computation.5 | async-start | bytes 20054016 | tf_op jit(solution)/shard_map/all_gather | solution.py:56
  7.9 2.8 copy-start.35
  7.9 2.9 copy-start.30
  7.9 4.1 copy-start.36
  7.9 4.4 copy-start.37
  8.0 42.5 %copy-start.28 = (bf16[96,24]{0,1:T(8,128)(2,1)S(1)}, bf16[96,24]{0,1:T(8,128)(2,1)}, u32[]{:S(2)}) copy-start(bf16[96,24]{0,1:T(8,128)(2,1)} %param.18) | copy-start | bytes 13828
  8.0 61.0 %copy-start = (bf16[1,128,1536]{2,1,0:T(8,128)(2,1)S(1)}, bf16[1,128,1536]{2,1,0:T(8,128)(2,1)}, u32[]{:S(2)}) copy-start(bf16[1,128,1536]{2,1,0:T(8,128)(2,1)} %param.12) | copy-start | bytes 1179652
  8.0 160.7 %all-gather.8.cloned.1.call-start = ((), (), s32[]{:S(2)}) async-start(), calls=%async_computation.6 | async-start | bytes 5013504 | tf_op jit(solution)/shard_map/all_gather | solution.py:58
  8.7 295.8 %all-gather.10.cloned.1.call-start = ((), (), s32[]{:S(2)}) async-start(), calls=%async_computation.7 | async-start | bytes 26738688 | tf_op jit(solution)/shard_map/all_gather | solution.py:104
  9.5 61.4 %copy-start.38 = (s32[1,128]{1,0:T(1,128)S(1)}, s32[1,128]{1,0:T(1,128)}, u32[]{:S(2)}) copy-start(s32[1,128]{1,0:T(1,128)} %param.15) | copy-start | bytes 1540
  9.5 395.6 %all-gather.12.cloned.1.call-start = ((), (), s32[]{:S(2)}) async-start(), calls=%async_computation.8 | async-start | bytes 13369344 | tf_op jit(solution)/shard_map/all_gather | solution.py:105
  10.0 508.6 %reduce-scatter.10.cloned.1.call-start = ((), (), s32[]{:S(2)}) async-start(), calls=%async_computation.10 | async-start | bytes 5013504 | tf_op jit(solution)/shard_map/reduce_scatter | solution.py:208
  68.9 55.0 %copy-start.17 = (bf16[1536,24]{0,1:T(8,128)(2,1)}, bf16[1536,24]{0,1:T(8,128)(2,1)S(1)}, u32[]{:S(2)}) copy-start(bf16[1536,24]{0,1:T(8,128)(2,1)S(1)} %reshape.224) | copy-start | bytes 221188
  69.1 0.5 copy-start.31
  69.6 54.3 %copy-start.23 = (f32[128]{0:T(128)}, f32[128]{0:T(128)S(1)}, u32[]{:S(2)}) copy-start(f32[128]{0:T(128)S(1)} %fusion.76) | copy-start | bytes 1540
  71.5 53.2 %copy-start.26 = (pred[128,128]{0,1:T(8,128)(4,1)}, pred[128,128]{0,1:T(8,128)(4,1)S(1)}, u32[]{:S(2)}) copy-start(pred[128,128]{0,1:T(8,128)(4,1)S(1)} %get-tuple-element.159) | copy-start | bytes 49156
  71.5 54.4 %copy-start.18 = (pred[128,128]{0,1:T(8,128)(4,1)}, pred[128,128]{0,1:T(8,128)(4,1)S(1)}, u32[]{:S(2)}) copy-start(pred[128,128]{0,1:T(8,128)(4,1)S(1)} %get-tuple-element.160) | copy-start | bytes 49156
  124.3 1.2 copy-start.14
  124.5 1.0 copy-start.15
  124.7 1.2 copy-start.3
  125.5 1.1 copy-start.1
  125.5 1.1 copy-start.19
  125.9 0.8 copy-start.21
  171.9 132.6 %copy-start.33 = (f32[128]{0:T(128)}, f32[128]{0:T(128)S(1)}, u32[]{:S(2)}) copy-start(f32[128]{0:T(128)S(1)} %get-tuple-element.139) | copy-start | bytes 1540
  304.5 100.5 %copy-start.7 = (bf16[1,128,1536]{2,1,0:T(8,128)(2,1)S(1)}, bf16[1,128,1536]{2,1,0:T(8,128)(2,1)}, u32[]{:S(2)}) copy-start(bf16[1,128,1536]{2,1,0:T(8,128)(2,1)} %param.13) | copy-start | bytes 1179652
  431.0 9.7 copy-start.34
  431.1 9.7 copy-start.13
  431.1 9.7 copy-start.27
  444.6 212.1 %reduce-scatter.14.cloned.1.call-start = ((), (), s32[]{:S(2)}) async-start(), calls=%async_computation.12 | async-start | bytes 13369344 | tf_op jit(solution)/shard_map/reduce_scatter | solution.py:126
  453.6 0.7 copy-start.20
  453.6 0.7 copy-start.22
  453.6 400.5 %reduce-scatter.8.cloned.1.call-start = ((), (), s32[]{:S(2)}) async-start(), calls=%async_computation.9 | async-start | bytes 20054016 | tf_op jit(solution)/shard_map/reduce_scatter | solution.py:202
  460.4 3.1 copy-start.5
  463.5 4.7 copy-start.2
  490.6 610.1 %reduce-scatter.12.cloned.1.call-start = ((), (), s32[]{:S(2)}) async-start(), calls=%async_computation.11 | async-start | bytes 26738688 | tf_op jit(solution)/shard_map/reduce_scatter | solution.py:123
  504.5 1.0 copy-start.4
  504.5 1.1 copy-start.6
  504.5 6.0 copy-start.24
  504.5 688.8 %reduce-scatter.16.cloned.1.call-start = ((), (), s32[]{:S(2)}) async-start(), calls=%async_computation.13 | async-start | bytes 417792
  510.5 590.2 %copy-start.25 = (bf16[128,24]{0,1:T(8,128)(2,1)}, bf16[128,24]{0,1:T(8,128)(2,1)S(1)}, u32[]{:S(2)}) copy-start(bf16[128,24]{0,1:T(8,128)(2,1)S(1)} %get-tuple-element.138) | copy-start | bytes 18436
  511.7 750.0 %all-reduce.11.cloned.1.call-start = ((), (), s32[]{:S(2)}) async-start(), calls=%async_computation.14 | async-start | bytes 7667712 | tf_op jit(solution)/shard_map/psum | solution.py:221
  1100.7 0.8 copy-start.39
  1100.7 44.0 %copy-start.8 = (bf16[128,1536]{1,0:T(8,128)(2,1)S(1)}, bf16[128,1536]{1,0:T(8,128)(2,1)}, u32[]{:S(2)}) copy-start(bf16[128,1536]{1,0:T(8,128)(2,1)} %copy.79) | copy-start | bytes 1179652
  1100.7 44.0 %copy-start.9 = (bf16[128,1536]{1,0:T(8,128)(2,1)S(1)}, bf16[128,1536]{1,0:T(8,128)(2,1)}, u32[]{:S(2)}) copy-start(bf16[128,1536]{1,0:T(8,128)(2,1)} %copy.78) | copy-start | bytes 1179652
  1100.7 44.0 %copy-start.10 = (bf16[128,1536]{1,0:T(8,128)(2,1)S(1)}, bf16[128,1536]{1,0:T(8,128)(2,1)}, u32[]{:S(2)}) copy-start(bf16[128,1536]{1,0:T(8,128)(2,1)} %copy.77) | copy-start | bytes 1179652
  1100.7 44.0 %copy-start.16 = (bf16[128,1536]{1,0:T(8,128)(2,1)S(1)}, bf16[128,1536]{1,0:T(8,128)(2,1)}, u32[]{:S(2)}) copy-start(bf16[128,1536]{1,0:T(8,128)(2,1)} %get-tuple-element.144) | copy-start | bytes 1179652
  1157.5 1.4 copy-start.29
  1157.5 34.7 %copy-start.32 = (f32[128]{0:T(128)S(1)}, f32[128]{0:T(128)}, u32[]{:S(2)}) copy-start(f32[128]{0:T(128)} %copy-done.31) | copy-start | bytes 1540
  1263.6 3.1 copy-start.12
  1266.7 1.6 copy-start.11
Sparse Core Ops, SparseCore 0:
  9.6 103.5 all-gather.5
  115.5 53.2 all-gather.7
  170.2 134.2 all-gather.9
  306.6 98.3 all-gather.11
  444.7 73.8 reduce-scatter.9
  522.5 134.0 reduce-scatter.13
  660.8 193.2 reduce-scatter.7
  858.2 242.4 reduce-scatter.11
  1104.2 55.0 reduce-scatter.15
  1161.6 100.0 all-reduce.10
where the time goes:
time: 1290 us; the launch traced here: 1280 us
  waiting for transfers between devices  953 us (74%)
  matrix products  139 us (11%)
  blocking collectives  133 us (10%)
  between operations  17.9 us (1%)
  other arithmetic  17.3 us (1%)
  local copies, waits for them, and re-layouts  16.8 us (1%)
    reduce_scatter x1, waiting for transfers between devices, per_device(): lax.psum_scatter(in_full.astype(jnp.bfloat16), 'fsdp', scatter_dimension=...  247 us
    reduce_scatter x1, waiting for transfers between devices, per_device(): lax.psum_scatter(in_attn_full.astype(jnp.bfloat16), 'fsdp', scatter_dimen...  197 us
    reduce_scatter x1, waiting for transfers between devices, per_device(): lax.psum_scatter(down_full.astype(jnp.bfloat16), 'fsdp', scatter_dimensio...  138 us
    all_gather x1, waiting for transfers between devices, per_device(): lax.all_gather(ffn_in, 'fsdp', axis=2, tiled=True)  132 us
    all_gather x1, waiting for transfers between devices, per_device(): lax.all_gather(ffn_down, 'fsdp', axis=0, tiled=True)  86.5 us
    unnamed x2, blocking collectives  69.7 us
    psum x1, waiting for transfers between devices, per_device(): lax.psum(grad_ffn_in.astype(jnp.bfloat16), 'rep').astype(jnp.float32)  60.7 us
    all_gather x1, waiting for transfers between devices, per_device(): lax.all_gather(attn_in, 'fsdp', axis=0, tiled=True)  41.6 us
  transfers between devices with their start and end apart: 10, of which 9 were waited for; matrix products, arithmetic and copies ran while one was open for 10% of the time, Pallas kernels for 0%

commit v1 on v0

v1 whole, which is shorter than its diff:
```python
import functools

import jax
import jax.numpy as jnp
from jax import lax
from jax.experimental import pallas as pl
from jax.experimental.pallas import tpu as pltpu
from jax.sharding import PartitionSpec as P

H = 24
HD = 64
PIC = 32
TP = 8
DEPTH = 4
EPSILON = 1e-06
NEGATIVE = -1e30
MESH = pl.DeviceIdType.MESH
BF16 = jnp.bfloat16
F32 = jnp.float32
VMEM = pl.BlockSpec(memory_space=pltpu.VMEM)
ANY = pl.BlockSpec(memory_space=pl.ANY)


class Net:
    def __init__(self, reps, share, sems):
        self.reps, self.share, self.sems = reps, share, sems
        self.r = lax.axis_index("rep")
        self.f = lax.axis_index("fsdp")
        self.t = lax.div(self.f, share)
        self.u = lax.rem(self.f, share)
        self.z = lax.div(self.t, 2)
        self.x = lax.rem(self.t, 2)
        self.taken = 0
        self.sent = []

    def take(self, count=1):
        base = self.taken
        self.taken += count
        return base

    def place(self, t):
        return t * self.share + self.u

    def grid(self, z, x):
        return (z * 2 + x) * self.share + self.u

    def partners(self):
        for k in range(1, self.share):
            yield k, lax.rem(self.u + k, self.share)

    def greet(self, peers):
        barrier = pltpu.get_barrier_semaphore()
        total = 0
        for cond, r, f in peers:
            if cond is None:
                pl.semaphore_signal(barrier, 1, device_id=(r, f), device_id_type=MESH)
                total = total + 1
            else:

                @pl.when(cond)
                def _():
                    pl.semaphore_signal(barrier, 1, device_id=(r, f), device_id_type=MESH)

                total = total + cond.astype(jnp.int32)
        pl.semaphore_wait(barrier, total)

    def plane_peers(self):
        return [
            (self.z < DEPTH - 1, self.r, self.grid(self.z + 1, self.x)),
            (self.z > 0, self.r, self.grid(self.z - 1, self.x)),
            (None, self.r, self.grid(self.z, 1 - self.x)),
        ]

    def share_peers(self):
        return [(None, self.r, self.t * self.share + u) for _, u in self.partners()]

    def rep_peers(self):
        return [(None, lax.rem(self.r + k, self.reps), self.f) for k in range(1, self.reps)]

    def all_plane_peers(self):
        return [(None, self.r, self.place(lax.rem(self.t + k, TP))) for k in range(1, TP)]

    def send(self, src, dst, ssem, rsem, f, r=None, cond=None):
        copy = pltpu.make_async_remote_copy(
            src_ref=src,
            dst_ref=dst,
            send_sem=self.sems.at[ssem],
            recv_sem=self.sems.at[rsem],
            device_id=(self.r if r is None else r, f),
            device_id_type=MESH,
        )
        if cond is None:
            copy.start()
        else:
            pl.when(cond)(copy.start)
        self.sent.append((cond, copy))

    def arrive(self, dst, rsem, cond=None):
        copy = pltpu.make_async_remote_copy(
            src_ref=dst,
            dst_ref=dst,
            send_sem=self.sems.at[rsem],
            recv_sem=self.sems.at[rsem],
            device_id=(self.r, self.f),
            device_id_type=MESH,
        )
        if cond is None:
            copy.wait_recv()
        else:
            pl.when(cond)(copy.wait_recv)

    def drain(self):
        for cond, copy in self.sent:
            if cond is None:
                copy.wait_send()
            else:
                pl.when(cond)(copy.wait_send)
        self.sent = []


class Flood:
    def __init__(self, net, src, dst):
        self.net, self.src, self.dst = net, src, dst
        self.recv = net.take(TP)
        self.up, self.down = net.take(DEPTH), net.take(DEPTH)
        self.side = net.take(2 * DEPTH)

    def step(self, d):
        net = self.net
        z, x = net.z, net.x
        for k, way in enumerate((0,) if d == 0 else (-1, 1)):
            zo = jnp.clip(z + way * d, 0, DEPTH - 1)
            have = None if d == 0 else ((z - d >= 0) if way < 0 else (z + d <= DEPTH - 1))
            origin = zo * 2 + x
            dst = self.dst(origin)
            src = self.src if d == 0 else dst
            if d:
                net.arrive(dst, self.recv + origin, have)

            def also(cond):
                return cond if have is None else have & cond

            if way <= 0:
                net.send(
                    src, dst, self.up + d, self.recv + origin,
                    net.grid(jnp.minimum(z + 1, DEPTH - 1), x), cond=also(z < DEPTH - 1),
                )
            if way >= 0:
                net.send(
                    src, dst, self.down + d, self.recv + origin,
                    net.grid(jnp.maximum(z - 1, 0), x), cond=also(z > 0),
                )
            net.send(src, dst, self.side + 2 * d + k, self.recv + origin, net.grid(z, 1 - x), cond=have)

    def finish(self):
        for zo in range(DEPTH):
            origin = zo * 2 + 1 - self.net.x
            self.net.arrive(self.dst(origin), self.recv + origin)


def flood_all(floods):
    for d in range(DEPTH):
        for flood in floods:
            flood.step(d)
    for flood in floods:
        flood.finish()


class Collect:
    def __init__(self, net, part, side, up, down, stage, out):
        self.net, self.part, self.side, self.up, self.down = net, part, side, up, down
        self.stage, self.out = stage, out
        self.side_send, self.side_recv = net.take(DEPTH), net.take(DEPTH)
        self.up_send, self.up_recv = net.take(DEPTH), net.take(DEPTH)
        self.down_send, self.down_recv = net.take(DEPTH), net.take(DEPTH)

    def targets(self, d):
        z = self.net.z
        if d == 0:
            return [(0, z, None)]
        return [
            (1, jnp.minimum(z + d, DEPTH - 1), z + d <= DEPTH - 1),
            (-1, jnp.maximum(z - d, 0), z - d >= 0),
        ]

    def begin(self, d):
        net = self.net
        for way, zo, have in self.targets(d):
            net.send(
                self.part(zo * 2 + 1 - net.x), self.side(zo), self.side_send + zo, self.side_recv + zo,
                net.grid(net.z, 1 - net.x), cond=have,
            )

    def step(self, d):
        net = self.net
        z = net.z
        for way, zo, have in self.targets(d):

            def run(way=way, zo=zo):
                net.arrive(self.side(zo), self.side_recv + zo)
                if way == 0:
                    net.arrive(self.up(zo), self.up_recv + zo, z > 0)
                    net.arrive(self.down(zo), self.down_recv + zo, z < DEPTH - 1)
                    base = self.part(zo * 2 + net.x)[...].astype(F32) + self.side(zo)[...].astype(F32)
                    self.out[...] = base

                    @pl.when(z > 0)
                    def _():
                        self.out[...] += self.up(zo)[...].astype(F32)

                    @pl.when(z < DEPTH - 1)
                    def _():
                        self.out[...] += self.down(zo)[...].astype(F32)

                    return
                behind, sem = (self.up, self.up_recv) if way > 0 else (self.down, self.down_recv)
                more = z > 0 if way > 0 else z < DEPTH - 1
                net.arrive(behind(zo), sem + zo, more)
                base = self.part(zo * 2 + net.x)[...].astype(F32) + self.side(zo)[...].astype(F32)

                @pl.when(more)
                def _():
                    self.stage(zo)[...] = (base + behind(zo)[...].astype(F32)).astype(BF16)

                @pl.when(jnp.logical_not(more))
                def _():
                    self.stage(zo)[...] = base.astype(BF16)

            if have is None:
                run()
            else:
                pl.when(have)(run)
            if way > 0:
                net.send(
                    self.stage(zo), self.up(zo), self.up_send + zo, self.up_recv + zo,
                    net.grid(jnp.minimum(z + 1, DEPTH - 1), net.x), cond=have,
                )
            if way < 0:
                net.send(
                    self.stage(zo), self.down(zo), self.down_send + zo, self.down_recv + zo,
                    net.grid(jnp.maximum(z - 1, 0), net.x), cond=have,
                )


def collect_all(collects):
    for d in range(DEPTH - 1, -1, -1):
        for collect in collects:
            collect.begin(d)
    for d in range(DEPTH - 1, -1, -1):
        for collect in collects:
            collect.step(d)


def call(body, name, number, operands, in_specs, outs, scratch, sems, limit=60 << 20):
    return pl.pallas_call(
        body,
        name=name,
        out_shape=tuple(shape for shape, _ in outs),
        in_specs=in_specs,
        out_specs=tuple(spec for _, spec in outs),
        scratch_shapes=list(scratch) + [pltpu.SemaphoreType.DMA((sems,))],
        compiler_params=pltpu.CompilerParams(
            collective_id=number, has_side_effects=True, vmem_limit_bytes=limit
        ),
    )(*operands)


def chunk(rows, count, c):
    return pl.ds(c * (rows // count), rows // count)


def opening(reps, share, x, split, small, w_out, ffn_in, ffn_down):
    n = TP * share
    rows, cols = x.shape
    depth, width = split.shape[1:]

    def body(x_ref, w_ref, small_ref, wo_ref, wi_ref, wd_ref, xs, wc, smalls, wos, wis, wds, local, sems):
        net = Net(reps, share, sems)
        net.greet(
            [(None, net.r, lax.rem(net.f + k, n)) for k in range(1, n)]
        )
        own = [
            pltpu.make_async_copy(x_ref, xs.at[net.t], local.at[0]),
            pltpu.make_async_copy(w_ref.at[net.t], wc.at[net.f], local.at[1]),
            pltpu.make_async_copy(small_ref, smalls.at[net.f], local.at[2]),
            pltpu.make_async_copy(wo_ref, wos.at[net.u], local.at[3]),
        ]
        floods = [
            Flood(net, x_ref.at[chunk(rows, 2, c)], lambda t, c=c: xs.at[t, chunk(rows, 2, c)]) for c in range(2)
        ]
        small_send, small_recv = net.take(n), net.take(n)
        w_send, w_recv = net.take(TP), net.take(n)
        w_pass = net.take(share * TP)
        other = net.take(6 * share)
        for k in range(1, n):
            net.send(small_ref, smalls.at[net.f], small_send + k, small_recv + net.f, lax.rem(net.f + k, n))
        for k in range(1, TP):
            t = lax.rem(net.t + k, TP)
            net.send(w_ref.at[t], wc.at[net.f], w_send + k, w_recv + net.f, net.place(t))
        for flood in floods:
            flood.step(0)
        for k, u in net.partners():
            f = net.t * share + u
            slot = share - 1 - k
            net.send(w_ref.at[net.t], wc.at[net.f], w_send, w_recv + net.f, f) if share == 2 else net.send(
                w_ref.at[net.t], wc.at[net.f], other + 5 * share + k, w_recv + net.f, f
            )
            net.send(wo_ref, wos.at[net.u], other + k, other + share + net.u, f)
            net.send(wi_ref, wis.at[slot], other + 2 * share + k, other + 3 * share + slot, f)
            net.send(wd_ref, wds.at[slot], other + 4 * share + k, w_pass + slot, f)
        for copy in own:
            copy.start()
        for d in range(1, DEPTH):
            for flood in floods:
                flood.step(d)
        for k in range(1, TP):
            t = lax.rem(net.t + k, TP)
            source = net.place(t)
            net.arrive(wc.at[source], w_recv + source)
            for j, u in net.partners():
                net.send(
                    wc.at[source], wc.at[source], w_pass + share * k + j, w_recv + source, net.t * share + u
                )
        for k, u in net.partners():
            slot = k - 1
            net.arrive(wos.at[u], other + share + u)
            net.arrive(wis.at[slot], other + 3 * share + slot)
            net.arrive(wds.at[slot], w_pass + slot)
            for t in range(TP):
                net.arrive(wc.at[t * share + u], w_recv + t * share + u)
        for k in range(1, n):
            f = lax.rem(net.f + k, n)
            net.arrive(smalls.at[f], small_recv + f)
        for flood in floods:
            flood.finish()
        net.drain()
        for copy in own:
            copy.wait()

    shape = jax.ShapeDtypeStruct
    return call(
        body, "opening", 1, (x, split, small, w_out, ffn_in, ffn_down), [VMEM, VMEM, VMEM, VMEM, ANY, ANY],
        [
            (shape((TP, rows, cols), BF16), VMEM),
            (shape((n, depth, width), BF16), VMEM),
            (shape((n,) + small.shape, BF16), VMEM),
            (shape((share,) + w_out.shape, BF16), VMEM),
            (shape((share - 1,) + ffn_in.shape, BF16), ANY),
            (shape((share - 1,) + ffn_down.shape, BF16), ANY),
        ],
        [pltpu.SemaphoreType.DMA((4,))], 400,
    )


def gather_plane(reps, share, name, number, blocks, pieces=2):
    count = len(blocks)
    rows = blocks[0].shape[0]

    def body(*refs):
        srcs, dsts, local, sems = refs[:count], refs[count : 2 * count], refs[-2], refs[-1]
        net = Net(reps, share, sems)
        net.greet(net.plane_peers())
        floods = [
            Flood(net, src.at[chunk(rows, pieces, c)], lambda t, c=c, dst=dst: dst.at[t, chunk(rows, pieces, c)])
            for src, dst in zip(srcs, dsts)
            for c in range(pieces)
        ]
        own = [pltpu.make_async_copy(srcs[i], dsts[i].at[net.t], local.at[i]) for i in range(count)]
        for flood in floods:
            flood.step(0)
        for copy in own:
            copy.start()
        for d in range(1, DEPTH):
            for flood in floods:
                flood.step(d)
        for flood in floods:
            flood.finish()
        net.drain()
        for copy in own:
            copy.wait()

    return call(
        body, name, number, blocks, [VMEM] * count,
        [(jax.ShapeDtypeStruct((TP,) + block.shape, block.dtype), VMEM) for block in blocks],
        [pltpu.SemaphoreType.DMA((count,))], 24 * count * pieces,
    )


def scatter_plane(reps, share, name, number, parts, pieces=2):
    count = len(parts)
    _, rows, cols = parts[0].shape

    def body(*refs):
        srcs, outs = refs[:count], refs[count : 2 * count]
        side, up, down, stage, sems = refs[2 * count :]
        net = Net(reps, share, sems)
        net.greet(net.plane_peers())
        collects = []
        for i in range(count):
            for c in range(pieces):
                rc = chunk(rows, pieces, c)
                collects.append(
                    Collect(
                        net,
                        lambda t, i=i, rc=rc: srcs[i].at[t, rc],
                        *[lambda z, i=i, rc=rc, ref=ref: ref.at[i, z, rc] for ref in (side, up, down, stage)],
                        outs[i].at[rc],
                    )
                )
        collect_all(collects)
        net.drain()

    buffer = pltpu.VMEM((count, DEPTH, rows, cols), BF16)
    return call(
        body, name, number, parts, [VMEM] * count,
        [(jax.ShapeDtypeStruct((rows, cols), F32), VMEM)] * count,
        [buffer] * 4, 24 * count * pieces,
    )


def share_sum(reps, share, name, number, own_parts, given_parts):
    count = len(own_parts)

    def body(*refs):
        own, given = refs[:count], refs[count : 2 * count]
        outs = refs[2 * count : 3 * count]
        got = refs[3 * count : 4 * count]
        sems = refs[-1]
        net = Net(reps, share, sems)
        net.greet(net.share_peers() + net.rep_peers())
        first, arrived = net.take(count * share), net.take(count * share)
        away, back = net.take(count * reps), net.take(count * reps)
        for i in range(count):
            for k, u in net.partners():
                slot = share - 1 - k
                net.send(
                    given[i].at[k - 1], got[i].at[slot], first + i * share + k, arrived + i * share + slot,
                    net.t * share + u,
                )
        for i in range(count):
            for slot in range(share - 1):
                net.arrive(got[i].at[slot], arrived + i * share + slot)
            rows = own[i].shape[0]
            step = 256 if rows % 256 == 0 else rows

            @pl.loop(0, rows // step)
            def _(j):
                at = pl.ds(pl.multiple_of(j * step, step), step)
                total = own[i][at].astype(F32)
                for slot in range(share - 1):
                    total = total + got[i][slot, at].astype(F32)
                outs[i][net.r, at] = total.astype(BF16)

            for k in range(1, reps):
                net.send(
                    outs[i].at[net.r], outs[i].at[net.r], away + i * reps + k, back + i * reps + net.r,
                    net.f, r=lax.rem(net.r + k, reps),
                )
        for i in range(count):
            for k in range(1, reps):
                r = lax.rem(net.r + k, reps)
                net.arrive(outs[i].at[r], back + i * reps + r)
        net.drain()

    return call(
        body, name, number, tuple(own_parts) + tuple(given_parts), [VMEM] * (2 * count),
        [(jax.ShapeDtypeStruct((reps,) + part.shape, BF16), VMEM) for part in own_parts],
        [pltpu.VMEM(part.shape, BF16) for part in given_parts], 2 * count * (share + reps),
    )


def exchange_in(reps, share, number, part):
    _, _, depth, width = part.shape

    def body(part_ref, out, got, stage, sems):
        net = Net(reps, share, sems)
        net.greet(net.share_peers() + net.rep_peers() + net.all_plane_peers())
        first, arrived = net.take(TP * share), net.take(TP * share)
        over, landed = net.take(TP), net.take(TP)
        away, back = net.take(TP * reps), net.take(TP * reps)
        for j in range(TP):
            t = lax.rem(net.t + 1 + j, TP)
            for k, u in net.partners():
                slot = share - 1 - k
                net.send(
                    part_ref.at[t, u], got.at[slot, t], first + share * j + k, arrived + share * t + slot,
                    net.t * share + u,
                )
        for j in range(TP):
            t = lax.rem(net.t + 1 + j, TP)
            total = part_ref[t, net.u].astype(F32)
            for slot in range(share - 1):
                net.arrive(got.at[slot, t], arrived + share * t + slot)
                total = total + got[slot, t].astype(F32)
            if j < TP - 1:
                stage[j] = total.astype(BF16)
                net.send(stage.at[j], out.at[net.r, net.t], over + j, landed + net.t, net.place(t))
            else:
                out[net.r, net.t] = total.astype(BF16)
        for j in range(TP):
            t = lax.rem(net.t - j + TP, TP)
            if j:
                net.arrive(out.at[net.r, t], landed + t)
            for k in range(1, reps):
                net.send(
                    out.at[net.r, t], out.at[net.r, t], away + reps * j + k, back + TP * net.r + t,
                    net.f, r=lax.rem(net.r + k, reps),
                )
        for k in range(1, reps):
            r = lax.rem(net.r + k, reps)
            for t in range(TP):
                net.arrive(out.at[r, t], back + TP * r + t)
        net.drain()

    return call(
        body, "exchange_in", number, (part,), [VMEM],
        [(jax.ShapeDtypeStruct((reps, TP, depth, width), BF16), VMEM)],
        [pltpu.VMEM((share - 1, TP, depth, width), BF16), pltpu.VMEM((TP - 1, depth, width), BF16)],
        2 * TP * (share + reps + 1),
    )[0]


def exchange_small(reps, share, number, part):
    n = TP * share

    def body(part_ref, out, local, sems):
        net = Net(reps, share, sems)
        net.greet([(None, net.r, lax.rem(net.f + k, n)) for k in range(1, n)] + net.rep_peers())
        own = pltpu.make_async_copy(part_ref.at[net.f], out.at[net.r, net.f], local.at[0])
        own.start()
        over, landed = net.take(n), net.take(n)
        away, back = net.take(reps), net.take(reps)
        for k in range(1, n):
            f = lax.rem(net.f + k, n)
            net.send(part_ref.at[f], out.at[net.r, net.f], over + k, landed + net.f, f)
        own.wait()
        for k in range(1, n):
            f = lax.rem(net.f + k, n)
            net.arrive(out.at[net.r, f], landed + f)
        for k in range(1, reps):
            net.send(
                out.at[net.r], out.at[net.r], away + k, back + net.r, net.f, r=lax.rem(net.r + k, reps)
            )
        for k in range(1, reps):
            r = lax.rem(net.r + k, reps)
            net.arrive(out.at[r], back + r)
        net.drain()

    return call(
        body, "exchange_small", number, (part,), [VMEM],
        [(jax.ShapeDtypeStruct((reps,) + part.shape, F32), VMEM)],
        [pltpu.SemaphoreType.DMA((1,))], 2 * (n + reps),
    )[0]


def dot(spec, a, b):
    return jnp.einsum(spec, a, b, preferred_element_type=F32)


def per_device(
    reps,
    share,
    tokens,
    cotangent,
    pic_start,
    valid_mask,
    gain_attn,
    attn_in,
    forget_w,
    forget_bias,
    attn_out,
    gain_ffn,
    ffn_in,
    ffn_down,
):
    n = TP * share
    _, seq, model = tokens.shape
    held = attn_in.shape[0]
    heads = H // TP
    width = heads * HD
    f = lax.axis_index("fsdp")
    t = f // share
    u = f % share
    layer_in = tokens[0].astype(F32)

    split = jnp.transpose(attn_in.reshape(held, 4, TP, width), (2, 0, 1, 3)).reshape(TP, held, 4 * width)
    small = jnp.concatenate([forget_w.T, gain_attn[None], gain_ffn[None]])
    small = jnp.pad(small, ((0, 0), (0, 128 - held)))
    marks = jnp.concatenate(
        [valid_mask.astype(BF16), jnp.broadcast_to(pic_start.astype(BF16)[:, None], (1, seq))]
    )
    small = jnp.concatenate([small, marks, jnp.zeros((32 - H - 4, 128), BF16)])
    xs, w_cols, smalls, w_rows, other_in, other_down = opening(
        reps, share, tokens[0], split, small, attn_out, ffn_in, ffn_down
    )
    w_cols = w_cols.reshape(model, 4 * width)
    w_rows = w_rows.reshape(width, model)
    gain_a = smalls[:, H, :held].reshape(model).astype(F32)
    gain_f = smalls[:, H + 1, :held].reshape(model).astype(F32)
    w_forget = lax.dynamic_slice_in_dim(smalls, heads * t, heads, axis=1)[:, :, :held]
    w_forget = jnp.transpose(w_forget, (1, 0, 2)).reshape(heads, model)
    bias = lax.dynamic_slice_in_dim(forget_bias, heads * t, heads).astype(F32)
    plane = smalls.reshape(TP, share, 32, 128)
    plane = lax.dynamic_index_in_dim(plane, u, axis=1, keepdims=False)
    key_valid = plane[:, H + 2] > 0
    starts = plane[:, H + 3, 0].astype(jnp.int32)

    xs = xs.astype(F32)
    inverse = lax.rsqrt(jnp.mean(xs * xs, axis=-1, keepdims=True) + EPSILON)
    rows_a = (xs * inverse * gain_a).astype(BF16).reshape(TP * seq, model)
    projected = dot("sd,de->se", rows_a, w_cols)

    def by_head(k):
        return projected[:, k * width : (k + 1) * width].astype(BF16).reshape(TP, seq, heads, HD)

    queries, keys_all, values_all = by_head(0), by_head(1), by_head(2)
    out_gate = jax.nn.sigmoid(projected[:, 3 * width :])
    forget_logit = (dot("sd,hd->sh", rows_a, w_forget) + bias).reshape(TP, seq, heads)
    decay_sum = jnp.cumsum(jax.nn.log_sigmoid(forget_logit), axis=1)
    positions = jnp.arange(seq, dtype=jnp.int32)
    inside = (positions[None] >= starts[:, None]) & (positions[None] < starts[:, None] + PIC)
    causal = positions[None, :] <= positions[:, None]
    allowed = ((causal[None] | inside[:, :, None] & inside[:, None, :]) & key_valid[:, None, :])[:, None]
    decay_heads = jnp.transpose(decay_sum, (0, 2, 1))
    spread = decay_heads[:, :, :, None] - decay_heads[:, :, None, :]
    decay_bias = jnp.where(causal, spread, -spread)
    scores = dot("gihe,gjhe->ghij", queries, keys_all) * HD ** (-0.5) + decay_bias
    masked = jnp.where(allowed, scores, NEGATIVE)
    row_max = jnp.max(masked, axis=-1, keepdims=True)
    weights = jnp.where(allowed, jnp.exp(masked - row_max), 0.0)
    probability = weights / jnp.sum(weights, axis=-1, keepdims=True)
    prob_low = probability.astype(BF16)
    attended = dot("ghij,gjhe->gihe", prob_low, values_all).reshape(TP * seq, width)
    gated_rows = (attended * out_gate).astype(BF16)
    attn_part = dot("si,io->so", gated_rows, w_rows).astype(BF16).reshape(TP, seq, model)
    (branch_attn,) = scatter_plane(reps, share, "sum_attn", 2, (attn_part,))
    middle = layer_in + branch_attn
    scale_f = lax.rsqrt(jnp.mean(middle * middle, axis=-1, keepdims=True) + EPSILON)
    rows_f_own = (middle * scale_f * gain_f).astype(BF16)

    rows_f, ffn_grad = gather_plane(reps, share, "gather_rows", 3, (rows_f_own, cotangent[0]))
    rows_f = rows_f.reshape(TP * seq, model)
    ffn_grad = ffn_grad.reshape(TP * seq, model)
    ffn_part, rows_part, in_grads, down_grads = 0.0, 0.0, [], []
    for k in range(share):
        w_in = ffn_in if k == 0 else other_in[k - 1]
        w_down = ffn_down if k == 0 else other_down[k - 1]
        gate_part = dot("sd,df->sf", rows_f, w_in[0])
        up_part = dot("sd,df->sf", rows_f, w_in[1])
        gate_sig = jax.nn.sigmoid(gate_part)
        hidden = (gate_part * gate_sig * up_part).astype(BF16)
        ffn_part = ffn_part + dot("sf,fd->sd", hidden, w_down)
        hidden_grad = dot("sd,fd->sf", ffn_grad, w_down)
        down_grads.append(dot("sf,sd->fd", hidden, ffn_grad).astype(BF16))
        gate_grad = (hidden_grad * up_part * gate_sig * (1.0 + gate_part * (1.0 - gate_sig))).astype(BF16)
        up_grad = (hidden_grad * gate_part * gate_sig).astype(BF16)
        in_grads.append(
            jnp.concatenate(
                [dot("sd,sf->df", rows_f, gate_grad).astype(BF16), dot("sd,sf->df", rows_f, up_grad).astype(BF16)]
            )
        )
        rows_part = rows_part + dot("sf,df->sd", gate_grad, w_in[0]) + dot("sf,df->sd", up_grad, w_in[1])
    rows_f_grad, branch_ffn = scatter_plane(
        reps, share, "sum_ffn", 4,
        (rows_part.astype(BF16).reshape(TP, seq, model), ffn_part.astype(BF16).reshape(TP, seq, model)),
    )
    result = middle + branch_ffn
    out_grad = cotangent[0].astype(F32)
    lifted = rows_f_grad * gain_f
    dotted_f = jnp.mean(middle * lifted, axis=-1, keepdims=True)
    middle_grad = out_grad + scale_f * lifted - middle * (scale_f * scale_f * scale_f) * dotted_f
    gain_f_grad = jnp.sum(rows_f_grad * middle * scale_f, axis=0)

    (branch_grad,) = gather_plane(reps, share, "gather_grad", 5, (middle_grad.astype(BF16),))
    ffn_in_sum, ffn_down_sum = share_sum(
        reps, share, "ffn_grads", 6, (in_grads[0], down_grads[0]),
        (jnp.stack(in_grads[1:]), jnp.stack(down_grads[1:])),
    )
    branch_grad = branch_grad.reshape(TP * seq, model)
    gated_grad = dot("so,io->si", branch_grad, w_rows)
    out_part = dot("si,so->io", gated_rows, branch_grad).astype(BF16).reshape(share, width // share, model)
    attended_grad = (gated_grad * out_gate).astype(BF16).reshape(TP, seq, heads, HD)
    outgate_grad = gated_grad * attended * (out_gate * (1.0 - out_gate))
    prob_grad = dot("gihe,gjhe->ghij", attended_grad, values_all)
    score_grad = probability * (prob_grad - jnp.sum(probability * prob_grad, axis=-1, keepdims=True))
    dotted_grad = (score_grad * HD ** (-0.5)).astype(BF16)
    query_grad = dot("ghij,gjhe->gihe", dotted_grad, keys_all)
    key_grad = dot("ghij,gihe->gjhe", dotted_grad, queries)
    value_grad = dot("ghij,gihe->gjhe", prob_low, attended_grad)
    signed = jnp.where(causal, score_grad, -score_grad)
    decay_grad = jnp.sum(signed, axis=-1) - jnp.sum(signed, axis=-2)
    later_sums = jnp.cumsum(decay_grad[..., ::-1], axis=-1)[..., ::-1]
    logit_grad = jnp.transpose(later_sums, (0, 2, 1)) * jax.nn.sigmoid(-forget_logit)
    bias_grad = jnp.sum(logit_grad, axis=(0, 1))
    logit_low = logit_grad.astype(BF16).reshape(TP * seq, heads)
    proj_grad = jnp.concatenate(
        [g.reshape(TP * seq, width) for g in (query_grad, key_grad, value_grad)] + [outgate_grad], axis=1
    ).astype(BF16)
    w_cols_grad = dot("sd,se->de", rows_a, proj_grad).astype(BF16).reshape(TP, share, held, 4 * width)
    forget_part = dot("sh,sd->hd", logit_low, rows_a)
    rows_a_part = dot("se,de->sd", proj_grad, w_cols) + dot("sh,hd->sd", logit_low, w_forget)
    (rows_a_grad,) = scatter_plane(
        reps, share, "sum_rows", 7, (rows_a_part.astype(BF16).reshape(TP, seq, model),)
    )
    own_out = lax.dynamic_index_in_dim(out_part, u, axis=0, keepdims=False)
    given_out = jnp.stack(
        [lax.dynamic_index_in_dim(out_part, (u + k) % share, axis=0, keepdims=False) for k in range(1, share)]
    )
    (out_sum,) = share_sum(reps, share, "out_grads", 8, (own_out,), (given_out,))
    in_sum = exchange_in(reps, share, 9, w_cols_grad)
    scale_a = lax.rsqrt(jnp.mean(layer_in * layer_in, axis=-1, keepdims=True) + EPSILON)
    lifted = rows_a_grad * gain_a
    dotted_a = jnp.mean(layer_in * lifted, axis=-1, keepdims=True)
    input_grad = middle_grad + scale_a * lifted - layer_in * (scale_a * scale_a * scale_a) * dotted_a
    gain_a_grad = jnp.sum(rows_a_grad * layer_in * scale_a, axis=0)

    valid_rows = valid_mask[0].astype(F32)
    valid_col = valid_rows[:, None]
    scalars = jnp.stack(
        [
            jnp.sum(result * result * valid_col),
            jnp.sum(branch_attn * branch_attn * valid_col),
            jnp.sum(branch_ffn * branch_ffn * valid_col),
            jnp.sum(valid_rows),
        ]
    )
    scalars = jnp.concatenate([scalars, bias_grad, jnp.zeros((held - 4 - heads,), F32)])
    tiles = jnp.concatenate(
        [
            gain_a_grad.reshape(1, n, held),
            gain_f_grad.reshape(1, n, held),
            forget_part.reshape(heads, n, held),
            jnp.broadcast_to(scalars, (1, n, held)),
            jnp.zeros((8 - heads - 3, n, held), F32),
        ]
    )
    tiles = jnp.pad(jnp.transpose(tiles, (1, 0, 2)), ((0, 0), (0, 0), (0, 128 - held)))
    gathered = exchange_small(reps, share, 10, tiles)
    grad_gain_a = jnp.sum(gathered[:, :, 0, :held], axis=(0, 1))
    grad_gain_f = jnp.sum(gathered[:, :, 1, :held], axis=(0, 1))
    by_chip = gathered.reshape(reps, TP, share, 8, 128)
    grad_forget = jnp.sum(by_chip[:, :, :, 2 : 2 + heads, :held], axis=(0, 2)).reshape(H, held).T
    square_sums = jnp.sum(gathered[:, :, 2 + heads, :4], axis=(0, 1))
    bias_total = jnp.sum(by_chip[:, :, :, 2 + heads, 4 : 4 + heads], axis=(0, 2)).reshape(H)
    stats = jnp.sqrt(square_sums[:3] / (square_sums[3] * model) + EPSILON)

    def over_reps(values_in):
        return jnp.sum(values_in.astype(F32), axis=0)

    grad_in = over_reps(in_sum).reshape(TP, held, 4, width)
    grad_in = jnp.transpose(grad_in, (1, 2, 0, 3)).reshape(held, 4 * model)
    return (
        result.astype(BF16)[None],
        input_grad[None],
        grad_gain_a,
        grad_in,
        grad_forget,
        bias_total,
        over_reps(out_sum),
        grad_gain_f,
        over_reps(ffn_in_sum).reshape(ffn_in.shape),
        over_reps(ffn_down_sum),
        stats,
    )


def solution(mesh):
    placed = (
        P(("rep", "fsdp"), None, None),
        P(("rep", "fsdp"), None, None),
        P(("rep", "fsdp")),
        P(("rep", "fsdp"), None),
        P("fsdp"),
        P("fsdp", None),
        P("fsdp", None),
        P(),
        P("fsdp", None),
        P("fsdp"),
        P(None, None, "fsdp"),
        P("fsdp", None),
    )
    return jax.shard_map(
        functools.partial(per_device, mesh.shape["rep"], mesh.shape["fsdp"] // TP),
        mesh=mesh,
        in_specs=placed,
        out_specs=(
            P(("rep", "fsdp"), None, None),
            P(("rep", "fsdp"), None, None),
            P("fsdp"),
            P("fsdp", None),
            P("fsdp", None),
            P(),
            P("fsdp", None),
            P("fsdp"),
            P(None, None, "fsdp"),
            P("fsdp", None),
            P(),
        ),
        check_vma=False,
    )
```

time: 1290 us -> 661 us (0.51)
  waiting for transfers between devices: 953 us -> 0 us
  Pallas kernels: 0 us -> 457 us
  blocking collectives: 133 us -> 0 us
  matrix products: 139 us -> 84 us
  local copies, waits for them, and re-layouts: 16.8 us -> 57.6 us
  other arithmetic: 17.3 us -> 51.5 us
  between operations: 17.9 us -> 2.97 us
    reduce_scatter x4 -> x0, waiting for transfers between devices: 589 us -> none  [the longest x1 247 us: per_device(): lax.psum_scatter(in_full.astype(jnp.bfloat16), 'fsdp', scatter_dimension=...]
    pallas_call x0 -> x10, Pallas kernels: none -> 457 us  [call(): pl.pallas_call(body, name=name, out_shape=tuple((shape for shape, _ in ou...]
    all_gather x4 -> x0, waiting for transfers between devices: 301 us -> none  [the longest x1 132 us: per_device(): lax.all_gather(ffn_in, 'fsdp', axis=2, tiled=True)]
    unnamed x2 -> x0, blocking collectives: 69.7 us -> none
    psum x1 -> x0, waiting for transfers between devices: 60.7 us -> none  [per_device(): lax.psum(grad_ffn_in.astype(jnp.bfloat16), 'rep').astype(jnp.float32)]
    dot_general x21 -> x32, matrix products: 136 us -> 79.9 us  [dot(): return jnp.einsum(spec, a, b, preferred_element_type=F32)]
    psum x2 -> x0, blocking collectives: 44.5 us -> none  [the longest x1 39.2 us: per_device(): lax.psum((square_sums, bias_grad), ('rep', 'fsdp'))]
    reduce_sum x3 -> x13, other arithmetic: 1.33 us -> 26.7 us  [the longest x4 11.7 us: over_reps(): return jnp.sum(values_in.astype(F32), axis=0)]
  transfers between devices with their start and end apart: 10 -> 0, of which waited for: 9 -> 0; matrix products, arithmetic and copies ran while one was open for 10% -> 0% of each run, Pallas kernels for 0% -> 0%
where the time goes in v1:
time: 661 us; the launch traced here: 653 us
  Pallas kernels  457 us (69%)
  matrix products  84 us (13%)
  local copies, waits for them, and re-layouts  57.6 us (9%)
  other arithmetic  51.5 us (8%)
    pallas_call x10, Pallas kernels, call(): pl.pallas_call(body, name=name, out_shape=tuple((shape for shape, _ in ou...  457 us
    dot_general x32, matrix products, dot(): return jnp.einsum(spec, a, b, preferred_element_type=F32)  79.9 us

profile of v1, /device:TPU:0, one launch (start us, length us, event | category | flops | bytes accessed | tf_op | source)
XLA Modules:
  0.0 653.1 jit_solution(10034027330502172316)
XLA Ops:
  0.6 3.0 reshape.320
  4.3 2.2 reshape.321.w_ref
  8.6 71.2 %opening.1 = (bf16[8,128,1536]{2,1,0:T(8,128)(2,1)}, bf16[16,96,768]{2,1,0:T(8,128)(2,1)}, bf16[16,32,128]{2,1,0:T(8,128)(2,1)}, bf16[2,96,1536]{2,1,0:T(8,128)(...) custom-call(bf16[128,1536]{1,0:T(8,128)(2,1)} %bitcast.262, bf16[8,96,768]{2,1,0:T(8,128)(2,1)} %reshape.321.w_ref, ...), custom_call_target="tpu_custom_call" | custom-call | tf_op jit(solution)/shard_map/opening/pallas_call | solution.py:255
  80.7 2.7 fusion.2
  85.2 4.4 fusion.111
  93.4 1.4 reshape.328
  94.8 2.2 divide_bitcast_fusion
  97.7 1.7 copy.143
  99.4 2.0 fusion.117
  101.4 1.8 copy.144
  103.8 1.5 constant_dynamic-slice_fusion.1
  105.3 2.2 copy.138
  107.4 1.4 compare_bitcast_fusion
  108.8 1.3 copy.139
  111.6 1.7 or_and_fusion
  113.3 1.8 copy.169
  115.2 1.8 copy.168
  117.0 4.2 fusion.112
  121.1 1.8 convolution_bitcast_fusion
  124.2 1.4 fusion.26
  125.6 2.7 convolution_convert_fusion
  128.3 40.4 %sum_attn.1 = f32[128,1536]{1,0:T(8,128)} custom-call(bf16[8,128,1536]{2,1,0:T(8,128)(2,1)} %bitcast.253), custom_call_target="tpu_custom_call" | custom-call | tf_op jit(solution)/shard_map/sum_attn/pallas_call | solution.py:255
  168.7 2.2 multiply_reduce_fusion.6
  171.5 2.0 multiply_convert_fusion.8.refs_0_
  173.5 72.8 %gather_rows.1 = (bf16[8,128,1536]{2,1,0:T(8,128)(2,1)}, bf16[8,128,1536]{2,1,0:T(8,128)(2,1)}) custom-call(bf16[128,1536]{1,0:T(8,128)(2,1)} %multiply_convert_fusion.8.refs_0_, bf16[128,1536]{1,0:T(8,128)(2,1)} %bitcast.269), custom_call_target="tpu_custom_call" | custom-call | tf_op jit(solution)/shard_map/gather_rows/pallas_call | solution.py:255
  246.3 3.2 fusion.32
  252.0 2.2 multiply_convert_fusion.1
  261.3 3.8 add_convert_fusion.2
  266.1 2.7 add_convert_fusion.1
  268.8 71.8 %sum_ffn.1 = (f32[128,1536]{1,0:T(8,128)}, f32[128,1536]{1,0:T(8,128)}) custom-call(bf16[8,128,1536]{2,1,0:T(8,128)(2,1)} %bitcast.260, bf16[8,128,1536]{2,1,0:T(8,128)(2,1)} %bitcast.257), custom_call_target="tpu_custom_call" | custom-call | tf_op jit(solution)/shard_map/sum_ffn/pallas_call | solution.py:255
  340.6 3.7 multiply_reduce_fusion.1
  345.6 35.7 %gather_grad.1 = bf16[8,128,1536]{2,1,0:T(8,128)(2,1)} custom-call(bf16[128,1536]{1,0:T(8,128)(2,1)} %get-tuple-element.50.refs_0_), custom_call_target="tpu_custom_call" | custom-call | tf_op jit(solution)/shard_map/gather_grad/pallas_call | solution.py:255
  381.3 4.4 fusion.56
  387.6 1.6 fusion.60
  389.2 4.4 fusion.15
  395.7 4.3 fusion.14
  401.4 7.5 %fusion.76 = f32[1024,1536]{1,0:T(8,128)} fusion(bf16[1536,768]{1,0:T(8,128)(2,1)} %bitcast.313, bf16[1024,192]{0,1:T(8,128)(2,1)} %get-tuple-element.55, bf16[1024,192]{0,1:T(8,128)(2,1)} %bitcast.288, bf16[1024,192]{0,1:T(8,128)(2,1)} %bitcast.290, bf16[1024,192]{0,1:T(8,128)(2,1)S(1)} %bitcast.292), kind=kOutput, calls=%fused_computation.135 | convolution fusion | flops 2422210560 | bytes 10223616 | tf_op jit(solution)/shard_map/se,de->sd/dot_general | solution.py:557
  411.4 5.5 add_convert_fusion
  416.9 35.8 %sum_rows.1 = f32[128,1536]{1,0:T(8,128)} custom-call(bf16[8,128,1536]{2,1,0:T(8,128)(2,1)} %bitcast.259), custom_call_target="tpu_custom_call" | custom-call | tf_op jit(solution)/shard_map/sum_rows/pallas_call | solution.py:255
  452.7 1.4 fusion.25
  454.1 2.5 fusion.22
  458.0 2.8 copy.161
  460.8 3.6 fusion.120
  465.0 2.6 concatenate.25
  468.2 1.5 concatenate.26
  469.7 1.5 pad.9.part_ref
  471.2 12.0 %exchange_small.1 = f32[2,16,8,128]{3,2,1,0:T(8,128)} custom-call(f32[16,8,128]{2,1,0:T(8,128)} %pad.9.part_ref), custom_call_target="tpu_custom_call" | custom-call | tf_op jit(solution)/shard_map/exchange_small/pallas_call | solution.py:255
  483.2 1.5 slice_reduce_fusion.3
  484.8 5.2 convolution_convert_fusion.1
  490.0 42.7 %exchange_in.1 = bf16[2,8,96,768]{3,2,1,0:T(8,128)(2,1)} custom-call(bf16[8,2,96,768]{3,2,1,0:T(8,128)(2,1)} %bitcast.266), custom_call_target="tpu_custom_call" | custom-call | tf_op jit(solution)/shard_map/exchange_in/pallas_call | solution.py:255
  532.7 3.7 convert_reduce_fusion.1
  536.4 3.6 reshape.346
  540.1 3.5 copy.162
  543.6 4.6 reshape.347
  551.3 1.6 convolution_convert_fusion.8
  552.9 2.0 constant_dynamic-slice_fusion
  554.9 12.8 %out_grads.1 = bf16[2,96,1536]{2,1,0:T(8,128)(2,1)} custom-call(bf16[96,1536]{1,0:T(8,128)(2,1)} %get-tuple-element.67.refs_0_, bf16[1,96,1536]{2,1,0:T(8,128)(2,1)} %get-tuple-element.66.refs_1_), custom_call_target="tpu_custom_call" | custom-call | tf_op jit(solution)/shard_map/out_grads/pallas_call | solution.py:255
  567.6 2.0 convert_reduce_fusion.3
  569.7 3.1 convolution_convert_fusion.6
  575.1 1.9 convolution_convert_fusion.5.refs_1_
  580.4 1.9 fusion.5.refs_3_
  582.3 61.8 %ffn_grads.1 = (bf16[2,3072,256]{2,1,0:T(8,128)(2,1)}, bf16[2,256,1536]{2,1,0:T(8,128)(2,1)}) custom-call(bf16[3072,256]{1,0:T(8,128)(2,1)} %pad_maximum_fusion.1.refs_0_, bf16[256,1536]{1,0:T(8,128)(2,1)} %convolution_convert_fusion.5.refs_1_, bf16[1,3072,256]{2,1,0:T(8,128)(2,1)} %maximum_bitcast_fusion.refs_2_, bf16[1,256,1536]{2,1,0:T(8,128)(2,1)} %fusion.5.refs_3_), custom_call_target="tpu_custom_call" | custom-call | tf_op jit(solution)/shard_map/ffn_grads/pallas_call | solution.py:255
  644.2 4.5 convert_reduce_fusion
  648.7 1.4 convert_reduce_fusion.2
  (179 shorter events, 46.1 us)
Async XLA Ops:
  3.7 2.9 copy-start.49
  3.7 3.4 copy-start.37
  3.7 3.4 copy-start.42
  3.7 3.4 copy-start.43
  80.7 2.8 copy-start.2
  83.6 1.7 copy-start.48
  90.6 30.5 %copy-start.16 = (bf16[24,8,8,128]{3,2,1,0:T(8,128)(2,1)}, bf16[24,8,8,128]{3,2,1,0:T(8,128)(2,1)S(1)}, u32[]{:S(2)}) copy-start(bf16[24,8,8,128]{3,2,1,0:T(8,128)(2,1)S(1)} %copy.167) | copy-start | bytes 1179652
  122.9 2.8 copy-start.27
  123.4 0.9 copy-start.10
  125.6 2.7 copy-start.6
  128.3 40.4 %copy-start.3 = (bf16[1,128,1536]{2,1,0:T(8,128)(2,1)S(1)}, bf16[1,128,1536]{2,1,0:T(8,128)(2,1)}, u32[]{:S(2)}) copy-start(bf16[1,128,1536]{2,1,0:T(8,128)(2,1)} %param.12) | copy-start | bytes 1179652
  246.3 3.2 copy-start.26
  246.3 3.3 copy-start.44
  249.6 1.4 copy-start.12
  249.6 2.4 copy-start.46
  254.2 1.0 copy-start.18
  254.2 1.6 copy-start.5
  255.8 1.1 copy-start.8
  259.2 1.1 copy-start.20
  259.2 1.1 copy-start.22
  259.2 5.9 copy-start.24
  265.1 1.0 copy-start.29
  268.8 71.8 %copy-start.1 = (f32[128,1536]{1,0:T(8,128)S(1)}, f32[128,1536]{1,0:T(8,128)}, u32[]{:S(2)}) copy-start(f32[128,1536]{1,0:T(8,128)} %get-tuple-element.53) | copy-start | bytes 2359300
  268.8 71.8 %copy-start.41 = (f32[128]{0:T(128)S(1)}, f32[128]{0:T(128)}, u32[]{:S(2)}) copy-start(f32[128]{0:T(128)} %get-tuple-element.77) | copy-start | bytes 1540
  340.6 3.8 copy-start.9
  340.6 3.8 copy-start.15
  345.6 35.7 %copy-start.11 = (f32[8,128,3,64]{1,0,3,2:T(8,128)S(1)}, f32[8,128,3,64]{1,0,3,2:T(8,128)}, u32[]{:S(2)}) copy-start(f32[8,128,3,64]{1,0,3,2:T(8,128)} %copy-done.10) | copy-start | bytes 2359300
  381.3 4.5 copy-start.51
  381.3 4.5 copy-start.53
  385.9 1.8 copy-start.17
  389.2 6.5 copy-start.31
  401.4 7.6 %copy-start.33 = (bf16[24,8,8,128]{3,1,2,0:T(8,128)(2,1)}, bf16[24,8,8,128]{3,1,2,0:T(8,128)(2,1)S(1)}, u32[]{:S(2)}) copy-start(bf16[24,8,8,128]{3,1,2,0:T(8,128)(2,1)S(1)} %copy.225) | copy-start | bytes 1179652
  401.4 7.6 %copy-start.13 = (f32[8,3,128,128]{2,3,1,0:T(8,128)S(1)}, f32[8,3,128,128]{2,3,1,0:T(8,128)}, u32[]{:S(2)}) copy-start(f32[8,3,128,128]{2,3,1,0:T(8,128)} %fusion.60) | copy-start | bytes 4718596
  401.4 7.5 %copy-start.36 = (pred[128,128]{0,1:T(8,128)(4,1)S(1)}, pred[128,128]{0,1:T(8,128)(4,1)}, u32[]{:S(2)}) copy-start(pred[128,128]{0,1:T(8,128)(4,1)} %iota_compare_fusion) | copy-start | bytes 49156
  401.4 7.5 %copy-start.52 = (f32[8,3,128,128]{2,3,1,0:T(8,128)S(1)}, f32[8,3,128,128]{2,3,1,0:T(8,128)}, u32[]{:S(2)}) copy-start(f32[8,3,128,128]{2,3,1,0:T(8,128)} %get-tuple-element.82) | copy-start | bytes 4718596
  401.4 7.5 %copy-start.54 = (f32[8,3,128]{2,1,0:T(4,128)S(1)}, f32[8,3,128]{2,1,0:T(4,128)}, u32[]{:S(2)}) copy-start(f32[8,3,128]{2,1,0:T(4,128)} %get-tuple-element.81) | copy-start | bytes 36868
  409.0 1.8 copy-start.35
  409.0 2.4 copy-start.34
  416.9 35.8 %copy-start.4 = (bf16[1,128,1536]{2,1,0:T(8,128)(2,1)S(1)}, bf16[1,128,1536]{2,1,0:T(8,128)(2,1)}, u32[]{:S(2)}) copy-start(bf16[1,128,1536]{2,1,0:T(8,128)(2,1)} %param.12) | copy-start | bytes 1179652
  416.9 35.8 %copy-start.38 = (f32[128]{0:T(128)S(1)}, f32[128]{0:T(128)}, u32[]{:S(2)}) copy-start(f32[128]{0:T(128)} %get-tuple-element.74) | copy-start | bytes 1540
  416.9 37.2 %copy-start.40 = (f32[128]{0:T(128)S(1)}, f32[128]{0:T(128)}, u32[]{:S(2)}) copy-start(f32[128]{0:T(128)} %get-tuple-element.73) | copy-start | bytes 1540
  460.8 3.6 copy-start.50
  460.8 4.2 copy-start.39
  460.8 24.0 %copy-start.32 = (bf16[24,8,8,128]{3,1,2,0:T(8,128)(2,1)S(1)}, bf16[24,8,8,128]{3,1,2,0:T(8,128)(2,1)}, u32[]{:S(2)}) copy-start(bf16[24,8,8,128]{3,1,2,0:T(8,128)(2,1)} %copy.223) | copy-start | bytes 1179652
  543.6 7.7 %copy-start = (bf16[8,128,1536]{2,1,0:T(8,128)(2,1)S(1)}, bf16[8,128,1536]{2,1,0:T(8,128)(2,1)}, u32[]{:S(2)}) copy-start(bf16[8,128,1536]{2,1,0:T(8,128)(2,1)} %gather_grad.1) | copy-start | bytes 9437188
  543.6 7.7 %copy-start.7 = (bf16[1024,192]{0,1:T(8,128)(2,1)S(1)}, bf16[1024,192]{0,1:T(8,128)(2,1)}, u32[]{:S(2)}) copy-start(bf16[1024,192]{0,1:T(8,128)(2,1)} %copy-done.6) | copy-start | bytes 1179652
  552.9 16.8 %copy-start.23 = (bf16[1024,256]{1,0:T(8,128)(2,1)S(1)}, bf16[1024,256]{1,0:T(8,128)(2,1)}, u32[]{:S(2)}) copy-start(bf16[1024,256]{1,0:T(8,128)(2,1)} %copy-done.22) | copy-start | bytes 1572868
  569.7 3.1 copy-start.21
  569.7 3.1 copy-start.47
  572.8 2.3 copy-start.45
  573.8 1.3 copy-start.25
  575.1 1.9 copy-start.28
  577.0 1.0 copy-start.19
  579.1 1.3 copy-start.30
  644.1 4.6 copy-start.14

commit v2 on v0

v2 whole, which is shorter than its diff:
```python
import functools

import jax
import jax.numpy as jnp
from jax import lax
from jax.experimental import pallas as pl
from jax.experimental.pallas import tpu as pltpu
from jax.sharding import PartitionSpec as P

H = 24
HD = 64
PIC = 32
TP = 8
DEPTH = 4
EPSILON = 1e-06
NEGATIVE = -1e30
MESH = pl.DeviceIdType.MESH
BF16 = jnp.bfloat16
F32 = jnp.float32
VMEM = pl.BlockSpec(memory_space=pltpu.VMEM)
ANY = pl.BlockSpec(memory_space=pl.ANY)


class Net:
    def __init__(self, reps, share, sems):
        self.reps, self.share, self.sems = reps, share, sems
        self.r = lax.axis_index("rep")
        self.f = lax.axis_index("fsdp")
        self.t = lax.div(self.f, share)
        self.u = lax.rem(self.f, share)
        self.z = lax.div(self.t, 2)
        self.x = lax.rem(self.t, 2)
        self.none = self.f * 0
        self.taken = 0
        self.sent = []

    def take(self, count=1):
        base = self.taken
        self.taken += count
        return base

    def place(self, t):
        return t * self.share + self.u

    def grid(self, z, x):
        return (z * 2 + x) * self.share + self.u

    def partners(self):
        for k in range(1, self.share):
            yield k, lax.rem(self.u + k, self.share)

    def greet(self, peers):
        barrier = pltpu.get_barrier_semaphore()
        total = 0
        for cond, r, f in peers:
            if cond is None:
                pl.semaphore_signal(barrier, 1, device_id=(r, f), device_id_type=MESH)
                total = total + 1
            else:

                @pl.when(cond)
                def _():
                    pl.semaphore_signal(barrier, 1, device_id=(r, f), device_id_type=MESH)

                total = total + cond.astype(jnp.int32)
        pl.semaphore_wait(barrier, total)

    def plane_peers(self):
        return [
            (self.z < DEPTH - 1, self.r, self.grid(self.z + 1, self.x)),
            (self.z > 0, self.r, self.grid(self.z - 1, self.x)),
            (None, self.r, self.grid(self.z, 1 - self.x)),
        ]

    def share_peers(self):
        return [(None, self.r, self.t * self.share + u) for _, u in self.partners()]

    def rep_peers(self):
        return [(None, lax.rem(self.r + k, self.reps), self.f) for k in range(1, self.reps)]

    def all_plane_peers(self):
        return [(None, self.r, self.place(lax.rem(self.t + k, TP))) for k in range(1, TP)]

    def copy(self, src, dst, ssem, rsem, f, r=None):
        return pltpu.make_async_remote_copy(
            src_ref=src,
            dst_ref=dst,
            send_sem=self.sems.at[ssem],
            recv_sem=self.sems.at[rsem],
            device_id=(self.r if r is None else r, f),
            device_id_type=MESH,
        )

    def send(self, src, dst, ssem, rsem, f, r=None, cond=None):
        copy = self.copy(src, dst, ssem, rsem, f, r)
        if cond is None:
            copy.start()
        else:
            pl.when(cond)(copy.start)
        self.sent.append((cond, copy))

    def arrive(self, dst, rsem, cond=None):
        copy = pltpu.make_async_remote_copy(
            src_ref=dst,
            dst_ref=dst,
            send_sem=self.sems.at[rsem],
            recv_sem=self.sems.at[rsem],
            device_id=(self.r, self.f),
            device_id_type=MESH,
        )
        if cond is None:
            copy.wait_recv()
        else:
            pl.when(cond)(copy.wait_recv)

    def drain(self):
        for cond, copy in self.sent:
            if cond is None:
                copy.wait_send()
            else:
                pl.when(cond)(copy.wait_send)
        self.sent = []


def nearest(z, k):
    swapped = (1, 0, 2, 3)[k] if isinstance(k, int) else None
    far = lax.div(z, 2)
    edge = z + far * (3 - 2 * z)
    if swapped is None:
        inner = jnp.where(k == 0, 1, jnp.where(k == 1, 0, k))
        place = jnp.where(edge == 0, k, inner)
    else:
        place = k + edge * (swapped - k)
    return far * 3 + (1 - 2 * far) * place


class Wave:
    def __init__(self, net, block):
        self.net, self.block = net, block
        self.recv = net.take(TP)
        self.up, self.down, self.side = net.take(DEPTH), net.take(DEPTH), net.take(DEPTH)

    def copies(self, k):
        net = self.net
        z, x = net.z, net.x
        zo = nearest(z, k)
        t = zo * 2 + x
        block, sem = self.block(t), self.recv + t
        return [
            (
                (zo <= z) & (z < DEPTH - 1),
                net.copy(block, block, self.up + k, sem, net.grid(jnp.minimum(z + 1, DEPTH - 1), x)),
            ),
            (
                (zo >= z) & (z > 0),
                net.copy(block, block, self.down + k, sem, net.grid(jnp.maximum(z - 1, 0), x)),
            ),
            (None, net.copy(block, block, self.side + k, sem, net.grid(z, 1 - x))),
        ]

    def hand_on(self, k, own=False):
        net = self.net
        t = nearest(net.z, k) * 2 + net.x
        if not own:
            net.arrive(self.block(t), self.recv + t, None if isinstance(k, int) else k > 0)
        for cond, copy in self.copies(k):
            if cond is None:
                copy.start()
            else:
                pl.when(cond)(copy.start)

    def across(self, k):
        t = nearest(self.net.z, k) * 2 + 1 - self.net.x
        self.net.arrive(self.block(t), self.recv + t)

    def drain(self):
        @pl.loop(0, DEPTH)
        def _(k):
            for cond, copy in self.copies(k):
                if cond is None:
                    copy.wait_send()
                else:
                    pl.when(cond)(copy.wait_send)


class Gather:
    def __init__(self, net, part, side, up, down, total):
        self.net, self.part, self.side, self.up, self.down, self.total = net, part, side, up, down, total
        self.sems = [net.take(DEPTH) for _ in range(6)]

    def across(self, k):
        net = self.net
        zo = nearest(net.z, k)
        return net.copy(
            self.part(zo * 2 + 1 - net.x), self.side(zo), self.sems[0] + zo, self.sems[1] + zo,
            net.grid(net.z, 1 - net.x),
        )

    def along(self, k):
        net = self.net
        z = net.z
        zo = nearest(z, k)
        part = self.part(zo * 2 + net.x)
        return [
            (
                zo > z,
                net.copy(
                    part, self.up(zo), self.sems[2] + zo, self.sems[3] + zo,
                    net.grid(jnp.minimum(z + 1, DEPTH - 1), net.x),
                ),
            ),
            (
                zo < z,
                net.copy(
                    part, self.down(zo), self.sems[4] + zo, self.sems[5] + zo,
                    net.grid(jnp.maximum(z - 1, 0), net.x),
                ),
            ),
        ]

    def begin(self, k):
        self.across(k).start()

    def step(self, k):
        net = self.net
        z = net.z
        zo = nearest(z, k)
        part = self.part(zo * 2 + net.x)
        net.arrive(self.side(zo), self.sems[1] + zo)
        self.total[...] = part[...].astype(F32) + self.side(zo)[...].astype(F32)
        for cond, ref, sem in (
            ((zo >= z) & (z > 0), self.up(zo), self.sems[3]),
            ((zo <= z) & (z < DEPTH - 1), self.down(zo), self.sems[5]),
        ):

            @pl.when(cond)
            def _():
                net.arrive(ref, sem + zo)
                self.total[...] += ref[...].astype(F32)

        @pl.when(zo != z)
        def _():
            part[...] = self.total[...].astype(BF16)

        for cond, copy in self.along(k):
            pl.when(cond)(copy.start)

    def drain(self):
        @pl.loop(0, DEPTH)
        def _(k):
            self.across(k).wait_send()
            for cond, copy in self.along(k):
                pl.when(cond)(copy.wait_send)


def call(body, name, number, operands, in_specs, outs, scratch, sems, limit=60 << 20):
    return pl.pallas_call(
        body,
        name=name,
        out_shape=tuple(shape for shape, _ in outs),
        in_specs=in_specs,
        out_specs=tuple(spec for _, spec in outs),
        scratch_shapes=list(scratch) + [pltpu.SemaphoreType.DMA((sems,))],
        compiler_params=pltpu.CompilerParams(
            collective_id=number, has_side_effects=True, vmem_limit_bytes=limit
        ),
    )(*operands)


def chunk(rows, count, c):
    return pl.ds(c * (rows // count), rows // count)


def matmul_nt(a, b):
    return lax.dot_general(a, b, (((1,), (1,)), ((), ())), preferred_element_type=F32)


def matmul_tn(a, b):
    return lax.dot_general(a, b, (((0,), (0,)), ((), ())), preferred_element_type=F32)


def matmul(a, b):
    return jnp.dot(a, b, preferred_element_type=F32)


def tile(j, size):
    return pl.ds(pl.multiple_of(j * size, size), size)


PIECES = 2


def feed_forward(reps, share, x, branch, gain, valid, cot, w_in, w_down):
    seq, model = x.shape
    hs = w_in.shape[2]
    hidden_all = share * hs
    rows_all = TP * seq
    pair = 2 * seq
    half = seq // PIECES

    def body(
        x_ref, branch_ref, gain_ref, valid_ref, cot_ref, in_ref, down_ref,
        act_ref, grad_ref, sums_ref, in_out, down_out,
        middle, rows, cot_all, w_all, wd, hid, grads, part, side, up, down, rows_sum, ffn_sum,
        in_part, down_part, in_got, down_got, local, sems,
    ):
        net = Net(reps, share, sems)
        own = [
            pltpu.make_async_copy(in_ref.at[0], w_all.at[:, pl.ds(0, hs)], local.at[0]),
            pltpu.make_async_copy(in_ref.at[1], w_all.at[:, pl.ds(hs, hs)], local.at[1]),
            pltpu.make_async_copy(down_ref, wd.at[pl.ds(0, hs)], local.at[2]),
            pltpu.make_async_copy(cot_ref, cot_all, local.at[3]),
        ]
        for copy in own:
            copy.start()

        def block(ref, t):
            return ref.at[tile(t, seq)]

        middle[...] = x_ref[...].astype(F32) + branch_ref[...]
        scale = lax.rsqrt(jnp.mean(middle[...] * middle[...], axis=-1, keepdims=True) + EPSILON)
        block(rows, net.t)[...] = (middle[...] * scale * gain_ref[1:2]).astype(BF16)
        net.greet(net.plane_peers() + net.share_peers() + net.rep_peers())

        waves = [
            Wave(net, lambda t, c=c: rows.at[pl.ds(pl.multiple_of(t * seq + c * half, half), half)])
            for c in range(PIECES)
        ]
        weights = net.take(3 * share), net.take(3 * share)
        for wave in waves:
            wave.hand_on(0, own=True)
        arriving = []
        for k, u in net.partners():
            f, p = net.t * share + u, share - k
            for j, (src, dst) in enumerate(
                [
                    (in_ref.at[0], w_all.at[:, pl.ds(2 * hs * p, hs)]),
                    (in_ref.at[1], w_all.at[:, pl.ds(2 * hs * p + hs, hs)]),
                    (down_ref, wd.at[pl.ds(hs * p, hs)]),
                ]
            ):
                net.send(src, dst, weights[0] + 3 * k + j, weights[1] + 3 * p + j, f)
                arriving.append((dst, weights[1] + 3 * p + j))

        def unit(k):
            at = tile(nearest(net.z, k), pair)
            projected = matmul(rows[at], w_all[...])
            hidden_grad = matmul_nt(cot_all[at], wd[...])
            for p in range(share):
                gate = projected[:, 2 * hs * p : 2 * hs * p + hs]
                lift = projected[:, 2 * hs * p + hs : 2 * hs * (p + 1)]
                back = hidden_grad[:, hs * p : hs * (p + 1)]
                sig = jax.nn.sigmoid(gate)
                silu = gate * sig
                hid[at, hs * p : hs * (p + 1)] = (silu * lift).astype(BF16)
                grads[at, 2 * hs * p : 2 * hs * p + hs] = (
                    back * lift * sig * (1.0 + gate * (1.0 - sig))
                ).astype(BF16)
                grads[at, 2 * hs * p + hs : 2 * hs * (p + 1)] = (back * silu).astype(BF16)

            @pl.loop(0, 3)
            def _(j):
                to = tile(j, model // 3)
                part[0, at, to] = matmul_nt(grads[at], w_all[to]).astype(BF16)
                part[1, at, to] = matmul(hid[at], wd[:, to]).astype(BF16)

        @pl.loop(1, DEPTH + 1)
        def _(k):
            @pl.when(k < DEPTH)
            def _():
                for wave in waves:
                    wave.hand_on(k)

            @pl.when(k == 1)
            def _():
                for copy in own:
                    copy.wait()
                for dst, sem in arriving:
                    net.arrive(dst, sem)

            for wave in waves:
                wave.across(k - 1)
            unit(k - 1)

        def piece(ref, i, c, count):
            return lambda j: ref.at[i, pl.ds(pl.multiple_of(j * seq + c * half, half), half)]

        gathers = [
            [
                Gather(
                    net, piece(part, i, c, TP), piece(side, i, c, DEPTH), piece(up, i, c, DEPTH),
                    piece(down, i, c, DEPTH), total.at[pl.ds(c * half, half)],
                )
                for c in range(PIECES)
            ]
            for i, total in enumerate((rows_sum, ffn_sum))
        ]
        for both in gathers:

            @pl.loop(0, DEPTH)
            def _(j):
                for gather in both:
                    gather.begin(DEPTH - 1 - j)

        @pl.loop(0, model // 256)
        def _(j):
            at = tile(j, 256)
            in_part[at] = matmul_tn(rows[:, at], grads[...]).astype(BF16)

        @pl.loop(0, 3)
        def _(j):
            at = tile(j, model // 3)
            down_part[:, at] = matmul_tn(hid[...], cot_all[:, at]).astype(BF16)

        first, arrived = net.take(2 * share), net.take(2 * share)
        away, back = net.take(2 * reps), net.take(2 * reps)
        for k, u in net.partners():
            f, slot = net.t * share + u, share - 1 - k
            net.send(
                in_part.at[:, pl.ds(2 * hs * k, 2 * hs)], in_got.at[slot], first + 2 * k, arrived + 2 * slot, f
            )
            net.send(
                down_part.at[pl.ds(hs * k, hs)], down_got.at[slot], first + 2 * k + 1, arrived + 2 * slot + 1, f
            )

        def own_grads():
            for slot in range(share - 1):
                net.arrive(in_got.at[slot], arrived + 2 * slot)
                net.arrive(down_got.at[slot], arrived + 2 * slot + 1)

            @pl.loop(0, model // 256)
            def _(j):
                at = tile(j, 256)
                total = in_part[at, : 2 * hs].astype(F32)
                for slot in range(share - 1):
                    total = total + in_got[slot, at].astype(F32)
                in_out[net.r, at] = total.astype(BF16)

            total = down_part[:hs].astype(F32)
            for slot in range(share - 1):
                total = total + down_got[slot].astype(F32)
            down_out[net.r] = total.astype(BF16)
            for k in range(1, reps):
                r = lax.rem(net.r + k, reps)
                net.send(in_out.at[net.r], in_out.at[net.r], away + 2 * k, back + 2 * net.r, net.f, r=r)
                net.send(down_out.at[net.r], down_out.at[net.r], away + 2 * k + 1, back + 2 * net.r + 1, net.f, r=r)

        def steps(both, start, stop):
            @pl.loop(start, stop)
            def _(j):
                for gather in both:
                    gather.step(DEPTH - 1 - j)

        steps(gathers[0], 0, 2)
        own_grads()
        steps(gathers[0], 2, DEPTH)
        steps(gathers[1], 0, DEPTH)

        result = middle[...] + ffn_sum[...]
        act_ref[...] = result.astype(BF16)
        valid_col = valid_ref[...]
        scale = lax.rsqrt(jnp.mean(middle[...] * middle[...], axis=-1, keepdims=True) + EPSILON)
        lifted = rows_sum[...] * gain_ref[1:2]
        mean = jnp.mean(middle[...] * lifted, axis=-1, keepdims=True)
        grad_ref[...] = (
            block(cot_all, net.t)[...].astype(F32) + scale * lifted - middle[...] * (scale * scale * scale) * mean
        )
        sums_ref[...] = jnp.zeros_like(sums_ref)
        sums_ref[0:1] = jnp.sum(rows_sum[...] * middle[...] * scale, axis=0, keepdims=True)
        sums_ref[1:2] = jnp.sum(result * result * valid_col, axis=0, keepdims=True)
        sums_ref[2:3] = jnp.sum(branch_ref[...] * branch_ref[...] * valid_col, axis=0, keepdims=True)
        sums_ref[3:4] = jnp.sum(ffn_sum[...] * ffn_sum[...] * valid_col, axis=0, keepdims=True)
        for k in range(1, reps):
            r = lax.rem(net.r + k, reps)
            net.arrive(in_out.at[r], back + 2 * r)
            net.arrive(down_out.at[r], back + 2 * r + 1)
        net.drain()
        for wave in waves:
            wave.drain()
        for gather in gathers[0] + gathers[1]:
            gather.drain()

    shape = jax.ShapeDtypeStruct
    line = pltpu.VMEM((2, DEPTH * seq, model), BF16)
    return call(
        body, "feed_forward", 3, (x, branch, gain, valid, cot, w_in, w_down), [VMEM] * 4 + [ANY] * 3,
        [
            (shape((seq, model), BF16), VMEM),
            (shape((seq, model), F32), VMEM),
            (shape((8, model), F32), VMEM),
            (shape((reps, model, 2 * hs), BF16), VMEM),
            (shape((reps, hs, model), BF16), VMEM),
        ],
        [
            pltpu.VMEM((seq, model), F32),
            pltpu.VMEM((rows_all, model), BF16),
            pltpu.VMEM((rows_all, model), BF16),
            pltpu.VMEM((model, 2 * hidden_all), BF16),
            pltpu.VMEM((hidden_all, model), BF16),
            pltpu.VMEM((rows_all, hidden_all), BF16),
            pltpu.VMEM((rows_all, 2 * hidden_all), BF16),
            pltpu.VMEM((2, rows_all, model), BF16),
            line, line, line,
            pltpu.VMEM((seq, model), F32),
            pltpu.VMEM((seq, model), F32),
            pltpu.VMEM((model, 2 * hidden_all), BF16),
            pltpu.VMEM((hidden_all, model), BF16),
            pltpu.VMEM((share - 1, model, 2 * hs), BF16),
            pltpu.VMEM((share - 1, hs, model), BF16),
            pltpu.SemaphoreType.DMA((4,)),
        ],
        40 * PIECES + 24 * 2 * PIECES + 20 * share + 10 * reps,
    )


HEADS = H // TP
ROWS = 16


def lane_mask(shape, low, high):
    lane = lax.broadcasted_iota(jnp.int32, shape, 1)
    return (lane >= low) & (lane < high)


def head_pieces(t, block):
    base = block * H * HD + t * HEADS * HD
    return [(base, 2 * HD, block * 2 * HD), (base + 2 * HD, HD, 8 * HD + block * HD)]


def attention(reps, share, x, cot, w_in, small, w_out, bias_row, bias_col):
    n = TP * share
    seq, model = x.shape
    held = w_in.shape[0]
    width = 4 * HEADS * HD
    rows_all = TP * seq
    pair = 2 * seq
    half = seq // PIECES
    last = HEADS - 1

    def body(
        x_ref, cot_ref, in_ref, small_ref, out_ref, bias_row_ref, bias_col_ref,
        branch_ref, cot_out, rows_out, proj_out, sig_out, att_out, prob_out, logit_ref, wc_out, wo_out, wf_ref, gains_ref,
        xs, cots, rows, proj, sig, att, prob, wc, wo, split, smalls, lines, part, side, up, down, gated, local, sems,
    ):
        net = Net(reps, share, sems)

        def seq_block(ref, t):
            return ref.at[tile(t, seq)]

        def held_rows(f):
            return wc.at[tile(f, held)]

        own = [
            pltpu.make_async_copy(x_ref, seq_block(xs, net.t), local.at[0]),
            pltpu.make_async_copy(cot_ref, seq_block(cots, net.t), local.at[1]),
            pltpu.make_async_copy(small_ref, smalls.at[net.f], local.at[2]),
            pltpu.make_async_copy(out_ref, wo.at[tile(net.u, held)], local.at[3]),
        ]
        for copy in own:
            copy.start()
        for t in range(TP):
            for block in range(4):
                for column, wide, to in head_pieces(t, block):
                    split[t, :, to : to + wide] = in_ref[:, column : column + wide]
        wo[share * held :] = jnp.zeros((wo.shape[0] - share * held, model), BF16)
        others = [lax.rem(net.f + k, n) for k in range(n)]
        chips = [lax.rem(net.t + k, TP) for k in range(TP)]
        partners = list(net.partners())
        net.greet([(None, net.r, f) for f in others[1:]])

        small_send, small_recv = net.take(n), net.take(n)
        w_send, w_recv = net.take(TP), net.take(n)
        w_pass = net.take(share * TP)
        wo_send, wo_recv = net.take(share), net.take(share)
        for k in range(1, n):
            net.send(small_ref, smalls.at[net.f], small_send + k, small_recv + net.f, others[k])
        for k in range(1, TP):
            net.send(split.at[chips[k]], held_rows(net.f), w_send + k, w_recv + net.f, net.place(chips[k]))
        own_cols = pltpu.make_async_copy(split.at[net.t], held_rows(net.f), local.at[4])
        own_cols.start()
        for k, u in partners:
            f = net.t * share + u
            net.send(split.at[net.t], held_rows(net.f), w_pass + k, w_recv + net.f, f)
            net.send(out_ref, wo.at[tile(net.u, held)], wo_send + k, wo_recv + net.u, f)

        def pieces(ref):
            return [
                Wave(net, lambda t, c=c: ref.at[pl.ds(pl.multiple_of(t * seq + c * half, half), half)])
                for c in range(PIECES)
            ]

        waves, cot_waves = pieces(xs), pieces(cots)
        for copy in own:
            copy.wait()
        for wave in waves:
            wave.hand_on(0, own=True)
        for wave in cot_waves:
            wave.copies(0)[2][1].start()

        def weights():
            for k in range(1, TP):
                source = net.place(chips[k])
                net.arrive(held_rows(source), w_recv + source)
                for j, u in partners:
                    net.send(
                        held_rows(source), held_rows(source), w_pass + share * k + j, w_recv + source,
                        net.t * share + u,
                    )
            for k in range(1, n):
                net.arrive(smalls.at[others[k]], small_recv + others[k])
            for j in range(model // 128):
                line = jnp.zeros((32, 128), F32)
                for f in range(j * 128 // held, ((j + 1) * 128 - 1) // held + 1):
                    start = f * held - j * 128
                    piece = pltpu.roll(smalls[f].astype(F32), net.none + start % 128, 1)
                    line = jnp.where(lane_mask((32, 128), start, start + held), piece, line)
                lines[:, j * 128 : (j + 1) * 128] = line
            pick = lax.broadcasted_iota(jnp.int32, (ROWS, 32), 0) + HEADS * net.t
            pick = pick == lax.broadcasted_iota(jnp.int32, (ROWS, 32), 1)
            pick &= lax.broadcasted_iota(jnp.int32, (ROWS, 32), 0) < HEADS
            wf_ref[...] = matmul(pick.astype(BF16), lines[...].astype(BF16)).astype(BF16)
            gains_ref[...] = lines[H : H + 8]
            for k, u in partners:
                net.arrive(wo.at[tile(u, held)], wo_recv + u)
                for t in range(TP):
                    net.arrive(held_rows(t * share + u), w_recv + t * share + u)
            own_cols.wait()

        square = (seq, seq)
        at_row = lax.broadcasted_iota(jnp.int32, square, 0)
        at_col = lax.broadcasted_iota(jnp.int32, square, 1)

        def unit(k):
            place = nearest(net.z, k)
            at = tile(place, pair)
            values_in = xs[at].astype(F32)
            inverse = lax.rsqrt(jnp.mean(values_in * values_in, axis=-1, keepdims=True) + EPSILON)
            rows[at] = (values_in * inverse * gains_ref[0:1]).astype(BF16)
            projected = matmul(rows[at], wc[...])
            proj[at] = projected.astype(BF16)
            sig[at, : 2 * HD] = jax.nn.sigmoid(projected[:, 6 * HD : 8 * HD])
            tail = pltpu.roll(jax.nn.sigmoid(projected[:, 10 * HD : 12 * HD]), net.none + HD, 1)
            sig[at, 2 * HD :] = jnp.where(lane_mask(tail.shape, 0, HD), tail, 0.0)

            @pl.loop(0, 2)
            def _(j):
                t = place * 2 + j
                here = tile(t, seq)
                marks = smalls[net.place(t)].astype(F32)
                valid = marks[H + 2 : H + 3]
                start = marks[H + 3 : H + 4].astype(jnp.int32)
                causal = at_col <= at_row
                inside = (at_row >= start) & (at_row < start + PIC) & (at_col >= start) & (at_col < start + PIC)
                allowed = (causal | inside) & (valid > 0.0)
                sign = jnp.where(causal, 1.0, -1.0)
                below = sign * 0.5 + 0.5
                logit_col = matmul_nt(rows[here], wf_ref[...]) + bias_row_ref[...]
                logit_row = matmul_nt(wf_ref[...], rows[here]) + bias_col_ref[...]
                logit_ref[t] = logit_row
                decay_col = jnp.dot(
                    below, log_sigmoid(logit_col), precision=lax.Precision.HIGHEST, preferred_element_type=F32
                )
                decay_row = lax.dot_general(
                    log_sigmoid(logit_row), below, (((1,), (1,)), ((), ())),
                    precision=lax.Precision.HIGHEST, preferred_element_type=F32,
                )
                outs = []
                for h in range(HEADS):
                    if h < last:
                        query = jnp.where(lane_mask((seq, 2 * HD), h * HD, h * HD + HD), proj[here, : 2 * HD], 0)
                        key, value = proj[here, 2 * HD : 4 * HD], proj[here, 4 * HD : 6 * HD]
                    else:
                        query = jnp.where(lane_mask((seq, 2 * HD), 0, HD), proj[here, 8 * HD : 10 * HD], 0)
                        key = pltpu.roll(proj[here, 8 * HD : 10 * HD].astype(F32), net.none + HD, 1).astype(BF16)
                        value = proj[here, 10 * HD :]
                    scores = matmul_nt(query, key) * HD ** (-0.5)
                    scores = scores + sign * (decay_col[:, h : h + 1] - decay_row[h : h + 1])
                    masked = jnp.where(allowed, scores, NEGATIVE)
                    weights_now = jnp.exp(masked - jnp.max(masked, axis=-1, keepdims=True))
                    probability = weights_now / jnp.sum(weights_now, axis=-1, keepdims=True)
                    prob[t * HEADS + h] = probability
                    outs.append(matmul(probability.astype(BF16), value))
                low = lane_mask((seq, 2 * HD), 0, HD)
                att[here, : 2 * HD] = jnp.where(low, outs[0], outs[1])
                att[here, 2 * HD :] = jnp.where(low, outs[2], 0.0)

            gated[...] = (att[at] * sig[at]).astype(BF16)

            @pl.loop(0, 3)
            def _(j):
                to = tile(j, model // 3)
                part[at, to] = matmul(gated[...], wo[:, to]).astype(BF16)

        for wave in waves:
            wave.hand_on(1)
        weights()

        @pl.loop(1, DEPTH + 1)
        def _(k):
            @pl.when((k > 1) & (k < DEPTH))
            def _():
                for wave in waves:
                    wave.hand_on(k)

            @pl.when(k == DEPTH - 1)
            def _():
                for wave in cot_waves:
                    for cond, copy in wave.copies(0)[:2]:
                        pl.when(cond)(copy.start)

            for wave in waves:
                wave.across(k - 1)
            unit(k - 1)

        keep = [
            pltpu.make_async_copy(src, dst, local.at[5 + i])
            for i, (src, dst) in enumerate(
                [
                    (rows, rows_out), (proj, proj_out), (sig, sig_out), (att, att_out), (prob, prob_out),
                    (wc, wc_out), (wo, wo_out),
                ]
            )
        ]
        gathers = [
            Gather(
                net,
                *[
                    lambda j, ref=ref, c=c: ref.at[pl.ds(pl.multiple_of(j * seq + c * half, half), half)]
                    for ref in (part, side, up, down)
                ],
                branch_ref.at[pl.ds(c * half, half)],
            )
            for c in range(PIECES)
        ]

        @pl.loop(0, DEPTH)
        def _(j):
            for gather in gathers:
                gather.begin(DEPTH - 1 - j)

        for copy in keep:
            copy.start()

        @pl.loop(0, DEPTH)
        def _(j):
            for gather in gathers:
                gather.step(DEPTH - 1 - j)

            @pl.when(j < DEPTH - 1)
            def _():
                for wave in cot_waves:
                    wave.hand_on(j + 1)

        for k in range(DEPTH):
            for wave in cot_waves:
                wave.across(k)
        save = pltpu.make_async_copy(cots, cot_out, local.at[1])
        save.start()
        net.drain()
        for wave in waves + cot_waves:
            wave.drain()
        for gather in gathers:
            gather.drain()
        for copy in keep:
            copy.wait()
        save.wait()

    shape = jax.ShapeDtypeStruct
    line = pltpu.VMEM((DEPTH * seq, model), BF16)
    kept = [
        ((rows_all, model), BF16),
        ((rows_all, model), BF16),
        ((rows_all, width), BF16),
        ((rows_all, 4 * HD), F32),
        ((rows_all, 4 * HD), F32),
        ((TP * HEADS, seq, seq), F32),
    ]
    return call(
        body, "attention", 1, (x, cot, w_in, small, w_out, bias_row, bias_col),
        [ANY, ANY, VMEM, VMEM, ANY, VMEM, VMEM],
        [(shape((seq, model), F32), VMEM)]
        + [(shape(*what), ANY) for what in kept]
        + [
            (shape((TP, ROWS, seq), F32), VMEM),
            (shape((model, width), BF16), ANY),
            (shape((4 * HD, model), BF16), ANY),
            (shape((ROWS, model), BF16), VMEM),
            (shape((8, model), F32), VMEM),
        ],
        [pltpu.VMEM((rows_all, model), BF16)]
        + [pltpu.VMEM(*what) for what in kept]
        + [
            pltpu.VMEM((model, width), BF16),
            pltpu.VMEM((4 * HD, model), BF16),
            pltpu.VMEM((TP, held, width), BF16),
            pltpu.VMEM((n, 32, 128), BF16),
            pltpu.VMEM((32, model), F32),
            pltpu.VMEM((rows_all, model), BF16),
            line, line, line,
            pltpu.VMEM((pair, 4 * HD), BF16),
            pltpu.SemaphoreType.DMA((12,)),
        ],
        2 * 20 * PIECES + 24 * PIECES + 3 * n + TP + share * TP + 2 * share,
    )


def attention_back(
    reps, share, x, middle_grad, sums, valid, rows_a, proj, sig, att, prob, logit, wc, wo, wf, gains
):
    n = TP * share
    seq, model = x.shape
    width = 4 * HEADS * HD
    held = model // n
    rows_all = TP * seq
    pair = 2 * seq
    half = seq // PIECES
    last = HEADS - 1
    window = 256

    def body(
        x_ref, grad_ref, sums_ref, valid_ref, rows_in, proj_in, sig_in, att_in, prob_in, logit_ref, wc_in, wo_in, wf_ref,
        gains_ref, input_ref, in_ref, out_ref, small_ref,
        rows, proj, sig, att, prob, wcs, wos, bgs, pg, gated, part, side, up, down, rows_sum, ag, og, low_logit, bias_sum,
        forget_sum, lines, in_part, in_got, in_all, out_part, out_got, out_all, small_got, small_mid, local, sems,
    ):
        net = Net(reps, share, sems)
        others = [lax.rem(net.f + k, n) for k in range(n)]
        chips = [lax.rem(net.t + k, TP) for k in range(TP)]
        partners = list(net.partners())
        own = [
            pltpu.make_async_copy(src, dst, local.at[i])
            for i, (src, dst) in enumerate(
                [
                    (wo_in, wos), (sig_in, sig), (att_in, att), (proj_in, proj), (prob_in, prob), (rows_in, rows),
                    (wc_in, wcs),
                ]
            )
        ]
        for copy in own:
            copy.start()
        bgs[tile(net.t, seq)] = grad_ref[...].astype(BF16)
        net.greet([(None, net.r, f) for f in others[1:]] + net.rep_peers())
        waves = [
            Wave(net, lambda t, c=c: bgs.at[pl.ds(pl.multiple_of(t * seq + c * half, half), half)])
            for c in range(PIECES)
        ]
        for wave in waves:
            wave.hand_on(0, own=True)
        bias_sum[...] = jnp.zeros_like(bias_sum)
        forget_sum[...] = jnp.zeros_like(forget_sum)
        for copy in own:
            copy.wait()

        square = (seq, seq)
        causal = lax.broadcasted_iota(jnp.int32, square, 1) <= lax.broadcasted_iota(jnp.int32, square, 0)
        below = jnp.where(causal, 1.0, 0.0)
        low = lane_mask((seq, 2 * HD), 0, HD)
        head_row = lax.broadcasted_iota(jnp.int32, (ROWS, seq), 0)

        def unit(k):
            place = nearest(net.z, k)
            at = tile(place, pair)
            gated_grad = matmul_nt(bgs[at], wos[...])
            gate, attended = sig[at], att[at]
            ag[...] = (gated_grad * gate).astype(BF16)
            gated[at] = (attended * gate).astype(BF16)
            gate_grad = gated_grad * attended * (gate * (1.0 - gate))
            pg[at, 6 * HD : 8 * HD] = gate_grad[:, : 2 * HD].astype(BF16)
            og[...] = pltpu.roll(gate_grad[:, 2 * HD :], net.none + HD, 1)

            @pl.loop(0, 2)
            def _(j):
                t = place * 2 + j
                here = tile(t, seq)
                inner = tile(j, seq)
                swapped = pltpu.roll(proj[here, 8 * HD : 10 * HD].astype(F32), net.none + HD, 1).astype(BF16)
                decay_grad = jnp.zeros((ROWS, seq), F32)
                found = []
                for h in range(HEADS):
                    probability = prob[t * HEADS + h]
                    if h < last:
                        back_all = ag[inner, : 2 * HD]
                        back = jnp.where(lane_mask((seq, 2 * HD), h * HD, h * HD + HD), back_all, 0)
                        query, key, value = (proj[here, 2 * HD * i : 2 * HD * (i + 1)] for i in range(3))
                    else:
                        back = back_all = ag[inner, 2 * HD :]
                        query, key, value = swapped, swapped, proj[here, 10 * HD :]
                    prob_grad = matmul_nt(back, value)
                    score_grad = probability * (
                        prob_grad - jnp.sum(probability * prob_grad, axis=-1, keepdims=True)
                    )
                    dotted_grad = (score_grad * HD ** (-0.5)).astype(BF16)
                    found.append(
                        (
                            matmul(dotted_grad, key),
                            matmul_tn(dotted_grad, query),
                            matmul_tn(probability.astype(BF16), back_all),
                        )
                    )
                    signed = jnp.where(causal, score_grad, -score_grad)
                    line = jnp.sum(signed.T - signed, axis=0, keepdims=True)
                    decay_grad = jnp.where(head_row == h, line, decay_grad)
                for i in range(3):
                    pg[here, 2 * HD * i : 2 * HD * (i + 1)] = jnp.where(low, found[0][i], found[1][i]).astype(BF16)
                pg[here, 8 * HD : 10 * HD] = jnp.where(low, found[2][0], found[2][1]).astype(BF16)
                pg[here, 10 * HD :] = jnp.where(low, found[2][2], og[inner]).astype(BF16)
                later = jnp.dot(decay_grad, below, precision=lax.Precision.HIGHEST, preferred_element_type=F32)
                logit_grad = later * jax.nn.sigmoid(-logit_ref[t])
                bias_sum[...] += logit_grad
                low_logit[j] = logit_grad.astype(BF16)
                forget_sum[...] += matmul(logit_grad.astype(BF16), rows[here])

            @pl.loop(0, 3)
            def _(i):
                to = tile(i, model // 3)
                main = matmul_nt(pg[at], wcs[to])
                for j in range(2):
                    extra = matmul_tn(low_logit[j], wf_ref[:, to])
                    part[tile(place * 2 + j, seq), to] = (main[j * seq : (j + 1) * seq] + extra).astype(BF16)

        @pl.loop(1, DEPTH + 1)
        def _(k):
            @pl.when(k < DEPTH)
            def _():
                for wave in waves:
                    wave.hand_on(k)

            for wave in waves:
                wave.across(k - 1)
            unit(k - 1)

        gathers = [
            Gather(
                net,
                *[
                    lambda j, ref=ref, c=c: ref.at[pl.ds(pl.multiple_of(j * seq + c * half, half), half)]
                    for ref in (part, side, up, down)
                ],
                rows_sum.at[pl.ds(c * half, half)],
            )
            for c in range(PIECES)
        ]

        @pl.loop(0, DEPTH)
        def _(j):
            for gather in gathers:
                gather.begin(DEPTH - 1 - j)

        @pl.loop(0, model // 256)
        def _(j):
            at = tile(j, 256)
            in_part[at] = matmul_tn(rows[:, at], pg[...]).astype(BF16)

        @pl.loop(0, 3)
        def _(j):
            at = tile(j, model // 3)
            out_part[:, at] = matmul_tn(gated[...], bgs[:, at]).astype(BF16)

        def owned(t, u):
            return tile(t * share + u, held)

        in_send, in_recv = net.take(share * TP), net.take(share * TP)
        out_send, out_recv = net.take(share), net.take(share)
        over, landed = net.take(TP), net.take(TP)
        away, back_in = net.take(TP * reps), net.take(TP * reps)
        out_away, out_back = net.take(reps), net.take(reps)
        small_send, small_recv = net.take(n), net.take(n)
        mid_send, mid_recv = net.take(reps), net.take(reps)
        for k, u in partners:
            slot, f = share - 1 - k, net.t * share + u
            for j in range(TP):
                t = chips[(j + 1) % TP]
                net.send(
                    in_part.at[owned(t, u)], in_got.at[slot, t], in_send + share * j + k, in_recv + share * t + slot, f
                )
            net.send(out_part.at[tile(u, held)], out_got.at[slot], out_send + k, out_recv + slot, f)

        def steps(start, stop):
            @pl.loop(start, stop)
            def _(j):
                for gather in gathers:
                    gather.step(DEPTH - 1 - j)

        steps(0, 1)
        for j in range(TP):
            t = chips[(j + 1) % TP]
            total = in_part[owned(t, net.u)].astype(F32)
            for slot in range(share - 1):
                net.arrive(in_got.at[slot, t], in_recv + share * t + slot)
                total = total + in_got[slot, t].astype(F32)
            if j < TP - 1:
                in_part[owned(t, net.u)] = total.astype(BF16)
            else:
                in_all[net.r, t] = total.astype(BF16)
        total = out_part[tile(net.u, held)].astype(F32)
        for slot in range(share - 1):
            net.arrive(out_got.at[slot], out_recv + slot)
            total = total + out_got[slot].astype(F32)
        out_all[net.r] = total.astype(BF16)
        for j in range(TP - 1):
            t = chips[j + 1]
            net.send(in_part.at[owned(t, net.u)], in_all.at[net.r, net.t], over + j, landed + net.t, net.place(t))
        replicas = [lax.rem(net.r + k, reps) for k in range(reps)]
        for k in range(1, reps):
            net.send(
                out_all.at[net.r], out_all.at[net.r], out_away + k, out_back + net.r, net.f, r=replicas[k]
            )
            net.send(
                in_all.at[net.r, net.t], in_all.at[net.r, net.t], away + k, back_in + TP * net.r + net.t, net.f,
                r=replicas[k],
            )
        steps(1, DEPTH)

        layer_in = x_ref[...].astype(F32)
        scale = lax.rsqrt(jnp.mean(layer_in * layer_in, axis=-1, keepdims=True) + EPSILON)
        lifted = rows_sum[...] * gains_ref[0:1]
        mean = jnp.mean(layer_in * lifted, axis=-1, keepdims=True)
        input_ref[...] = grad_ref[...] + scale * lifted - layer_in * (scale * scale * scale) * mean
        lines[...] = jnp.zeros_like(lines)
        lines[0:1, :model] = jnp.sum(rows_sum[...] * layer_in * scale, axis=0, keepdims=True)
        lines[1:2, :model] = sums_ref[0:1]
        lines[2 : 2 + HEADS, :model] = forget_sum[:HEADS]
        for i in range(3):
            lines[5 + i : 6 + i] = jnp.broadcast_to(
                jnp.sum(sums_ref[1 + i : 2 + i], axis=1, keepdims=True), (1, model + window)
            )
        lines[8:9] = jnp.broadcast_to(jnp.sum(valid_ref[...], axis=0, keepdims=True), (1, model + window))
        lines[9 : 9 + HEADS] = jnp.broadcast_to(
            jnp.sum(bias_sum[:HEADS], axis=1, keepdims=True), (HEADS, model + window)
        )

        def seen(f):
            return pl.ds(pl.multiple_of(lax.div(f * held, 128) * 128, 128), window)

        small_got[net.f] = lines[:, seen(net.f)]
        for k in range(1, n):
            net.send(
                lines.at[:, seen(others[k])], small_got.at[net.f], small_send + k, small_recv + net.f, others[k]
            )
        for j in range(1, TP):
            t = chips[TP - j]
            net.arrive(in_all.at[net.r, t], landed + t)
            for k in range(1, reps):
                net.send(
                    in_all.at[net.r, t], in_all.at[net.r, t], away + reps * j + k, back_in + TP * net.r + t, net.f,
                    r=replicas[k],
                )
        for k in range(1, n):
            net.arrive(small_got.at[others[k]], small_recv + others[k])
        for t in range(TP):
            total = small_got[t * share]
            for u in range(1, share):
                total = total + small_got[t * share + u]
            small_mid[net.r, t] = total
        for k in range(1, reps):
            net.send(
                small_mid.at[net.r], small_mid.at[net.r], mid_send + k, mid_recv + net.r, net.f, r=replicas[k]
            )
        for k in range(1, reps):
            r = replicas[k]
            net.arrive(out_all.at[r], out_back + r)
            for t in range(TP):
                net.arrive(in_all.at[r, t], back_in + TP * r + t)
            net.arrive(small_mid.at[r], mid_recv + r)
        for t in range(TP):
            for block in range(4):
                for column, wide, to in head_pieces(t, block):
                    total = in_all[0, t, :, to : to + wide].astype(F32)
                    for r in range(1, reps):
                        total = total + in_all[r, t, :, to : to + wide].astype(F32)
                    in_ref[:, column : column + wide] = total
        total, small = out_all[0].astype(F32), small_mid[0]
        for r in range(1, reps):
            total = total + out_all[r].astype(F32)
            small = small + small_mid[r]
        out_ref[...] = total
        small_ref[...] = small
        net.drain()
        for wave in waves:
            wave.drain()
        for gather in gathers:
            gather.drain()

    shape = jax.ShapeDtypeStruct
    line = pltpu.VMEM((DEPTH * seq, model), BF16)
    return call(
        body, "attention_back", 5,
        (x, middle_grad, sums, valid, rows_a, proj, sig, att, prob, logit, wc, wo, wf, gains),
        [VMEM] * 4 + [ANY] * 5 + [VMEM, ANY, ANY, VMEM, VMEM],
        [
            (shape((seq, model), F32), VMEM),
            (shape((held, 4 * model), F32), VMEM),
            (shape((held, model), F32), VMEM),
            (shape((TP, ROWS, window), F32), VMEM),
        ],
        [
            pltpu.VMEM((rows_all, model), BF16),
            pltpu.VMEM((rows_all, width), BF16),
            pltpu.VMEM((rows_all, 4 * HD), F32),
            pltpu.VMEM((rows_all, 4 * HD), F32),
            pltpu.VMEM((TP * HEADS, seq, seq), F32),
            pltpu.VMEM((model, width), BF16),
            pltpu.VMEM((4 * HD, model), BF16),
            pltpu.VMEM((rows_all, model), BF16),
            pltpu.VMEM((rows_all, width), BF16),
            pltpu.VMEM((rows_all, 4 * HD), BF16),
            pltpu.VMEM((rows_all, model), BF16),
            line, line, line,
            pltpu.VMEM((seq, model), F32),
            pltpu.VMEM((pair, 4 * HD), BF16),
            pltpu.VMEM((pair, 2 * HD), F32),
            pltpu.VMEM((2, ROWS, seq), BF16),
            pltpu.VMEM((ROWS, seq), F32),
            pltpu.VMEM((ROWS, model), F32),
            pltpu.VMEM((ROWS, model + window), F32),
            pltpu.VMEM((model, width), BF16),
            pltpu.VMEM((share - 1, TP, held, width), BF16),
            pltpu.VMEM((reps, TP, held, width), BF16),
            pltpu.VMEM((4 * HD, model), BF16),
            pltpu.VMEM((share - 1, held, model), BF16),
            pltpu.VMEM((reps, held, model), BF16),
            pltpu.VMEM((n, ROWS, window), F32),
            pltpu.VMEM((reps, TP, ROWS, window), F32),
            pltpu.SemaphoreType.DMA((8,)),
        ],
        20 * PIECES + 24 * PIECES + 2 * share * (TP + 1) + 2 * TP + 2 * reps * (TP + 2) + 2 * n,
    )


def log_sigmoid(values_in):
    return jnp.minimum(values_in, 0.0) - jnp.log1p(jnp.exp(-jnp.abs(values_in)))


def per_device(
    reps,
    share,
    tokens,
    cotangent,
    pic_start,
    valid_mask,
    gain_attn,
    attn_in,
    forget_w,
    forget_bias,
    attn_out,
    gain_ffn,
    ffn_in,
    ffn_down,
):
    n = TP * share
    _, seq, model = tokens.shape
    held = attn_in.shape[0]
    heads = H // TP
    f = lax.axis_index("fsdp")
    t = f // share

    small = jnp.concatenate([forget_w.T, gain_attn[None], gain_ffn[None]])
    small = jnp.pad(small, ((0, 0), (0, 128 - held)))
    marks = jnp.concatenate(
        [valid_mask.astype(BF16), jnp.broadcast_to(pic_start.astype(BF16)[:, None], (1, seq))]
    )
    small = jnp.concatenate([small, marks, jnp.zeros((32 - H - 4, 128), BF16)])
    bias = lax.dynamic_slice_in_dim(forget_bias, heads * t, heads).astype(F32)
    bias = jnp.pad(bias, (0, ROWS - heads))
    branch_attn, cot, rows_a, proj, sig, att, probability, logit, w_cols, w_rows, w_forget, gains = attention(
        reps, share, tokens[0], cotangent[0], attn_in, small, attn_out, bias[None], bias[:, None]
    )
    valid_col = valid_mask[0].astype(F32)[:, None]
    activations, middle_grad, sums, ffn_in_sum, ffn_down_sum = feed_forward(
        reps, share, tokens[0], branch_attn, gains, valid_col, cot, ffn_in, ffn_down
    )
    input_grad, grad_in, grad_out, gathered = attention_back(
        reps, share, tokens[0], middle_grad, sums, valid_col, rows_a, proj, sig, att, probability, logit, w_cols, w_rows,
        w_forget, gains,
    )

    mine = lax.dynamic_slice_in_dim(gathered, f * held % 128, held, axis=2)
    together = jnp.sum(mine, axis=0)
    grad_forget = mine[:, 2 : 2 + heads].reshape(H, held).T
    bias_total = mine[:, 9 : 9 + heads, 0].reshape(H)
    stats = jnp.sqrt(together[5:8, 0] / (together[8, 0] * model) + EPSILON)

    def over_reps(values_in):
        return jnp.sum(values_in.astype(F32), axis=0)

    hs = ffn_in.shape[2]
    grad_ffn_in = over_reps(ffn_in_sum)
    grad_ffn_in = jnp.stack([grad_ffn_in[:, :hs], grad_ffn_in[:, hs:]])
    return (
        activations[None],
        input_grad[None],
        together[0],
        grad_in,
        grad_forget,
        bias_total,
        grad_out,
        together[1],
        grad_ffn_in,
        over_reps(ffn_down_sum),
        stats,
    )


def solution(mesh):
    placed = (
        P(("rep", "fsdp"), None, None),
        P(("rep", "fsdp"), None, None),
        P(("rep", "fsdp")),
        P(("rep", "fsdp"), None),
        P("fsdp"),
        P("fsdp", None),
        P("fsdp", None),
        P(),
        P("fsdp", None),
        P("fsdp"),
        P(None, None, "fsdp"),
        P("fsdp", None),
    )
    return jax.shard_map(
        functools.partial(per_device, mesh.shape["rep"], mesh.shape["fsdp"] // TP),
        mesh=mesh,
        in_specs=placed,
        out_specs=(
            P(("rep", "fsdp"), None, None),
            P(("rep", "fsdp"), None, None),
            P("fsdp"),
            P("fsdp", None),
            P("fsdp", None),
            P(),
            P("fsdp", None),
            P("fsdp"),
            P(None, None, "fsdp"),
            P("fsdp", None),
            P(),
        ),
        check_vma=False,
    )
```

time: 1290 us -> 419 us (0.32)
  waiting for transfers between devices: 953 us -> 0 us
  Pallas kernels: 0 us -> 392 us
  matrix products: 139 us -> 0 us
  blocking collectives: 133 us -> 0 us
  between operations: 17.9 us -> 2.07 us
    reduce_scatter x4 -> x0, waiting for transfers between devices: 589 us -> none  [the longest x1 247 us: per_device(): lax.psum_scatter(in_full.astype(jnp.bfloat16), 'fsdp', scatter_dimension=...]
    pallas_call x0 -> x3, Pallas kernels: none -> 392 us  [call(): pl.pallas_call(body, name=name, out_shape=tuple((shape for shape, _ in ou...]
    all_gather x4 -> x0, waiting for transfers between devices: 301 us -> none  [the longest x1 132 us: per_device(): lax.all_gather(ffn_in, 'fsdp', axis=2, tiled=True)]
    dot_general x21 -> x0, matrix products: 136 us -> none  [the longest x1 14.4 us: per_device(): jnp.einsum('ksf,kdf->sd', gate_up_grad, weight_ffn, preferred_element_typ...]
    unnamed x2 -> x0, blocking collectives: 69.7 us -> none
    psum x1 -> x0, waiting for transfers between devices: 60.7 us -> none  [per_device(): lax.psum(grad_ffn_in.astype(jnp.bfloat16), 'rep').astype(jnp.float32)]
    psum x2 -> x0, blocking collectives: 44.5 us -> none  [the longest x1 39.2 us: per_device(): lax.psum((square_sums, bias_grad), ('rep', 'fsdp'))]
    all_gather x1 -> x0, blocking collectives: 18.3 us -> none  [per_device(): lax.all_gather(forget_w, 'fsdp', axis=0, tiled=True)]
  transfers between devices with their start and end apart: 10 -> 0, of which waited for: 9 -> 0; matrix products, arithmetic and copies ran while one was open for 10% -> 0% of each run, Pallas kernels for 0% -> 0%
where the time goes in v2:
time: 419 us; the launch traced here: 413 us
  Pallas kernels  392 us (94%)
  local copies, waits for them, and re-layouts  10.6 us (3%)
  other arithmetic  8.15 us (2%)
    pallas_call x3, Pallas kernels, call(): pl.pallas_call(body, name=name, out_shape=tuple((shape for shape, _ in ou...  392 us

profile of v2, /device:TPU:0, one launch (start us, length us, event | category | flops | bytes accessed | tf_op | source)
XLA Modules:
  0.0 412.8 jit_solution(13707617121508522427)
XLA Ops:
  0.7 0.7 dynamic_slice.6
  1.4 0.5 convert_bitcast_fusion.1
  1.9 0.7 copy.32.bias_col_ref
  2.6 0.7 convert_bitcast_fusion
  3.3 0.7 fusion.4
  4.7 0.1 pad.18.clone
  4.8 0.1 pad.19.clone
  4.9 0.7 maximum_maximum_fusion.small_ref
  5.6 143.5 %attention.1 = (f32[128,1536]{1,0:T(8,128)}, bf16[1024,1536]{1,0:T(8,128)(2,1)}, bf16[1024,1536]{1,0:T(8,128)(2,1)}, bf16[1024,768]{1,0:T(8,128)(2,1)}, f32[1024...) custom-call(bf16[128,1536]{1,0:T(8,128)(2,1)} %bitcast.24, ...), custom_call_target="tpu_custom_call" | custom-call | tf_op jit(solution)/shard_map/attention/pallas_call | solution.py:257
  149.1 0.7 copy.33.valid_ref
  149.8 116.9 %feed_forward.1 = (bf16[128,1536]{1,0:T(8,128)(2,1)}, f32[128,1536]{1,0:T(8,128)}, f32[8,1536]{1,0:T(8,128)}, bf16[2,1536,512]{2,1,0:T(8,128)(2,1)}, bf16[2,256,1536]{2,1,0:T(8,128)(2,1)}) custom-call(bf16[128,1536]{1,0:T(8,128)(2,1)} %bitcast.25, f32[128,1536]{1,0:T(8,128)} %get-tuple-element.32.branch_ref, f32[8,1536]{1,0:T(8,128)} %get-tuple-element.33.gain_ref.gains_ref, ...), custom_call_target="tpu_custom_call" | custom-call | tf_op jit(solution)/shard_map/feed_forward/pallas_call | solution.py:257
  266.7 0.0 copy-start
  266.7 131.5 %attention_back.1 = (f32[128,1536]{1,0:T(8,128)}, f32[96,6144]{1,0:T(8,128)}, f32[96,1536]{1,0:T(8,128)}, f32[8,16,256]{2,1,0:T(8,128)}) custom-call(bf16[128,1536]{1,0:T(8,128)(2,1)} %bitcast.26, f32[128,1536]{1,0:T(8,128)} %get-tuple-element.36.grad_ref, f32[8,1536]{1,0:T(8,128)} %get-tuple-element.37.sums_ref, f32[128,1]{1,0:T(8,128)} %copy.33.valid_ref, ...), custom_call_target="tpu_custom_call" | custom-call | tf_op jit(solution)/shard_map/attention_back/pallas_call | solution.py:257
  398.2 1.0 dynamic-slice_reduce_fusion
  399.2 0.5 slice.37
  400.4 0.6 fusion.7
  401.1 0.0 copy-done
  401.1 0.6 convert_reduce_fusion
  401.7 0.2 slice_bitcast_fusion.1
  401.9 0.0 copy-start.2
  401.9 1.9 pad_maximum_fusion
  403.8 0.0 copy-start.5
  403.8 0.0 copy-start.3
  403.8 1.0 constant_dynamic-slice_fusion
  404.8 0.6 reshape.46
  405.4 0.5 slice_bitcast_fusion.2
  405.9 0.9 dynamic-slice_reduce_fusion.1
  406.9 0.6 reshape_squeeze.3
  407.5 0.0 copy-done.2
  407.5 0.0 copy-start.1
  407.5 1.4 convert_reduce_fusion.1
  408.8 0.0 copy-done.5
  408.8 0.7 copy.40
  409.6 0.0 copy-done.3
  409.6 0.9 copy.41
  410.5 0.0 copy-done.1
  410.5 0.0 copy-start.4
  410.5 1.4 copy.42
  411.9 0.1 copy-done.4
  411.9 0.8 copy.43
  (1 shorter events, 0.0 us)
Async XLA Ops:
  266.7 134.3 %copy-start = (bf16[2,1536,512]{2,1,0:T(8,128)(2,1)S(1)}, bf16[2,1536,512]{2,1,0:T(8,128)(2,1)}, u32[]{:S(2)}) copy-start(bf16[2,1536,512]{2,1,0:T(8,128)(2,1)} %get-tuple-element.51) | copy-start | bytes 9437188
  401.9 5.5 %copy-start.2 = (bf16[2,256,1536]{2,1,0:T(8,128)(2,1)S(1)}, bf16[2,256,1536]{2,1,0:T(8,128)(2,1)}, u32[]{:S(2)}) copy-start(bf16[2,256,1536]{2,1,0:T(8,128)(2,1)} %get-tuple-element.52) | copy-start | bytes 4718596
  403.8 5.1 %copy-start.5 = (bf16[128,1536]{1,0:T(8,128)(2,1)S(1)}, bf16[128,1536]{1,0:T(8,128)(2,1)}, u32[]{:S(2)}) copy-start(bf16[128,1536]{1,0:T(8,128)(2,1)} %get-tuple-element.35) | copy-start | bytes 1179652
  403.8 5.8 %copy-start.3 = (f32[128,1536]{1,0:T(8,128)S(1)}, f32[128,1536]{1,0:T(8,128)}, u32[]{:S(2)}) copy-start(f32[128,1536]{1,0:T(8,128)} %get-tuple-element.47) | copy-start | bytes 2359300
  407.5 3.0 copy-start.1
  410.5 1.5 copy-start.4

commit v3 on v2

--- a/solution.py
+++ b/solution.py
@@ -364,24 +364,6 @@
                 part[0, at, to] = matmul_nt(grads[at], w_all[to]).astype(BF16)
                 part[1, at, to] = matmul(hid[at], wd[:, to]).astype(BF16)
 
-        @pl.loop(1, DEPTH + 1)
-        def _(k):
-            @pl.when(k < DEPTH)
-            def _():
-                for wave in waves:
-                    wave.hand_on(k)
-
-            @pl.when(k == 1)
-            def _():
-                for copy in own:
-                    copy.wait()
-                for dst, sem in arriving:
-                    net.arrive(dst, sem)
-
-            for wave in waves:
-                wave.across(k - 1)
-            unit(k - 1)
-
         def piece(ref, i, c, count):
             return lambda j: ref.at[i, pl.ds(pl.multiple_of(j * seq + c * half, half), half)]
 
@@ -395,12 +377,36 @@
             ]
             for i, total in enumerate((rows_sum, ffn_sum))
         ]
-        for both in gathers:
-
-            @pl.loop(0, DEPTH)
-            def _(j):
-                for gather in both:
-                    gather.begin(DEPTH - 1 - j)
+        @pl.loop(1, DEPTH + 1)
+        def _(k):
+            @pl.when(k < DEPTH)
+            def _():
+                for wave in waves:
+                    wave.hand_on(k)
+
+            @pl.when(k == 1)
+            def _():
+                for copy in own:
+                    copy.wait()
+                for dst, sem in arriving:
+                    net.arrive(dst, sem)
+
+            for wave in waves:
+                wave.across(k - 1)
+
+            @pl.when(k == DEPTH)
+            def _():
+                for gather in gathers[0]:
+                    gather.begin(DEPTH - 2)
+
+            unit(k - 1)
+
+        for k in (DEPTH - 1, *range(DEPTH - 3, -1, -1)):
+            for gather in gathers[0]:
+                gather.begin(k)
+        for k in range(DEPTH - 1, -1, -1):
+            for gather in gathers[1]:
+                gather.begin(k)
 
         @pl.loop(0, model // 256)
         def _(j):
@@ -517,6 +523,10 @@
 ROWS = 16
 
 
+def cuts(reps, held):
+    return reps if held % (16 * reps) == 0 else 1
+
+
 def lane_mask(shape, low, high):
     lane = lax.broadcasted_iota(jnp.int32, shape, 1)
     return (lane >= low) & (lane < high)
@@ -536,6 +546,7 @@
     pair = 2 * seq
     half = seq // PIECES
     last = HEADS - 1
+    cut = cuts(reps, held)
 
     def body(
         x_ref, cot_ref, in_ref, small_ref, out_ref, bias_row_ref, bias_col_ref,
@@ -549,6 +560,15 @@
 
         def held_rows(f):
             return wc.at[tile(f, held)]
+
+        def spot(r):
+            return r if cut > 1 else 0
+
+        def piece_of(r):
+            return tile(spot(r), held // cut)
+
+        def held_piece(f, r):
+            return wc.at[pl.ds(pl.multiple_of(f * held + spot(r) * (held // cut), held // cut), held // cut)]
 
         own = [
             pltpu.make_async_copy(x_ref, seq_block(xs, net.t), local.at[0]),
@@ -566,21 +586,26 @@
         others = [lax.rem(net.f + k, n) for k in range(n)]
         chips = [lax.rem(net.t + k, TP) for k in range(TP)]
         partners = list(net.partners())
-        net.greet([(None, net.r, f) for f in others[1:]])
+        replicas = [lax.rem(net.r + k, reps) for k in range(reps)]
+        net.greet([(None, net.r, f) for f in others[1:]] + [(None, r, net.f) for r in replicas[1:cut]])
 
         small_send, small_recv = net.take(n), net.take(n)
-        w_send, w_recv = net.take(TP), net.take(n)
-        w_pass = net.take(share * TP)
+        w_send, w_recv = net.take(TP), net.take(n * cut)
+        w_pass = net.take(share * TP * (cut + 1))
+        w_away = net.take(TP * cut)
         wo_send, wo_recv = net.take(share), net.take(share)
         for k in range(1, n):
             net.send(small_ref, smalls.at[net.f], small_send + k, small_recv + net.f, others[k])
         for k in range(1, TP):
-            net.send(split.at[chips[k]], held_rows(net.f), w_send + k, w_recv + net.f, net.place(chips[k]))
+            net.send(
+                split.at[chips[k], piece_of(net.r)], held_piece(net.f, net.r), w_send + k, w_recv + cut * net.f + spot(net.r),
+                net.place(chips[k]),
+            )
         own_cols = pltpu.make_async_copy(split.at[net.t], held_rows(net.f), local.at[4])
         own_cols.start()
         for k, u in partners:
             f = net.t * share + u
-            net.send(split.at[net.t], held_rows(net.f), w_pass + k, w_recv + net.f, f)
+            net.send(split.at[net.t], held_rows(net.f), w_pass + k, w_recv + cut * net.f, f)
             net.send(out_ref, wo.at[tile(net.u, held)], wo_send + k, wo_recv + net.u, f)
 
         def pieces(ref):
@@ -598,14 +623,16 @@
             wave.copies(0)[2][1].start()
 
         def weights():
-            for k in range(1, TP):
-                source = net.place(chips[k])
-                net.arrive(held_rows(source), w_recv + source)
-                for j, u in partners:
-                    net.send(
-                        held_rows(source), held_rows(source), w_pass + share * k + j, w_recv + source,
-                        net.t * share + u,
-                    )
+            for q in range(cut):
+                r = replicas[q]
+                for k in range(1, TP):
+                    source = net.place(chips[k])
+                    got, sem = held_piece(source, r), w_recv + cut * source + spot(r)
+                    net.arrive(got, sem)
+                    for j, u in partners:
+                        net.send(got, got, w_pass + share * (TP * (q + 1) + k) + j, sem, net.t * share + u)
+                    for p in range(1, cut if q == 0 else 1):
+                        net.send(got, got, w_away + TP * p + k, sem, net.f, r=replicas[p])
             for k in range(1, n):
                 net.arrive(smalls.at[others[k]], small_recv + others[k])
             for j in range(model // 128):
@@ -622,8 +649,11 @@
             gains_ref[...] = lines[H : H + 8]
             for k, u in partners:
                 net.arrive(wo.at[tile(u, held)], wo_recv + u)
-                for t in range(TP):
-                    net.arrive(held_rows(t * share + u), w_recv + t * share + u)
+                net.arrive(held_rows(net.t * share + u), w_recv + cut * (net.t * share + u))
+                for k in range(1, TP):
+                    f = chips[k] * share + u
+                    for r in replicas[:cut]:
+                        net.arrive(held_piece(f, r), w_recv + cut * f + spot(r))
             own_cols.wait()
 
         square = (seq, seq)
@@ -642,7 +672,7 @@
             tail = pltpu.roll(jax.nn.sigmoid(projected[:, 10 * HD : 12 * HD]), net.none + HD, 1)
             sig[at, 2 * HD :] = jnp.where(lane_mask(tail.shape, 0, HD), tail, 0.0)
 
-            @pl.loop(0, 2)
+            @pl.loop(0, 2, unroll=True)
             def _(j):
                 t = place * 2 + j
                 here = tile(t, seq)
@@ -691,36 +721,6 @@
                 to = tile(j, model // 3)
                 part[at, to] = matmul(gated[...], wo[:, to]).astype(BF16)
 
-        for wave in waves:
-            wave.hand_on(1)
-        weights()
-
-        @pl.loop(1, DEPTH + 1)
-        def _(k):
-            @pl.when((k > 1) & (k < DEPTH))
-            def _():
-                for wave in waves:
-                    wave.hand_on(k)
-
-            @pl.when(k == DEPTH - 1)
-            def _():
-                for wave in cot_waves:
-                    for cond, copy in wave.copies(0)[:2]:
-                        pl.when(cond)(copy.start)
-
-            for wave in waves:
-                wave.across(k - 1)
-            unit(k - 1)
-
-        keep = [
-            pltpu.make_async_copy(src, dst, local.at[5 + i])
-            for i, (src, dst) in enumerate(
-                [
-                    (rows, rows_out), (proj, proj_out), (sig, sig_out), (att, att_out), (prob, prob_out),
-                    (wc, wc_out), (wo, wo_out),
-                ]
-            )
-        ]
         gathers = [
             Gather(
                 net,
@@ -733,10 +733,45 @@
             for c in range(PIECES)
         ]
 
-        @pl.loop(0, DEPTH)
-        def _(j):
+        for wave in waves:
+            wave.hand_on(1)
+        weights()
+
+        @pl.loop(1, DEPTH + 1)
+        def _(k):
+            @pl.when((k > 1) & (k < DEPTH))
+            def _():
+                for wave in waves:
+                    wave.hand_on(k)
+
+            @pl.when(k == DEPTH - 1)
+            def _():
+                for wave in cot_waves:
+                    for cond, copy in wave.copies(0)[:2]:
+                        pl.when(cond)(copy.start)
+
+            for wave in waves:
+                wave.across(k - 1)
+
+            @pl.when(k == DEPTH)
+            def _():
+                for gather in gathers:
+                    gather.begin(DEPTH - 2)
+
+            unit(k - 1)
+
+        keep = [
+            pltpu.make_async_copy(src, dst, local.at[5 + i])
+            for i, (src, dst) in enumerate(
+                [
+                    (rows, rows_out), (proj, proj_out), (sig, sig_out), (att, att_out), (prob, prob_out),
+                    (wc, wc_out), (wo, wo_out),
+                ]
+            )
+        ]
+        for k in (DEPTH - 1, *range(DEPTH - 3, -1, -1)):
             for gather in gathers:
-                gather.begin(DEPTH - 1 - j)
+                gather.begin(k)
 
         for copy in keep:
             copy.start()
@@ -800,7 +835,7 @@
             pltpu.VMEM((pair, 4 * HD), BF16),
             pltpu.SemaphoreType.DMA((12,)),
         ],
-        2 * 20 * PIECES + 24 * PIECES + 3 * n + TP + share * TP + 2 * share,
+        2 * 20 * PIECES + 24 * PIECES + (2 + cut) * n + (1 + cut) * (TP + share * TP) + 2 * share,
     )
 
 
@@ -816,12 +851,16 @@
     half = seq // PIECES
     last = HEADS - 1
     window = 256
+    cut = cuts(reps, held)
+    bit = held // cut
+    sheets = 1 if cut > 1 else reps
 
     def body(
         x_ref, grad_ref, sums_ref, valid_ref, rows_in, proj_in, sig_in, att_in, prob_in, logit_ref, wc_in, wo_in, wf_ref,
-        gains_ref, input_ref, in_ref, out_ref, small_ref,
+        gains_ref, input_ref, in_ref, out_ref, gains_out, forget_ref, bias_ref, stats_ref,
         rows, proj, sig, att, prob, wcs, wos, bgs, pg, gated, part, side, up, down, rows_sum, ag, og, low_logit, bias_sum,
-        forget_sum, lines, in_part, in_got, in_all, out_part, out_got, out_all, small_got, small_mid, local, sems,
+        forget_sum, lines, late, in_part, in_got, swapped_in, in_all, out_part, out_got, out_all, small_got, first_got,
+        small_mid, local, sems,
     ):
         net = Net(reps, share, sems)
         others = [lax.rem(net.f + k, n) for k in range(n)]
@@ -868,7 +907,7 @@
             pg[at, 6 * HD : 8 * HD] = gate_grad[:, : 2 * HD].astype(BF16)
             og[...] = pltpu.roll(gate_grad[:, 2 * HD :], net.none + HD, 1)
 
-            @pl.loop(0, 2)
+            @pl.loop(0, 2, unroll=True)
             def _(j):
                 t = place * 2 + j
                 here = tile(t, seq)
@@ -918,17 +957,6 @@
                     extra = matmul_tn(low_logit[j], wf_ref[:, to])
                     part[tile(place * 2 + j, seq), to] = (main[j * seq : (j + 1) * seq] + extra).astype(BF16)
 
-        @pl.loop(1, DEPTH + 1)
-        def _(k):
-            @pl.when(k < DEPTH)
-            def _():
-                for wave in waves:
-                    wave.hand_on(k)
-
-            for wave in waves:
-                wave.across(k - 1)
-            unit(k - 1)
-
         gathers = [
             Gather(
                 net,
@@ -941,10 +969,26 @@
             for c in range(PIECES)
         ]
 
-        @pl.loop(0, DEPTH)
-        def _(j):
+        @pl.loop(1, DEPTH + 1)
+        def _(k):
+            @pl.when(k < DEPTH)
+            def _():
+                for wave in waves:
+                    wave.hand_on(k)
+
+            for wave in waves:
+                wave.across(k - 1)
+
+            @pl.when(k == DEPTH)
+            def _():
+                for gather in gathers:
+                    gather.begin(DEPTH - 2)
+
+            unit(k - 1)
+
+        for k in (DEPTH - 1, *range(DEPTH - 3, -1, -1)):
             for gather in gathers:
-                gather.begin(DEPTH - 1 - j)
+                gather.begin(k)
 
         @pl.loop(0, model // 256)
         def _(j):
@@ -958,14 +1002,33 @@
 
         def owned(t, u):
             return tile(t * share + u, held)
+
+        def seen(f):
+            start = jnp.minimum(lax.div(f * held, 128) * 128, model - window)
+            return pl.ds(pl.multiple_of(start, 128), window)
+
+        small_send, small_recv = net.take(n), net.take(n)
+        lines[...] = jnp.zeros_like(lines)
+        lines[0:1] = sums_ref[0:1]
+        lines[1 : 1 + HEADS] = forget_sum[:HEADS]
+        for i in range(3):
+            lines[4 + i : 5 + i] = jnp.broadcast_to(jnp.sum(sums_ref[1 + i : 2 + i], axis=1, keepdims=True), (1, model))
+        lines[7:8] = jnp.broadcast_to(jnp.sum(valid_ref[...], axis=0, keepdims=True), (1, model))
+        lines[8 : 8 + HEADS] = jnp.broadcast_to(jnp.sum(bias_sum[:HEADS], axis=1, keepdims=True), (HEADS, model))
+        small_got[net.f] = lines[:, seen(net.f)]
+        for k in range(1, n):
+            net.send(
+                lines.at[:, seen(others[k])], small_got.at[net.f], small_send + k, small_recv + net.f, others[k]
+            )
 
         in_send, in_recv = net.take(share * TP), net.take(share * TP)
         out_send, out_recv = net.take(share), net.take(share)
         over, landed = net.take(TP), net.take(TP)
         away, back_in = net.take(TP * reps), net.take(TP * reps)
         out_away, out_back = net.take(reps), net.take(reps)
-        small_send, small_recv = net.take(n), net.take(n)
+        first_send, first_recv = net.take(n), net.take(n)
         mid_send, mid_recv = net.take(reps), net.take(reps)
+        swap_send, swap_recv = net.take(TP * reps), net.take(TP * reps)
         for k, u in partners:
             slot, f = share - 1 - k, net.t * share + u
             for j in range(TP):
@@ -975,6 +1038,15 @@
                 )
             net.send(out_part.at[tile(u, held)], out_got.at[slot], out_send + k, out_recv + slot, f)
 
+        replicas = [lax.rem(net.r + k, reps) for k in range(reps)]
+
+        def owned_bit(t, r):
+            start = (t * share + net.u) * held + (r * bit if cut > 1 else 0)
+            return pl.ds(pl.multiple_of(start, bit), bit)
+
+        def piece(r, t):
+            return in_all.at[0, t, tile(r, bit)] if cut > 1 else in_all.at[r, t]
+
         def steps(start, stop):
             @pl.loop(start, stop)
             def _(j):
@@ -988,62 +1060,60 @@
             for slot in range(share - 1):
                 net.arrive(in_got.at[slot, t], in_recv + share * t + slot)
                 total = total + in_got[slot, t].astype(F32)
-            if j < TP - 1:
-                in_part[owned(t, net.u)] = total.astype(BF16)
-            else:
-                in_all[net.r, t] = total.astype(BF16)
+            in_part[owned(t, net.u)] = total.astype(BF16)
+            if cut > 1:
+                for k in range(1, reps):
+                    net.send(
+                        in_part.at[owned_bit(t, replicas[k])], swapped_in.at[net.r, t], swap_send + TP * k + j,
+                        swap_recv + TP * net.r + t, net.f, r=replicas[k],
+                    )
         total = out_part[tile(net.u, held)].astype(F32)
         for slot in range(share - 1):
             net.arrive(out_got.at[slot], out_recv + slot)
             total = total + out_got[slot].astype(F32)
         out_all[net.r] = total.astype(BF16)
-        for j in range(TP - 1):
-            t = chips[j + 1]
-            net.send(in_part.at[owned(t, net.u)], in_all.at[net.r, net.t], over + j, landed + net.t, net.place(t))
-        replicas = [lax.rem(net.r + k, reps) for k in range(reps)]
+        steps(1, 2)
+        for j in range(TP):
+            t = chips[(j + 1) % TP]
+            here = owned_bit(t, net.r)
+            if cut > 1:
+                total = in_part[here].astype(F32)
+                for k in range(1, reps):
+                    net.arrive(swapped_in.at[replicas[k], t], swap_recv + TP * replicas[k] + t)
+                    total = total + swapped_in[replicas[k], t].astype(F32)
+                in_part[here] = total.astype(BF16)
+            if j < TP - 1:
+                net.send(in_part.at[here], piece(net.r, net.t), over + j, landed + net.t, net.place(t))
+            else:
+                piece(net.r, net.t)[...] = in_part[here]
         for k in range(1, reps):
             net.send(
                 out_all.at[net.r], out_all.at[net.r], out_away + k, out_back + net.r, net.f, r=replicas[k]
             )
             net.send(
-                in_all.at[net.r, net.t], in_all.at[net.r, net.t], away + k, back_in + TP * net.r + net.t, net.f,
-                r=replicas[k],
+                piece(net.r, net.t), piece(net.r, net.t), away + k, back_in + TP * net.r + net.t, net.f, r=replicas[k]
             )
-        steps(1, DEPTH)
+        steps(2, DEPTH)
 
         layer_in = x_ref[...].astype(F32)
         scale = lax.rsqrt(jnp.mean(layer_in * layer_in, axis=-1, keepdims=True) + EPSILON)
         lifted = rows_sum[...] * gains_ref[0:1]
         mean = jnp.mean(layer_in * lifted, axis=-1, keepdims=True)
         input_ref[...] = grad_ref[...] + scale * lifted - layer_in * (scale * scale * scale) * mean
-        lines[...] = jnp.zeros_like(lines)
-        lines[0:1, :model] = jnp.sum(rows_sum[...] * layer_in * scale, axis=0, keepdims=True)
-        lines[1:2, :model] = sums_ref[0:1]
-        lines[2 : 2 + HEADS, :model] = forget_sum[:HEADS]
-        for i in range(3):
-            lines[5 + i : 6 + i] = jnp.broadcast_to(
-                jnp.sum(sums_ref[1 + i : 2 + i], axis=1, keepdims=True), (1, model + window)
-            )
-        lines[8:9] = jnp.broadcast_to(jnp.sum(valid_ref[...], axis=0, keepdims=True), (1, model + window))
-        lines[9 : 9 + HEADS] = jnp.broadcast_to(
-            jnp.sum(bias_sum[:HEADS], axis=1, keepdims=True), (HEADS, model + window)
+        late[...] = jnp.broadcast_to(
+            jnp.sum(rows_sum[...] * layer_in * scale, axis=0, keepdims=True), (8, model)
         )
-
-        def seen(f):
-            return pl.ds(pl.multiple_of(lax.div(f * held, 128) * 128, 128), window)
-
-        small_got[net.f] = lines[:, seen(net.f)]
+        first_got[net.f] = late[:, seen(net.f)]
         for k in range(1, n):
             net.send(
-                lines.at[:, seen(others[k])], small_got.at[net.f], small_send + k, small_recv + net.f, others[k]
+                late.at[:, seen(others[k])], first_got.at[net.f], first_send + k, first_recv + net.f, others[k]
             )
         for j in range(1, TP):
             t = chips[TP - j]
-            net.arrive(in_all.at[net.r, t], landed + t)
+            net.arrive(piece(net.r, t), landed + t)
             for k in range(1, reps):
                 net.send(
-                    in_all.at[net.r, t], in_all.at[net.r, t], away + reps * j + k, back_in + TP * net.r + t, net.f,
-                    r=replicas[k],
+                    piece(net.r, t), piece(net.r, t), away + reps * j + k, back_in + TP * net.r + t, net.f, r=replicas[k]
                 )
         for k in range(1, n):
             net.arrive(small_got.at[others[k]], small_recv + others[k])
@@ -1051,7 +1121,14 @@
             total = small_got[t * share]
             for u in range(1, share):
                 total = total + small_got[t * share + u]
-            small_mid[net.r, t] = total
+            small_mid[net.r, t, :ROWS] = total
+        for k in range(1, n):
+            net.arrive(first_got.at[others[k]], first_recv + others[k])
+        for t in range(TP):
+            total = first_got[t * share]
+            for u in range(1, share):
+                total = total + first_got[t * share + u]
+            small_mid[net.r, t, ROWS:] = total
         for k in range(1, reps):
             net.send(
                 small_mid.at[net.r], small_mid.at[net.r], mid_send + k, mid_recv + net.r, net.f, r=replicas[k]
@@ -1060,21 +1137,41 @@
             r = replicas[k]
             net.arrive(out_all.at[r], out_back + r)
             for t in range(TP):
-                net.arrive(in_all.at[r, t], back_in + TP * r + t)
-            net.arrive(small_mid.at[r], mid_recv + r)
+                net.arrive(piece(r, t), back_in + TP * r + t)
         for t in range(TP):
             for block in range(4):
                 for column, wide, to in head_pieces(t, block):
                     total = in_all[0, t, :, to : to + wide].astype(F32)
-                    for r in range(1, reps):
+                    for r in range(1, sheets):
                         total = total + in_all[r, t, :, to : to + wide].astype(F32)
                     in_ref[:, column : column + wide] = total
+        for r in replicas[1:]:
+            net.arrive(small_mid.at[r], mid_recv + r)
         total, small = out_all[0].astype(F32), small_mid[0]
         for r in range(1, reps):
             total = total + out_all[r].astype(F32)
             small = small + small_mid[r]
         out_ref[...] = total
-        small_ref[...] = small
+        together = jnp.sum(small, axis=0)
+        turn = lax.rem(2 * window - (net.f * held - jnp.minimum(lax.div(net.f * held, 128) * 128, model - window)), window)
+        gain_rows = pltpu.roll(together, turn, 1)
+        gains_out[0:1] = gain_rows[ROWS : ROWS + 1, :held]
+        gains_out[1:2] = gain_rows[0:1, :held]
+        mean_squares = together[4:7, :128] / (together[7:8, :128] * model)
+        stats_ref[...] = jnp.sqrt(mean_squares + EPSILON)
+        forget = jnp.zeros((128, 128), F32)
+        biases = jnp.zeros((1, 128), F32)
+        lane = lax.broadcasted_iota(jnp.int32, (1, 128), 1)
+        for t in range(TP):
+            turned = pltpu.roll(small[t], turn, 1)[:, :128]
+            for h in range(HEADS):
+                row = HEADS * t + h
+                forget = jnp.where(
+                    lax.broadcasted_iota(jnp.int32, (128, 128), 0) == row, turned[1 + h : 2 + h], forget
+                )
+                biases = jnp.where(lane == row, small[t, 8 + h : 9 + h, :128], biases)
+        forget_ref[...] = forget.T[:held, :H]
+        bias_ref[...] = biases[:, :H]
         net.drain()
         for wave in waves:
             wave.drain()
@@ -1091,7 +1188,10 @@
             (shape((seq, model), F32), VMEM),
             (shape((held, 4 * model), F32), VMEM),
             (shape((held, model), F32), VMEM),
-            (shape((TP, ROWS, window), F32), VMEM),
+            (shape((2, held), F32), VMEM),
+            (shape((held, H), F32), VMEM),
+            (shape((1, H), F32), VMEM),
+            (shape((3, 128), F32), VMEM),
         ],
         [
             pltpu.VMEM((rows_all, model), BF16),
@@ -1112,18 +1212,21 @@
             pltpu.VMEM((2, ROWS, seq), BF16),
             pltpu.VMEM((ROWS, seq), F32),
             pltpu.VMEM((ROWS, model), F32),
-            pltpu.VMEM((ROWS, model + window), F32),
+            pltpu.VMEM((ROWS, model), F32),
+            pltpu.VMEM((8, model), F32),
             pltpu.VMEM((model, width), BF16),
             pltpu.VMEM((share - 1, TP, held, width), BF16),
-            pltpu.VMEM((reps, TP, held, width), BF16),
+            pltpu.VMEM((reps, TP, bit, width) if cut > 1 else (1, 1, 16, 128), BF16),
+            pltpu.VMEM((sheets, TP, held, width), BF16),
             pltpu.VMEM((4 * HD, model), BF16),
             pltpu.VMEM((share - 1, held, model), BF16),
             pltpu.VMEM((reps, held, model), BF16),
             pltpu.VMEM((n, ROWS, window), F32),
-            pltpu.VMEM((reps, TP, ROWS, window), F32),
+            pltpu.VMEM((n, 8, window), F32),
+            pltpu.VMEM((reps, TP, ROWS + 8, window), F32),
             pltpu.SemaphoreType.DMA((8,)),
         ],
-        20 * PIECES + 24 * PIECES + 2 * share * (TP + 1) + 2 * TP + 2 * reps * (TP + 2) + 2 * n,
+        20 * PIECES + 24 * PIECES + 2 * share * (TP + 1) + 2 * TP + 2 * reps * (2 * TP + 2) + 4 * n,
     )
 
 
@@ -1169,16 +1272,10 @@
     activations, middle_grad, sums, ffn_in_sum, ffn_down_sum = feed_forward(
         reps, share, tokens[0], branch_attn, gains, valid_col, cot, ffn_in, ffn_down
     )
-    input_grad, grad_in, grad_out, gathered = attention_back(
+    input_grad, grad_in, grad_out, grad_gains, grad_forget, bias_total, stats = attention_back(
         reps, share, tokens[0], middle_grad, sums, valid_col, rows_a, proj, sig, att, probability, logit, w_cols, w_rows,
         w_forget, gains,
     )
-
-    mine = lax.dynamic_slice_in_dim(gathered, f * held % 128, held, axis=2)
-    together = jnp.sum(mine, axis=0)
-    grad_forget = mine[:, 2 : 2 + heads].reshape(H, held).T
-    bias_total = mine[:, 9 : 9 + heads, 0].reshape(H)
-    stats = jnp.sqrt(together[5:8, 0] / (together[8, 0] * model) + EPSILON)
 
     def over_reps(values_in):
         return jnp.sum(values_in.astype(F32), axis=0)
@@ -1189,15 +1286,15 @@
     return (
         activations[None],
         input_grad[None],
-        together[0],
+        grad_gains[0],
         grad_in,
         grad_forget,
-        bias_total,
+        bias_total[0],
         grad_out,
-        together[1],
+        grad_gains[1],
         grad_ffn_in,
         over_reps(ffn_down_sum),
-        stats,
+        stats[:, 0],
     )
 
 

time: 419 us -> 403 us (0.962); the launches traced: 413 us -> 402 us
  Pallas kernels: 392 us -> 381 us
    pallas_call x3, Pallas kernels: 392 us -> 381 us  [call(): pl.pallas_call(body, name=name, out_shape=tuple((shape for shape, _ in ou...]
where the time goes in v3:
time: 403 us; the launch traced here: 402 us
  Pallas kernels  381 us (95%)
  local copies, waits for them, and re-layouts  11.1 us (3%)
  other arithmetic  8.07 us (2%)
    pallas_call x3, Pallas kernels, call(): pl.pallas_call(body, name=name, out_shape=tuple((shape for shape, _ in ou...  381 us

profile of v3, /device:TPU:0, one launch (start us, length us, event | category | flops | bytes accessed | tf_op | source)
XLA Modules:
  0.0 401.5 jit_solution(1057420383853834793)
XLA Ops:
  1.3 0.1 pad.18.clone
  1.4 0.7 dynamic_slice.3
  2.1 0.1 pad.19.clone
  2.2 0.5 convert_bitcast_fusion.1
  2.7 0.7 convert_bitcast_fusion
  3.4 0.7 copy.27.bias_col_ref
  4.1 0.7 fusion.4
  4.9 0.7 maximum_maximum_fusion.small_ref
  5.5 0.7 copy.28.valid_ref
  6.3 142.1 %attention.1 = (f32[128,1536]{1,0:T(8,128)}, bf16[1024,1536]{1,0:T(8,128)(2,1)}, bf16[1024,1536]{1,0:T(8,128)(2,1)}, bf16[1024,768]{1,0:T(8,128)(2,1)}, f32[1024...) custom-call(bf16[128,1536]{1,0:T(8,128)(2,1)} %bitcast.23, ...), custom_call_target="tpu_custom_call" | custom-call | tf_op jit(solution)/shard_map/attention/pallas_call | solution.py:257
  148.4 114.1 %feed_forward.1 = (bf16[128,1536]{1,0:T(8,128)(2,1)}, f32[128,1536]{1,0:T(8,128)}, f32[8,1536]{1,0:T(8,128)}, bf16[2,1536,512]{2,1,0:T(8,128)(2,1)}, bf16[2,256,1536]{2,1,0:T(8,128)(2,1)}) custom-call(bf16[128,1536]{1,0:T(8,128)(2,1)} %bitcast.24, f32[128,1536]{1,0:T(8,128)} %get-tuple-element.35.branch_ref, f32[8,1536]{1,0:T(8,128)} %get-tuple-element.36.gain_ref.gains_ref, ...), custom_call_target="tpu_custom_call" | custom-call | tf_op jit(solution)/shard_map/feed_forward/pallas_call | solution.py:257
  262.5 124.8 %attention_back.1 = (f32[128,1536]{1,0:T(8,128)}, f32[96,6144]{1,0:T(8,128)}, f32[96,1536]{1,0:T(8,128)}, f32[2,96]{1,0:T(2,128)}, f32[96,24]{1,0:T(8,128)}, /*index=5*/f32[1,24]{1,0:T(1,128)}, f32[3,128]{1,0:T(4,128)}) custom-call(bf16[128,1536]{1,0:T(8,128)(2,1)} %bitcast.25, f32[128,1536]{1,0:T(8,128)} %get-tuple-element.39.grad_ref, ...), custom_call_target="tpu_custom_call" | custom-call | tf_op jit(solution)/shard_map/attention_back/pallas_call | solution.py:257
  387.2 0.0 copy-start
  387.3 1.4 slice_reduce_fusion
  388.7 1.3 slice_bitcast_fusion.2
  390.0 1.5 copy.30
  391.4 2.9 convert_reduce_fusion.1
  394.4 0.0 copy-done
  394.4 0.6 convert_reduce_fusion
  395.0 0.2 slice_bitcast_fusion.1
  395.3 0.0 copy-start.4
  395.3 0.0 copy-start.2
  395.3 0.0 copy-start.1
  395.3 1.9 pad_maximum_fusion
  397.2 0.0 copy-done.4
  397.2 0.7 copy.37
  397.9 0.0 copy-done.2
  397.9 0.9 copy.38
  398.8 0.0 copy-done.1
  398.8 0.0 copy-start.5
  398.8 0.0 copy-start.3
  398.8 1.4 copy.39
  400.2 0.0 copy-done.5
  400.2 0.5 copy.40
  400.7 0.0 copy-done.3
  400.7 0.8 copy.41
  (1 shorter events, 0.0 us)
Async XLA Ops:
  387.2 7.2 %copy-start = (bf16[2,1536,512]{2,1,0:T(8,128)(2,1)S(1)}, bf16[2,1536,512]{2,1,0:T(8,128)(2,1)}, u32[]{:S(2)}) copy-start(bf16[2,1536,512]{2,1,0:T(8,128)(2,1)} %get-tuple-element.56) | copy-start | bytes 9437188
  395.3 1.9 copy-start.4
  395.3 2.6 copy-start.2
  395.3 3.5 copy-start.1
  398.8 1.4 copy-start.5
  398.8 1.9 copy-start.3

commit v4 on v3

--- a/solution.py
+++ b/solution.py
@@ -44,6 +44,9 @@
 
     def grid(self, z, x):
         return (z * 2 + x) * self.share + self.u
+
+    def pair(self):
+        return self.z + 1 - 2 * lax.rem(self.z, 2)
 
     def partners(self):
         for k in range(1, self.share):
@@ -135,8 +138,8 @@
 
 
 class Wave:
-    def __init__(self, net, block):
-        self.net, self.block = net, block
+    def __init__(self, net, block, bent=False):
+        self.net, self.block, self.bent = net, block, bent
         self.recv = net.take(TP)
         self.up, self.down, self.side = net.take(DEPTH), net.take(DEPTH), net.take(DEPTH)
 
@@ -158,20 +161,30 @@
             (None, net.copy(block, block, self.side + k, sem, net.grid(z, 1 - x))),
         ]
 
+    def turn(self):
+        if self.bent:
+            net = self.net
+            t = net.z * 2 + 1 - net.x
+            block, sem = self.block(t), self.recv + t
+            net.arrive(block, sem)
+            net.copy(block, block, self.side + 1, sem, net.grid(net.pair(), net.x)).start()
+
     def hand_on(self, k, own=False):
         net = self.net
         t = nearest(net.z, k) * 2 + net.x
         if not own:
             net.arrive(self.block(t), self.recv + t, None if isinstance(k, int) else k > 0)
-        for cond, copy in self.copies(k):
-            if cond is None:
-                copy.start()
-            else:
-                pl.when(cond)(copy.start)
+        up, down, side = self.copies(k)
+        for cond, copy in (up, down):
+            pl.when(cond)(copy.start)
+        if self.bent:
+            pl.when(net.none + k != 1)(side[1].start)
+        else:
+            side[1].start()
 
     def across(self, k):
         t = nearest(self.net.z, k) * 2 + 1 - self.net.x
-        self.net.arrive(self.block(t), self.recv + t)
+        self.net.arrive(self.block(t), self.recv + t, self.net.none + k > 0 if self.bent else None)
 
     def drain(self):
         @pl.loop(0, DEPTH)
@@ -184,8 +197,9 @@
 
 
 class Gather:
-    def __init__(self, net, part, side, up, down, total):
+    def __init__(self, net, part, side, up, down, total, bent=False):
         self.net, self.part, self.side, self.up, self.down, self.total = net, part, side, up, down, total
+        self.bent = bent
         self.sems = [net.take(DEPTH) for _ in range(6)]
 
     def across(self, k):
@@ -219,6 +233,18 @@
         ]
 
     def begin(self, k):
+        net = self.net
+        z, pair = net.z, net.pair()
+        if self.bent and k == 1:
+            net.copy(
+                self.part(pair * 2 + 1 - net.x), self.side(z), self.sems[0] + pair, self.sems[1] + z,
+                net.grid(pair, net.x),
+            ).start()
+            return
+        if self.bent and k == 0:
+            net.arrive(self.side(pair), self.sems[1] + pair)
+            part = self.part(z * 2 + 1 - net.x)
+            part[...] = (part[...].astype(F32) + self.side(pair)[...].astype(F32)).astype(BF16)
         self.across(k).start()
 
     def step(self, k):
@@ -226,8 +252,16 @@
         z = net.z
         zo = nearest(z, k)
         part = self.part(zo * 2 + net.x)
-        net.arrive(self.side(zo), self.sems[1] + zo)
-        self.total[...] = part[...].astype(F32) + self.side(zo)[...].astype(F32)
+        if self.bent:
+            self.total[...] = part[...].astype(F32)
+
+            @pl.when(k != 1)
+            def _():
+                net.arrive(self.side(zo), self.sems[1] + zo)
+                self.total[...] += self.side(zo)[...].astype(F32)
+        else:
+            net.arrive(self.side(zo), self.sems[1] + zo)
+            self.total[...] = part[...].astype(F32) + self.side(zo)[...].astype(F32)
         for cond, ref, sem in (
             ((zo >= z) & (z > 0), self.up(zo), self.sems[3]),
             ((zo <= z) & (z < DEPTH - 1), self.down(zo), self.sems[5]),
@@ -251,6 +285,19 @@
             self.across(k).wait_send()
             for cond, copy in self.along(k):
                 pl.when(cond)(copy.wait_send)
+
+
+def column(row):
+    size = row.shape[1]
+    square = (size, size)
+    same = lax.broadcasted_iota(jnp.int32, square, 0) == lax.broadcasted_iota(jnp.int32, square, 1)
+    return jnp.sum(jnp.where(same, row, 0.0), axis=1, keepdims=True)
+
+
+def begin_last(gathers, bent):
+    for gather in gathers:
+        if gather.bent == bent:
+            gather.begin(0)
 
 
 def call(body, name, number, operands, in_specs, outs, scratch, sems, limit=60 << 20):
@@ -386,6 +433,8 @@
 
             @pl.when(k == 1)
             def _():
+                for wave in waves:
+                    wave.turn()
                 for copy in own:
                     copy.wait()
                 for dst, sem in arriving:
@@ -401,17 +450,21 @@
 
             unit(k - 1)
 
-        for k in (DEPTH - 1, *range(DEPTH - 3, -1, -1)):
+        for k in (DEPTH - 1, *range(DEPTH - 3, 0, -1)):
             for gather in gathers[0]:
                 gather.begin(k)
-        for k in range(DEPTH - 1, -1, -1):
-            for gather in gathers[1]:
-                gather.begin(k)
+        begin_last(gathers[0], False)
 
         @pl.loop(0, model // 256)
         def _(j):
             at = tile(j, 256)
             in_part[at] = matmul_tn(rows[:, at], grads[...]).astype(BF16)
+
+        begin_last(gathers[0], True)
+        for k in range(DEPTH - 1, 0, -1):
+            for gather in gathers[1]:
+                gather.begin(k)
+        begin_last(gathers[1], False)
 
         @pl.loop(0, 3)
         def _(j):
@@ -458,13 +511,14 @@
                     gather.step(DEPTH - 1 - j)
 
         steps(gathers[0], 0, 2)
+        begin_last(gathers[1], True)
         own_grads()
         steps(gathers[0], 2, DEPTH)
         steps(gathers[1], 0, DEPTH)
 
         result = middle[...] + ffn_sum[...]
         act_ref[...] = result.astype(BF16)
-        valid_col = valid_ref[...]
+        valid_col = column(valid_ref[...].astype(F32))
         scale = lax.rsqrt(jnp.mean(middle[...] * middle[...], axis=-1, keepdims=True) + EPSILON)
         lifted = rows_sum[...] * gain_ref[1:2]
         mean = jnp.mean(middle[...] * lifted, axis=-1, keepdims=True)
@@ -537,7 +591,7 @@
     return [(base, 2 * HD, block * 2 * HD), (base + 2 * HD, HD, 8 * HD + block * HD)]
 
 
-def attention(reps, share, x, cot, w_in, small, w_out, bias_row, bias_col):
+def attention(reps, share, x, cot, w_in, w_out, forget, gain_a, gain_f, mask, start, bias):
     n = TP * share
     seq, model = x.shape
     held = w_in.shape[0]
@@ -549,7 +603,7 @@
     cut = cuts(reps, held)
 
     def body(
-        x_ref, cot_ref, in_ref, small_ref, out_ref, bias_row_ref, bias_col_ref,
+        x_ref, cot_ref, in_ref, out_ref, forget_ref, gain_a_ref, gain_f_ref, mask_ref, start_ref, bias_ref,
         branch_ref, cot_out, rows_out, proj_out, sig_out, att_out, prob_out, logit_ref, wc_out, wo_out, wf_ref, gains_ref,
         xs, cots, rows, proj, sig, att, prob, wc, wo, split, smalls, lines, part, side, up, down, gated, local, sems,
     ):
@@ -573,11 +627,18 @@
         own = [
             pltpu.make_async_copy(x_ref, seq_block(xs, net.t), local.at[0]),
             pltpu.make_async_copy(cot_ref, seq_block(cots, net.t), local.at[1]),
-            pltpu.make_async_copy(small_ref, smalls.at[net.f], local.at[2]),
             pltpu.make_async_copy(out_ref, wo.at[tile(net.u, held)], local.at[3]),
         ]
         for copy in own:
             copy.start()
+        small = lines.at[:, pl.ds(0, 128)]
+        small[...] = jnp.zeros((32, 128), F32)
+        small[:H, :held] = forget_ref[...].astype(F32)
+        small[H : H + 1, :held] = gain_a_ref[...].astype(F32)
+        small[H + 1 : H + 2, :held] = gain_f_ref[...].astype(F32)
+        small[H + 2 : H + 3, :seq] = mask_ref[...].astype(F32)
+        small[H + 3 : H + 4, :seq] = jnp.full((1, seq), start_ref[0], jnp.int32).astype(F32)
+        smalls[net.f] = small[...].astype(BF16)
         for t in range(TP):
             for block in range(4):
                 for column, wide, to in head_pieces(t, block):
@@ -595,7 +656,7 @@
         w_away = net.take(TP * cut)
         wo_send, wo_recv = net.take(share), net.take(share)
         for k in range(1, n):
-            net.send(small_ref, smalls.at[net.f], small_send + k, small_recv + net.f, others[k])
+            net.send(smalls.at[net.f], smalls.at[net.f], small_send + k, small_recv + net.f, others[k])
         for k in range(1, TP):
             net.send(
                 split.at[chips[k], piece_of(net.r)], held_piece(net.f, net.r), w_send + k, w_recv + cut * net.f + spot(net.r),
@@ -633,6 +694,9 @@
                         net.send(got, got, w_pass + share * (TP * (q + 1) + k) + j, sem, net.t * share + u)
                     for p in range(1, cut if q == 0 else 1):
                         net.send(got, got, w_away + TP * p + k, sem, net.f, r=replicas[p])
+                if q == 0:
+                    for wave in waves:
+                        wave.hand_on(2)
             for k in range(1, n):
                 net.arrive(smalls.at[others[k]], small_recv + others[k])
             for j in range(model // 128):
@@ -656,6 +720,14 @@
                         net.arrive(held_piece(f, r), w_recv + cut * f + spot(r))
             own_cols.wait()
 
+        own_head = lax.broadcasted_iota(jnp.int32, (ROWS, H), 0)
+        picked = own_head + HEADS * net.t == lax.broadcasted_iota(jnp.int32, (ROWS, H), 1)
+        bias_col = jnp.sum(
+            jnp.where(picked & (own_head < HEADS), bias_ref[...].astype(F32), 0.0), axis=1, keepdims=True
+        )
+        few = (ROWS, ROWS)
+        same = lax.broadcasted_iota(jnp.int32, few, 0) == lax.broadcasted_iota(jnp.int32, few, 1)
+        bias_row = jnp.sum(jnp.where(same, bias_col, 0.0), axis=0, keepdims=True)
         square = (seq, seq)
         at_row = lax.broadcasted_iota(jnp.int32, square, 0)
         at_col = lax.broadcasted_iota(jnp.int32, square, 1)
@@ -684,8 +756,8 @@
                 allowed = (causal | inside) & (valid > 0.0)
                 sign = jnp.where(causal, 1.0, -1.0)
                 below = sign * 0.5 + 0.5
-                logit_col = matmul_nt(rows[here], wf_ref[...]) + bias_row_ref[...]
-                logit_row = matmul_nt(wf_ref[...], rows[here]) + bias_col_ref[...]
+                logit_col = matmul_nt(rows[here], wf_ref[...]) + bias_row
+                logit_row = matmul_nt(wf_ref[...], rows[here]) + bias_col
                 logit_ref[t] = logit_row
                 decay_col = jnp.dot(
                     below, log_sigmoid(logit_col), precision=lax.Precision.HIGHEST, preferred_element_type=F32
@@ -735,20 +807,24 @@
 
         for wave in waves:
             wave.hand_on(1)
+            wave.turn()
         weights()
 
         @pl.loop(1, DEPTH + 1)
         def _(k):
-            @pl.when((k > 1) & (k < DEPTH))
+            @pl.when(k == 2)
             def _():
                 for wave in waves:
-                    wave.hand_on(k)
-
-            @pl.when(k == DEPTH - 1)
-            def _():
+                    wave.hand_on(DEPTH - 1)
                 for wave in cot_waves:
                     for cond, copy in wave.copies(0)[:2]:
                         pl.when(cond)(copy.start)
+                    wave.turn()
+
+            @pl.when(k == 3)
+            def _():
+                for wave in cot_waves:
+                    wave.hand_on(1)
 
             for wave in waves:
                 wave.across(k - 1)
@@ -769,9 +845,10 @@
                 ]
             )
         ]
-        for k in (DEPTH - 1, *range(DEPTH - 3, -1, -1)):
+        for k in (DEPTH - 1, *range(DEPTH - 3, 0, -1)):
             for gather in gathers:
                 gather.begin(k)
+        begin_last(gathers, False)
 
         for copy in keep:
             copy.start()
@@ -781,10 +858,14 @@
             for gather in gathers:
                 gather.step(DEPTH - 1 - j)
 
-            @pl.when(j < DEPTH - 1)
+            @pl.when(j == 0)
+            def _():
+                begin_last(gathers, True)
+
+            @pl.when(j < DEPTH - 2)
             def _():
                 for wave in cot_waves:
-                    wave.hand_on(j + 1)
+                    wave.hand_on(j + 2)
 
         for k in range(DEPTH):
             for wave in cot_waves:
@@ -811,8 +892,8 @@
         ((TP * HEADS, seq, seq), F32),
     ]
     return call(
-        body, "attention", 1, (x, cot, w_in, small, w_out, bias_row, bias_col),
-        [ANY, ANY, VMEM, VMEM, ANY, VMEM, VMEM],
+        body, "attention", 1, (x, cot, w_in, w_out, forget, gain_a, gain_f, mask, start, bias),
+        [ANY, ANY, VMEM, ANY, VMEM, VMEM, VMEM, VMEM, pl.BlockSpec(memory_space=pltpu.SMEM), VMEM],
         [(shape((seq, model), F32), VMEM)]
         + [(shape(*what), ANY) for what in kept]
         + [
@@ -840,7 +921,8 @@
 
 
 def attention_back(
-    reps, share, x, middle_grad, sums, valid, rows_a, proj, sig, att, prob, logit, wc, wo, wf, gains
+    reps, share, x, middle_grad, sums, valid, rows_a, proj, sig, att, prob, logit, wc, wo, wf, gains,
+    ffn_in, ffn_down,
 ):
     n = TP * share
     seq, model = x.shape
@@ -854,13 +936,15 @@
     cut = cuts(reps, held)
     bit = held // cut
     sheets = 1 if cut > 1 else reps
+    hs = ffn_down.shape[1]
 
     def body(
         x_ref, grad_ref, sums_ref, valid_ref, rows_in, proj_in, sig_in, att_in, prob_in, logit_ref, wc_in, wo_in, wf_ref,
-        gains_ref, input_ref, in_ref, out_ref, gains_out, forget_ref, bias_ref, stats_ref,
+        gains_ref, ffn_in_ref, ffn_down_ref,
+        input_ref, in_ref, out_ref, gains_out, forget_ref, bias_ref, stats_ref, ffn_in_out, ffn_down_out,
         rows, proj, sig, att, prob, wcs, wos, bgs, pg, gated, part, side, up, down, rows_sum, ag, og, low_logit, bias_sum,
         forget_sum, lines, late, in_part, in_got, swapped_in, in_all, out_part, out_got, out_all, small_got, first_got,
-        small_mid, local, sems,
+        small_mid, ffn_in, ffn_down, ffn_in_sum, ffn_down_sum, local, sems,
     ):
         net = Net(reps, share, sems)
         others = [lax.rem(net.f + k, n) for k in range(n)]
@@ -875,12 +959,20 @@
                 ]
             )
         ]
-        for copy in own:
+        ffn_parts = [
+            pltpu.make_async_copy(ffn_in_ref, ffn_in, local.at[7]),
+            pltpu.make_async_copy(ffn_down_ref, ffn_down, local.at[8]),
+        ]
+        ffn_totals = [
+            pltpu.make_async_copy(ffn_in_sum, ffn_in_out, local.at[9]),
+            pltpu.make_async_copy(ffn_down_sum, ffn_down_out, local.at[10]),
+        ]
+        for copy in own + ffn_parts:
             copy.start()
         bgs[tile(net.t, seq)] = grad_ref[...].astype(BF16)
         net.greet([(None, net.r, f) for f in others[1:]] + net.rep_peers())
         waves = [
-            Wave(net, lambda t, c=c: bgs.at[pl.ds(pl.multiple_of(t * seq + c * half, half), half)])
+            Wave(net, lambda t, c=c: bgs.at[pl.ds(pl.multiple_of(t * seq + c * half, half), half)], c == 1)
             for c in range(PIECES)
         ]
         for wave in waves:
@@ -964,7 +1056,7 @@
                     lambda j, ref=ref, c=c: ref.at[pl.ds(pl.multiple_of(j * seq + c * half, half), half)]
                     for ref in (part, side, up, down)
                 ],
-                rows_sum.at[pl.ds(c * half, half)],
+                rows_sum.at[pl.ds(c * half, half)], c == 1,
             )
             for c in range(PIECES)
         ]
@@ -976,6 +1068,11 @@
                 for wave in waves:
                     wave.hand_on(k)
 
+            @pl.when(k == 1)
+            def _():
+                for wave in waves:
+                    wave.turn()
+
             for wave in waves:
                 wave.across(k - 1)
 
@@ -986,9 +1083,10 @@
 
             unit(k - 1)
 
-        for k in (DEPTH - 1, *range(DEPTH - 3, -1, -1)):
+        for k in (DEPTH - 1, *range(DEPTH - 3, 0, -1)):
             for gather in gathers:
                 gather.begin(k)
+        begin_last(gathers, False)
 
         @pl.loop(0, model // 256)
         def _(j):
@@ -999,6 +1097,28 @@
         def _(j):
             at = tile(j, model // 3)
             out_part[:, at] = matmul_tn(gated[...], bgs[:, at]).astype(BF16)
+
+        begin_last(gathers, True)
+
+        def ffn_grads():
+            for copy in ffn_parts:
+                copy.wait()
+
+            @pl.loop(0, model // 256)
+            def _(j):
+                at = tile(j, 256)
+                for i in range(2):
+                    half_sum = ffn_in[0, at, i * hs : (i + 1) * hs].astype(F32)
+                    for r in range(1, reps):
+                        half_sum = half_sum + ffn_in[r, at, i * hs : (i + 1) * hs].astype(F32)
+                    ffn_in_sum[i, at] = half_sum
+                down_sum = ffn_down[0, :, at].astype(F32)
+                for r in range(1, reps):
+                    down_sum = down_sum + ffn_down[r, :, at].astype(F32)
+                ffn_down_sum[:, at] = down_sum
+
+            for copy in ffn_totals:
+                copy.start()
 
         def owned(t, u):
             return tile(t * share + u, held)
@@ -1013,7 +1133,7 @@
         lines[1 : 1 + HEADS] = forget_sum[:HEADS]
         for i in range(3):
             lines[4 + i : 5 + i] = jnp.broadcast_to(jnp.sum(sums_ref[1 + i : 2 + i], axis=1, keepdims=True), (1, model))
-        lines[7:8] = jnp.broadcast_to(jnp.sum(valid_ref[...], axis=0, keepdims=True), (1, model))
+        lines[7:8] = jnp.broadcast_to(jnp.sum(valid_ref[...].astype(F32), axis=1, keepdims=True), (1, model))
         lines[8 : 8 + HEADS] = jnp.broadcast_to(jnp.sum(bias_sum[:HEADS], axis=1, keepdims=True), (HEADS, model))
         small_got[net.f] = lines[:, seen(net.f)]
         for k in range(1, n):
@@ -1093,6 +1213,7 @@
             net.send(
                 piece(net.r, net.t), piece(net.r, net.t), away + k, back_in + TP * net.r + net.t, net.f, r=replicas[k]
             )
+        ffn_grads()
         steps(2, DEPTH)
 
         layer_in = x_ref[...].astype(F32)
@@ -1158,7 +1279,7 @@
         gains_out[0:1] = gain_rows[ROWS : ROWS + 1, :held]
         gains_out[1:2] = gain_rows[0:1, :held]
         mean_squares = together[4:7, :128] / (together[7:8, :128] * model)
-        stats_ref[...] = jnp.sqrt(mean_squares + EPSILON)
+        roots = jnp.sqrt(mean_squares + EPSILON)
         forget = jnp.zeros((128, 128), F32)
         biases = jnp.zeros((1, 128), F32)
         lane = lax.broadcasted_iota(jnp.int32, (1, 128), 1)
@@ -1170,28 +1291,33 @@
                     lax.broadcasted_iota(jnp.int32, (128, 128), 0) == row, turned[1 + h : 2 + h], forget
                 )
                 biases = jnp.where(lane == row, small[t, 8 + h : 9 + h, :128], biases)
-        forget_ref[...] = forget.T[:held, :H]
+        forget_ref[...] = forget[:H, :held]
         bias_ref[...] = biases[:, :H]
+        stats_ref[...] = jnp.where(lane == 0, roots[0:1], jnp.where(lane == 1, roots[1:2], roots[2:3]))[:, :3]
         net.drain()
         for wave in waves:
             wave.drain()
         for gather in gathers:
             gather.drain()
+        for copy in ffn_totals:
+            copy.wait()
 
     shape = jax.ShapeDtypeStruct
     line = pltpu.VMEM((DEPTH * seq, model), BF16)
     return call(
         body, "attention_back", 5,
-        (x, middle_grad, sums, valid, rows_a, proj, sig, att, prob, logit, wc, wo, wf, gains),
-        [VMEM] * 4 + [ANY] * 5 + [VMEM, ANY, ANY, VMEM, VMEM],
+        (x, middle_grad, sums, valid, rows_a, proj, sig, att, prob, logit, wc, wo, wf, gains, ffn_in, ffn_down),
+        [VMEM] * 4 + [ANY] * 5 + [VMEM, ANY, ANY, VMEM, VMEM, ANY, ANY],
         [
             (shape((seq, model), F32), VMEM),
             (shape((held, 4 * model), F32), VMEM),
             (shape((held, model), F32), VMEM),
             (shape((2, held), F32), VMEM),
-            (shape((held, H), F32), VMEM),
+            (shape((H, held), F32), VMEM),
             (shape((1, H), F32), VMEM),
-            (shape((3, 128), F32), VMEM),
+            (shape((1, 3), F32), VMEM),
+            (shape((2, model, hs), F32), ANY),
+            (shape((hs, model), F32), ANY),
         ],
         [
             pltpu.VMEM((rows_all, model), BF16),
@@ -1224,7 +1350,11 @@
             pltpu.VMEM((n, ROWS, window), F32),
             pltpu.VMEM((n, 8, window), F32),
             pltpu.VMEM((reps, TP, ROWS + 8, window), F32),
-            pltpu.SemaphoreType.DMA((8,)),
+            pltpu.VMEM((reps, model, 2 * hs), BF16),
+            pltpu.VMEM((reps, hs, model), BF16),
+            pltpu.VMEM((2, model, hs), F32),
+            pltpu.VMEM((hs, model), F32),
+            pltpu.SemaphoreType.DMA((11,)),
         ],
         20 * PIECES + 24 * PIECES + 2 * share * (TP + 1) + 2 * TP + 2 * reps * (2 * TP + 2) + 4 * n,
     )
@@ -1250,51 +1380,32 @@
     ffn_in,
     ffn_down,
 ):
-    n = TP * share
-    _, seq, model = tokens.shape
-    held = attn_in.shape[0]
-    heads = H // TP
-    f = lax.axis_index("fsdp")
-    t = f // share
-
-    small = jnp.concatenate([forget_w.T, gain_attn[None], gain_ffn[None]])
-    small = jnp.pad(small, ((0, 0), (0, 128 - held)))
-    marks = jnp.concatenate(
-        [valid_mask.astype(BF16), jnp.broadcast_to(pic_start.astype(BF16)[:, None], (1, seq))]
+    branch_attn, cot, rows_a, proj, sig, att, probability, logit, w_cols, w_rows, w_forget, gains = attention(
+        reps, share, tokens[0], cotangent[0], attn_in, attn_out, forget_w.T, gain_attn[None], gain_ffn[None],
+        valid_mask, pic_start, forget_bias[None],
     )
-    small = jnp.concatenate([small, marks, jnp.zeros((32 - H - 4, 128), BF16)])
-    bias = lax.dynamic_slice_in_dim(forget_bias, heads * t, heads).astype(F32)
-    bias = jnp.pad(bias, (0, ROWS - heads))
-    branch_attn, cot, rows_a, proj, sig, att, probability, logit, w_cols, w_rows, w_forget, gains = attention(
-        reps, share, tokens[0], cotangent[0], attn_in, small, attn_out, bias[None], bias[:, None]
+    activations, middle_grad, sums, ffn_in_sum, ffn_down_sum = feed_forward(
+        reps, share, tokens[0], branch_attn, gains, valid_mask, cot, ffn_in, ffn_down
     )
-    valid_col = valid_mask[0].astype(F32)[:, None]
-    activations, middle_grad, sums, ffn_in_sum, ffn_down_sum = feed_forward(
-        reps, share, tokens[0], branch_attn, gains, valid_col, cot, ffn_in, ffn_down
+    (
+        input_grad, grad_in, grad_out, grad_gains, grad_forget, bias_total, stats, grad_ffn_in, grad_ffn_down,
+    ) = attention_back(
+        reps, share, tokens[0], middle_grad, sums, valid_mask, rows_a, proj, sig, att, probability, logit, w_cols, w_rows,
+        w_forget, gains, ffn_in_sum, ffn_down_sum,
     )
-    input_grad, grad_in, grad_out, grad_gains, grad_forget, bias_total, stats = attention_back(
-        reps, share, tokens[0], middle_grad, sums, valid_col, rows_a, proj, sig, att, probability, logit, w_cols, w_rows,
-        w_forget, gains,
-    )
-
-    def over_reps(values_in):
-        return jnp.sum(values_in.astype(F32), axis=0)
-
-    hs = ffn_in.shape[2]
-    grad_ffn_in = over_reps(ffn_in_sum)
-    grad_ffn_in = jnp.stack([grad_ffn_in[:, :hs], grad_ffn_in[:, hs:]])
+
     return (
         activations[None],
         input_grad[None],
         grad_gains[0],
         grad_in,
-        grad_forget,
+        grad_forget.T,
         bias_total[0],
         grad_out,
         grad_gains[1],
         grad_ffn_in,
-        over_reps(ffn_down_sum),
-        stats[:, 0],
+        grad_ffn_down,
+        stats[0],
     )
 
 

time: 403 us -> 389 us (0.965)
  other arithmetic: 8.07 us -> 0 us
  Pallas kernels: 381 us -> 374 us
    pallas_call x3, Pallas kernels: 381 us -> 374 us  [call(): pl.pallas_call(body, name=name, out_shape=tuple((shape for shape, _ in ou...]
    unnamed x18 -> x25, local copies, waits for them, and re-layouts: 5.85 us -> 10.4 us
where the time goes in v4:
time: 389 us; the launch traced here: 387 us
  Pallas kernels  374 us (96%)
  local copies, waits for them, and re-layouts  11.7 us (3%)
    pallas_call x3, Pallas kernels, call(): pl.pallas_call(body, name=name, out_shape=tuple((shape for shape, _ in ou...  374 us
    unnamed x25, local copies, waits for them, and re-layouts  10.4 us

profile of v4, /device:TPU:0, one launch (start us, length us, event | category | flops | bytes accessed | tf_op | source)
XLA Modules:
  0.0 386.9 jit_solution(14689240250063839607)
XLA Ops:
  1.3 136.2 %attention.1 = (f32[128,1536]{1,0:T(8,128)}, bf16[1024,1536]{1,0:T(8,128)(2,1)}, bf16[1024,1536]{1,0:T(8,128)(2,1)}, bf16[1024,768]{1,0:T(8,128)(2,1)}, f32[1024...) custom-call(bf16[128,1536]{1,0:T(8,128)(2,1)} %bitcast.15, ...), custom_call_target="tpu_custom_call" | custom-call | tf_op jit(solution)/shard_map/attention/pallas_call | solution.py:304
  137.5 115.4 %feed_forward.1 = (bf16[128,1536]{1,0:T(8,128)(2,1)}, f32[128,1536]{1,0:T(8,128)}, f32[8,1536]{1,0:T(8,128)}, bf16[2,1536,512]{2,1,0:T(8,128)(2,1)}, bf16[2,256,1536]{2,1,0:T(8,128)(2,1)}) custom-call(bf16[128,1536]{1,0:T(8,128)(2,1)} %bitcast.16, f32[128,1536]{1,0:T(8,128)} %get-tuple-element.37.branch_ref, f32[8,1536]{1,0:T(8,128)} %get-tuple-element.38.gain_ref.gains_ref, ...), custom_call_target="tpu_custom_call" | custom-call | tf_op jit(solution)/shard_map/feed_forward/pallas_call | solution.py:304
  252.9 0.0 copy-start.4
  252.9 122.2 %attention_back.1 = (f32[128,1536]{1,0:T(8,128)}, f32[96,6144]{1,0:T(8,128)}, f32[96,1536]{1,0:T(8,128)}, f32[2,96]{1,0:T(2,128)}, f32[24,96]{1,0:T(8,128)}, /*i...) custom-call(bf16[128,1536]{1,0:T(8,128)(2,1)} %bitcast.17, ...), custom_call_target="tpu_custom_call" | custom-call | tf_op jit(solution)/shard_map/attention_back/pallas_call | solution.py:304
  375.1 0.0 copy-start.1
  375.1 1.3 slice_bitcast_fusion
  376.5 0.0 copy-done.4
  376.5 0.7 copy.33
  377.2 2.1 copy.34
  379.3 0.0 copy-done.1
  379.3 0.0 copy-start.5
  379.3 0.0 copy-start.7
  379.3 0.0 copy-start.3
  379.3 0.0 copy-start
  379.3 1.4 copy.35
  380.7 0.0 copy-done.5
  380.7 0.6 copy.36
  381.3 0.0 copy-done.7
  381.3 0.5 copy.37
  381.9 0.0 copy-done.3
  381.9 0.8 copy.38
  382.7 0.0 copy-done
  382.7 0.0 copy-start.2
  382.7 1.7 copy.39
  384.3 0.9 copy-done.2
  385.2 0.0 copy-start.6
  385.2 1.1 copy.40
  386.4 0.0 copy-done.6
  386.4 0.5 copy.41
Async XLA Ops:
  252.9 123.6 %copy-start.4 = (bf16[128,1536]{1,0:T(8,128)(2,1)S(1)}, bf16[128,1536]{1,0:T(8,128)(2,1)}, u32[]{:S(2)}) copy-start(bf16[128,1536]{1,0:T(8,128)(2,1)} %get-tuple-element.40) | copy-start | bytes 1179652
  375.1 4.2 %copy-start.1 = (f32[96,6144]{1,0:T(8,128)S(1)}, f32[96,6144]{1,0:T(8,128)}, u32[]{:S(2)}) copy-start(f32[96,6144]{1,0:T(8,128)} %get-tuple-element.79) | copy-start | bytes 7077892
  379.3 1.4 copy-start.5
  379.3 2.0 copy-start.7
  379.3 2.5 copy-start.3
  379.3 3.4 copy-start
  382.7 2.5 copy-start.2
  385.2 1.1 copy-start.6

commit v5 on v4

--- a/solution.py
+++ b/solution.py
@@ -292,6 +292,10 @@
     square = (size, size)
     same = lax.broadcasted_iota(jnp.int32, square, 0) == lax.broadcasted_iota(jnp.int32, square, 1)
     return jnp.sum(jnp.where(same, row, 0.0), axis=1, keepdims=True)
+
+
+def step_order(j):
+    return DEPTH - 1 - j + jnp.where(j == 1, 1, 0) - jnp.where(j == 0, 1, 0)
 
 
 def begin_last(gathers, bent):
@@ -829,10 +833,17 @@
             for wave in waves:
                 wave.across(k - 1)
 
+            @pl.when(k == DEPTH - 1)
+            def _():
+                for gather in gathers:
+                    gather.begin(1)
+
             @pl.when(k == DEPTH)
             def _():
                 for gather in gathers:
                     gather.begin(DEPTH - 2)
+                for wave in cot_waves:
+                    wave.hand_on(2)
 
             unit(k - 1)
 
@@ -845,9 +856,8 @@
                 ]
             )
         ]
-        for k in (DEPTH - 1, *range(DEPTH - 3, 0, -1)):
-            for gather in gathers:
-                gather.begin(k)
+        for gather in gathers:
+            gather.begin(DEPTH - 1)
         begin_last(gathers, False)
 
         for copy in keep:
@@ -856,16 +866,16 @@
         @pl.loop(0, DEPTH)
         def _(j):
             for gather in gathers:
-                gather.step(DEPTH - 1 - j)
+                gather.step(step_order(j))
 
             @pl.when(j == 0)
             def _():
                 begin_last(gathers, True)
 
-            @pl.when(j < DEPTH - 2)
+            @pl.when(j == 0)
             def _():
                 for wave in cot_waves:
-                    wave.hand_on(j + 2)
+                    wave.hand_on(DEPTH - 1)
 
         for k in range(DEPTH):
             for wave in cot_waves:
@@ -1076,6 +1086,11 @@
             for wave in waves:
                 wave.across(k - 1)
 
+            @pl.when(k == DEPTH - 1)
+            def _():
+                for gather in gathers:
+                    gather.begin(1)
+
             @pl.when(k == DEPTH)
             def _():
                 for gather in gathers:
@@ -1083,9 +1098,8 @@
 
             unit(k - 1)
 
-        for k in (DEPTH - 1, *range(DEPTH - 3, 0, -1)):
-            for gather in gathers:
-                gather.begin(k)
+        for gather in gathers:
+            gather.begin(DEPTH - 1)
         begin_last(gathers, False)
 
         @pl.loop(0, model // 256)
@@ -1171,7 +1185,7 @@
             @pl.loop(start, stop)
             def _(j):
                 for gather in gathers:
-                    gather.step(DEPTH - 1 - j)
+                    gather.step(step_order(j))
 
         steps(0, 1)
         for j in range(TP):

time: 389 us -> 386 us (level)
  no operation moved by 1% of the time
where the time goes in v5:
time: 386 us
  Pallas kernels  372 us (96%)
  local copies, waits for them, and re-layouts  11.7 us (3%)
    pallas_call x3, Pallas kernels, call(): pl.pallas_call(body, name=name, out_shape=tuple((shape for shape, _ in ou...  372 us
    unnamed x25, local copies, waits for them, and re-layouts  10.4 us

profile of v5, /device:TPU:0, one launch (start us, length us, event | category | flops | bytes accessed | tf_op | source)
XLA Modules:
  0.0 385.6 jit_solution(12059160068527490380)
XLA Ops:
  1.3 131.5 %attention.1 = (f32[128,1536]{1,0:T(8,128)}, bf16[1024,1536]{1,0:T(8,128)(2,1)}, bf16[1024,1536]{1,0:T(8,128)(2,1)}, bf16[1024,768]{1,0:T(8,128)(2,1)}, f32[1024...) custom-call(bf16[128,1536]{1,0:T(8,128)(2,1)} %bitcast.15, ...), custom_call_target="tpu_custom_call" | custom-call | tf_op jit(solution)/shard_map/attention/pallas_call | solution.py:308
  132.8 114.5 %feed_forward.1 = (bf16[128,1536]{1,0:T(8,128)(2,1)}, f32[128,1536]{1,0:T(8,128)}, f32[8,1536]{1,0:T(8,128)}, bf16[2,1536,512]{2,1,0:T(8,128)(2,1)}, bf16[2,256,1536]{2,1,0:T(8,128)(2,1)}) custom-call(bf16[128,1536]{1,0:T(8,128)(2,1)} %bitcast.16, f32[128,1536]{1,0:T(8,128)} %get-tuple-element.37.branch_ref, f32[8,1536]{1,0:T(8,128)} %get-tuple-element.38.gain_ref.gains_ref, ...), custom_call_target="tpu_custom_call" | custom-call | tf_op jit(solution)/shard_map/feed_forward/pallas_call | solution.py:308
  247.4 0.0 copy-start.4
  247.4 126.4 %attention_back.1 = (f32[128,1536]{1,0:T(8,128)}, f32[96,6144]{1,0:T(8,128)}, f32[96,1536]{1,0:T(8,128)}, f32[2,96]{1,0:T(2,128)}, f32[24,96]{1,0:T(8,128)}, /*i...) custom-call(bf16[128,1536]{1,0:T(8,128)(2,1)} %bitcast.17, ...), custom_call_target="tpu_custom_call" | custom-call | tf_op jit(solution)/shard_map/attention_back/pallas_call | solution.py:308
  373.8 0.0 copy-start.1
  373.8 1.3 slice_bitcast_fusion
  375.2 0.0 copy-done.4
  375.2 0.7 copy.33
  375.9 2.1 copy.34
  378.0 0.0 copy-done.1
  378.0 0.0 copy-start.5
  378.0 0.0 copy-start.7
  378.0 0.0 copy-start.3
  378.0 0.0 copy-start
  378.0 1.4 copy.35
  379.4 0.0 copy-done.5
  379.4 0.6 copy.36
  380.0 0.0 copy-done.7
  380.0 0.5 copy.37
  380.5 0.0 copy-done.3
  380.5 0.8 copy.38
  381.4 0.0 copy-done
  381.4 0.0 copy-start.2
  381.4 1.7 copy.39
  383.0 0.9 copy-done.2
  383.9 0.0 copy-start.6
  383.9 1.1 copy.40
  385.0 0.0 copy-done.6
  385.0 0.5 copy.41
Async XLA Ops:
  247.4 127.8 %copy-start.4 = (bf16[128,1536]{1,0:T(8,128)(2,1)S(1)}, bf16[128,1536]{1,0:T(8,128)(2,1)}, u32[]{:S(2)}) copy-start(bf16[128,1536]{1,0:T(8,128)(2,1)} %get-tuple-element.40) | copy-start | bytes 1179652
  373.8 4.2 %copy-start.1 = (f32[96,6144]{1,0:T(8,128)S(1)}, f32[96,6144]{1,0:T(8,128)}, u32[]{:S(2)}) copy-start(f32[96,6144]{1,0:T(8,128)} %get-tuple-element.79) | copy-start | bytes 7077892
  378.0 1.4 copy-start.5
  378.0 2.0 copy-start.7
  378.0 2.5 copy-start.3
  378.0 3.4 copy-start
  381.4 2.5 copy-start.2
  383.9 1.1 copy-start.6

commit v6 on v5

--- a/solution.py
+++ b/solution.py
@@ -1086,11 +1086,6 @@
             for wave in waves:
                 wave.across(k - 1)
 
-            @pl.when(k == DEPTH - 1)
-            def _():
-                for gather in gathers:
-                    gather.begin(1)
-
             @pl.when(k == DEPTH)
             def _():
                 for gather in gathers:
@@ -1098,8 +1093,9 @@
 
             unit(k - 1)
 
-        for gather in gathers:
-            gather.begin(DEPTH - 1)
+        for k in (DEPTH - 1, *range(DEPTH - 3, 0, -1)):
+            for gather in gathers:
+                gather.begin(k)
         begin_last(gathers, False)
 
         @pl.loop(0, model // 256)
@@ -1185,7 +1181,7 @@
             @pl.loop(start, stop)
             def _(j):
                 for gather in gathers:
-                    gather.step(step_order(j))
+                    gather.step(DEPTH - 1 - j)
 
         steps(0, 1)
         for j in range(TP):

time: 386 us -> 386 us (level)
  no operation moved by 1% of the time
where the time goes in v6:
time: 386 us; the launch traced here: 384 us
  Pallas kernels  371 us (96%)
  local copies, waits for them, and re-layouts  11.7 us (3%)
    pallas_call x3, Pallas kernels, call(): pl.pallas_call(body, name=name, out_shape=tuple((shape for shape, _ in ou...  371 us
    unnamed x25, local copies, waits for them, and re-layouts  10.4 us

profile of v6, /device:TPU:0, one launch (start us, length us, event | category | flops | bytes accessed | tf_op | source)
XLA Modules:
  0.0 383.8 jit_solution(13028513218519865442)
XLA Ops:
  1.3 131.5 %attention.1 = (f32[128,1536]{1,0:T(8,128)}, bf16[1024,1536]{1,0:T(8,128)(2,1)}, bf16[1024,1536]{1,0:T(8,128)(2,1)}, bf16[1024,768]{1,0:T(8,128)(2,1)}, f32[1024...) custom-call(bf16[128,1536]{1,0:T(8,128)(2,1)} %bitcast.15, ...), custom_call_target="tpu_custom_call" | custom-call | tf_op jit(solution)/shard_map/attention/pallas_call | solution.py:308
  132.8 114.5 %feed_forward.1 = (bf16[128,1536]{1,0:T(8,128)(2,1)}, f32[128,1536]{1,0:T(8,128)}, f32[8,1536]{1,0:T(8,128)}, bf16[2,1536,512]{2,1,0:T(8,128)(2,1)}, bf16[2,256,1536]{2,1,0:T(8,128)(2,1)}) custom-call(bf16[128,1536]{1,0:T(8,128)(2,1)} %bitcast.16, f32[128,1536]{1,0:T(8,128)} %get-tuple-element.37.branch_ref, f32[8,1536]{1,0:T(8,128)} %get-tuple-element.38.gain_ref.gains_ref, ...), custom_call_target="tpu_custom_call" | custom-call | tf_op jit(solution)/shard_map/feed_forward/pallas_call | solution.py:308
  247.4 0.0 copy-start.4
  247.4 124.6 %attention_back.1 = (f32[128,1536]{1,0:T(8,128)}, f32[96,6144]{1,0:T(8,128)}, f32[96,1536]{1,0:T(8,128)}, f32[2,96]{1,0:T(2,128)}, f32[24,96]{1,0:T(8,128)}, /*i...) custom-call(bf16[128,1536]{1,0:T(8,128)(2,1)} %bitcast.17, ...), custom_call_target="tpu_custom_call" | custom-call | tf_op jit(solution)/shard_map/attention_back/pallas_call | solution.py:308
  372.0 0.0 copy-start.1
  372.0 1.3 slice_bitcast_fusion
  373.4 0.0 copy-done.4
  373.4 0.7 copy.33
  374.1 2.1 copy.34
  376.2 0.0 copy-done.1
  376.2 0.0 copy-start.5
  376.2 0.0 copy-start.7
  376.2 0.0 copy-start.3
  376.2 0.0 copy-start
  376.2 1.4 copy.35
  377.6 0.0 copy-done.5
  377.6 0.6 copy.36
  378.2 0.0 copy-done.7
  378.2 0.5 copy.37
  378.8 0.0 copy-done.3
  378.8 0.8 copy.38
  379.6 0.0 copy-done
  379.6 0.0 copy-start.2
  379.6 1.7 copy.39
  381.2 0.9 copy-done.2
  382.1 0.0 copy-start.6
  382.1 1.1 copy.40
  383.3 0.0 copy-done.6
  383.3 0.5 copy.41
Async XLA Ops:
  247.4 126.0 %copy-start.4 = (bf16[128,1536]{1,0:T(8,128)(2,1)S(1)}, bf16[128,1536]{1,0:T(8,128)(2,1)}, u32[]{:S(2)}) copy-start(bf16[128,1536]{1,0:T(8,128)(2,1)} %get-tuple-element.40) | copy-start | bytes 1179652
  372.0 4.2 %copy-start.1 = (f32[96,6144]{1,0:T(8,128)S(1)}, f32[96,6144]{1,0:T(8,128)}, u32[]{:S(2)}) copy-start(f32[96,6144]{1,0:T(8,128)} %get-tuple-element.79) | copy-start | bytes 7077892
  376.2 1.4 copy-start.5
  376.2 2.0 copy-start.7
  376.2 2.5 copy-start.3
  376.2 3.4 copy-start
  379.6 2.5 copy-start.2
  382.1 1.1 copy-start.6
